TPU v7x, 32 devices: a whole 2x2x4 slice. The times are simulated.
32 devices in a mesh: groups: 2 (over y), expert: 16 (over z, x, core).
Axes of the slice: x: 2, y: 2, z: 4, core: 2. Of those that a mesh axis runs over, the one named last changes fastest.
Arguments:
- activations: bfloat16 [2, 512, 2048], P(None, ('groups', 'expert')), parts along dimension 1, may hold values from -6 to 6
- pick_weight: float32 [2, 512, 1], P(None, ('groups', 'expert')), parts along dimension 1, may hold values from 0.2 to 1
- expert_ids: int32 [2, 512, 1], P(None, ('groups', 'expert')), parts along dimension 1, may hold values from 0 to 7, as said below
- replica: int32 [2, 512, 1], P(None, ('groups', 'expert')), parts along dimension 1, may hold values from 0 to 4, as said below
- old_home: int32 [8], replicated, may hold values from 0 to 7, each once
- new_expert: int32 [32], P('groups'), parts along dimension 0, may hold values from 0 to 7, as said below
- gate_panel: bfloat16 [16, 2048, 384], P('expert'), may hold values from -0.125 to 0.125
- up_panel: bfloat16 [16, 2048, 384], P('expert'), may hold values from -0.125 to 0.125
- down_panel: bfloat16 [16, 2048, 384], P('expert'), may hold values from -0.21875 to 0.21875
Outputs:
- layer_output: bfloat16 [2, 512, 2048], P(None, ('groups', 'expert')), parts along dimension 1
- slot_load: int32 [32], P(('groups', 'expert')), parts along dimension 0
There are 2 independent parts, one for each index of `groups`. A program takes and returns all parts, laid end to end along the dimension named above; an argument that names none is the same for every part. Nothing has to cross between parts.
Inputs may be any that keep to these rules, and one draw needn't show every extreme that they name: `new_expert`: every expert is held by 1 or 5 slots. `expert_ids`: the 1 expert that a token names are different. replica[s, t, k] is below the number of slots that new_expert gives to expert_ids[s, t, k]. The picks of the 16 tokens of one device in one batch that land on one slot number at most 2, and in each batch some slot receives exactly 2 from every device.
All inputs are finite; a program needn't handle non-finite values.
Results may differ from a plain program's by a relative error of at most 0.0057.
Values may be sent and summed in bfloat16 or wider, within the bound.
No kernel may reach another device: no remote copies, remote signals or barrier semaphores. Data moves between devices by JAX's collectives and lax.ppermute only.
A program may use at most 128 MiB of HBM per device.

v0:
```python
import functools

import jax
import jax.numpy as jnp
from jax import lax
from jax.experimental import pallas as pl
from jax.experimental.pallas import tpu as pltpu
from jax.sharding import PartitionSpec as P


CAP = 2
REPL = 5
LANES = 128
SQUARE = 4
SMALL = 4 << 20
LARGE = 20 << 20
VMEM = pltpu.VMEM
SMEM = pltpu.SMEM
HBM = pltpu.MemorySpace.HBM
FETCH = 16 << 20


def slot_rank(new_expert, me):
    positions = jnp.arange(new_expert.shape[0], dtype=jnp.int32)
    mine = jnp.sum(jnp.where(positions == me, new_expert, 0))
    rank = jnp.sum(((new_expert == mine) & (positions < me)).astype(jnp.int32))
    return mine, rank


def gathered(
    activations,
    pick_weight,
    expert_ids,
    replica,
    old_home,
    new_expert,
    gate_panel,
    up_panel,
    down_panel,
):
    me = lax.axis_index("expert")
    batches, tokens, width = activations.shape
    top = expert_ids.shape[2]
    rows = batches * tokens
    x = activations.reshape(rows, width)
    picks = jnp.concatenate([expert_ids.reshape(rows, top), replica.reshape(rows, top)], axis=1)
    weights = pick_weight.reshape(rows, top)
    picks_all = lax.all_gather(picks, "expert", axis=0, tiled=True)
    weights_all = lax.all_gather(weights, "expert", axis=0, tiled=True)
    x_all = lax.all_gather(x, "expert", axis=0, tiled=True)
    ids_all = picks_all[:, :top]
    rep_all = picks_all[:, top:]
    mine, rank = slot_rank(new_expert, me)
    load = jnp.sum(((ids_all == mine) & (rep_all == rank)).astype(jnp.int32))
    labels = jnp.arange(old_home.shape[0], dtype=jnp.int32)
    held = jnp.sum(jnp.where(old_home == me // 2, labels, 0))
    scale = jnp.sum(jnp.where(ids_all == held, weights_all, 0.0), axis=1, keepdims=True)
    gate = jnp.dot(x_all, gate_panel[0], preferred_element_type=jnp.float32)
    up = jnp.dot(x_all, up_panel[0], preferred_element_type=jnp.float32)
    hidden = (jax.nn.silu(gate) * up).astype(jnp.bfloat16)
    part = lax.dot_general(
        hidden, down_panel[0], (((1,), (1,)), ((), ())), preferred_element_type=jnp.float32
    )
    part = (part * scale).astype(jnp.bfloat16)
    total = lax.psum_scatter(part, "expert", scatter_dimension=0, tiled=True)
    return total.reshape(batches, tokens, width), load.reshape(1)


def steps(index, size, count):
    whole = jnp.zeros_like(index)
    for step in range(1, count):
        whole = whole + (index >= step * size).astype(jnp.int32)
    return whole


def block_rows(batches, cap):
    return -(-(batches * cap + 1) // 8) * 8


def pick(cap, table, picks, x, blocks, sel_ref, experts):
    batches, tokens = picks.shape[0] // 2, picks.shape[1]
    count = batches * tokens
    high = block_rows(batches, cap)
    chip = lax.axis_index("expert") // 2

    def batch_of(index):
        return steps(index, tokens, batches)

    col = lax.broadcasted_iota(jnp.int32, (tokens, count), 1)
    spread = col - tokens * batch_of(col) == lax.broadcasted_iota(jnp.int32, (tokens, count), 0)
    spread = spread.astype(jnp.float32)
    own_lane = batch_of(lax.broadcasted_iota(jnp.int32, (batches, count), 1))
    own_lane = own_lane == lax.broadcasted_iota(jnp.int32, (batches, count), 0)

    def row_of(values):
        wide = jnp.dot(values.astype(jnp.float32), spread, preferred_element_type=jnp.float32)
        return jnp.sum(jnp.where(own_lane, wide, 0.0), axis=0, keepdims=True).astype(jnp.int32)

    ids = row_of(picks[:batches, :])
    reps = row_of(picks[batches:, :])
    target = jnp.zeros_like(ids)
    for expert in range(experts):
        target = jnp.where(ids == expert, table[0:1, expert : expert + 1], target)

    sub = lax.broadcasted_iota(jnp.int32, (8, count), 0)
    inside = (target == (sub ^ chip)) & (sub < SQUARE)
    before_from = lax.broadcasted_iota(jnp.int32, (count, count), 0)
    before_to = lax.broadcasted_iota(jnp.int32, (count, count), 1)
    before = (before_from < before_to) & (batch_of(before_from) == batch_of(before_to))
    earlier = jnp.dot(
        inside.astype(jnp.bfloat16),
        before.astype(jnp.bfloat16),
        preferred_element_type=jnp.float32,
    )
    position = jnp.sum(jnp.where(inside, earlier, 0.0), axis=0, keepdims=True).astype(jnp.int32)

    row = lax.broadcasted_iota(jnp.int32, (SQUARE * high, count), 0)
    peer = steps(row, high, SQUARE)
    left = row - high * peer
    group = steps(left, cap, batches + 1)
    left = left - cap * group
    lane = batch_of(lax.broadcasted_iota(jnp.int32, (SQUARE * high, count), 1))
    sel = ((target == (peer ^ chip)) & (position == left) & (group == lane)).astype(jnp.bfloat16)
    sel_ref[...] = sel
    meta_row = lax.broadcasted_iota(jnp.int32, (high, LANES), 0) == batches * cap
    meta_lane = lax.broadcasted_iota(jnp.int32, (high, LANES), 1)
    x = x()
    for q in range(SQUARE):
        part = jnp.dot(sel[q * high : (q + 1) * high], x, preferred_element_type=jnp.float32)
        meta = jnp.zeros((high, LANES), jnp.float32)
        for core in range(2):
            at = 2 * q + core
            hits = (ids == table[1:2, at : at + 1]) & (reps == table[2:3, at : at + 1])
            load = jnp.sum(hits.astype(jnp.float32), axis=1, keepdims=True)
            meta = jnp.where(meta_row & (meta_lane == core), load, meta)
        blocks[q][...] = part.astype(jnp.bfloat16)
        blocks[q][:, :LANES] = (part[:, :LANES] + meta).astype(jnp.bfloat16)


def pick_own_kernel(cap, home_hbm, new_hbm, x_hbm, picks_ref, *refs):
    blocks, sel_ref, table_ref = refs[:SQUARE], refs[SQUARE], refs[SQUARE + 1]
    home_ref, new_ref, x_ref, sem = refs[SQUARE + 2 :]
    copies = [
        pltpu.make_async_copy(source, target, sem.at[index])
        for index, (source, target) in enumerate(
            ((home_hbm, home_ref), (new_hbm, new_ref), (x_hbm, x_ref))
        )
    ]
    for copy in copies:
        copy.start()
    chip = lax.axis_index("expert") // 2
    slots = new_ref.shape[0]
    experts = home_ref.shape[0]
    copies[0].wait()
    copies[1].wait()
    row = lax.broadcasted_iota(jnp.int32, table_ref.shape, 0)
    lane = lax.broadcasted_iota(jnp.int32, table_ref.shape, 1)
    table = jnp.zeros(table_ref.shape, jnp.int32)
    for expert in range(experts):
        table = jnp.where((row == 0) & (lane == expert), home_ref[expert], table)
    for at in range(2 * SQUARE):
        slot = 2 * (chip ^ (at // 2)) + at % 2
        mine = new_ref[slot]
        rank = jnp.int32(0)
        for other in range(slots):
            rank = rank + ((new_ref[other] == mine) & (slot > other)).astype(jnp.int32)
        table = jnp.where((row == 1) & (lane == at), mine, table)
        table = jnp.where((row == 2) & (lane == at), rank, table)
    table_ref[...] = table

    def rows():
        copies[2].wait()
        return x_ref[...]

    pick(cap, table, picks_ref[...], rows, blocks, sel_ref, experts)


def pick_far_kernel(cap, experts, table_ref, x_ref, picks_ref, *refs):
    blocks, sel_ref = refs[:SQUARE], refs[SQUARE]
    pick(cap, table_ref[...], picks_ref[...], lambda: x_ref[...], blocks, sel_ref, experts)


def pick_shapes(cap, x, picks):
    batches = picks.shape[0] // 2
    high = block_rows(batches, cap)
    count, width = x.shape
    block = jax.ShapeDtypeStruct((high, width), jnp.bfloat16)
    sel = jax.ShapeDtypeStruct((SQUARE * high, count), jnp.bfloat16)
    cost = pl.CostEstimate(
        flops=2 * SQUARE * high * count * width, bytes_accessed=FETCH, transcendentals=0
    )
    return [block] * SQUARE + [sel], cost


def pick_own(cap, home, new, x, picks):
    shapes, cost = pick_shapes(cap, x, picks)
    return pl.pallas_call(
        functools.partial(pick_own_kernel, cap),
        out_shape=shapes + [jax.ShapeDtypeStruct((8, LANES), jnp.int32)],
        in_specs=[pl.BlockSpec(memory_space=HBM)] * 3 + [pl.BlockSpec(memory_space=VMEM)],
        out_specs=[pl.BlockSpec(memory_space=VMEM)] * (SQUARE + 2),
        scratch_shapes=[
            SMEM(home.shape, jnp.int32),
            SMEM(new.shape, jnp.int32),
            VMEM(x.shape, x.dtype),
            pltpu.SemaphoreType.DMA((3,)),
        ],
        cost_estimate=cost,
        compiler_params=pltpu.CompilerParams(vmem_limit_bytes=SMALL),
    )(home, new, x, picks)


def pick_far(cap, experts, table, x, picks):
    shapes, cost = pick_shapes(cap, x, picks)
    return pl.pallas_call(
        functools.partial(pick_far_kernel, cap, experts),
        out_shape=shapes,
        in_specs=[pl.BlockSpec(memory_space=VMEM)] * 3,
        out_specs=[pl.BlockSpec(memory_space=VMEM)] * (SQUARE + 1),
        cost_estimate=cost,
        compiler_params=pltpu.CompilerParams(vmem_limit_bytes=SMALL),
    )(table, x, picks)


def expert_kernel(meta, *refs):
    blocks, refs = refs[:SQUARE], refs[SQUARE:]
    gates, ups, downs, prior_ref = refs[:2], refs[2:4], refs[4:6], refs[6]
    outs, load_ref = refs[7 : 7 + SQUARE], refs[7 + SQUARE]
    high = blocks[0].shape[0]
    x = jnp.concatenate([block[...] for block in blocks], axis=0)
    contract = (((1,), (1,)), ((), ()))
    total = None
    for half in range(2):
        gate = jnp.dot(x, gates[half][0], preferred_element_type=jnp.float32)
        up = jnp.dot(x, ups[half][0], preferred_element_type=jnp.float32)
        hidden = (gate / (1.0 + jnp.exp(-gate)) * up).astype(jnp.bfloat16)
        part = lax.dot_general(
            hidden, downs[half][0], contract, preferred_element_type=jnp.float32
        )
        total = part if half == 0 else total + part
    total = total.astype(jnp.bfloat16)
    for q in range(SQUARE):
        outs[q][...] = total[q * high : (q + 1) * high]
    load = prior_ref[...]
    start = meta - meta % 8
    for block in blocks:
        load = load + block[start : start + 8, :LANES].astype(jnp.int32)
    load_ref[...] = load


def run_expert(meta, blocks, panels, far_panels, prior):
    high, width = blocks[0].shape
    half = panels[0].shape[2]
    rows = SQUARE * high
    return pl.pallas_call(
        functools.partial(expert_kernel, meta),
        out_shape=[jax.ShapeDtypeStruct((high, width), jnp.bfloat16)] * SQUARE
        + [jax.ShapeDtypeStruct(prior.shape, jnp.int32)],
        in_specs=[pl.BlockSpec(memory_space=VMEM)] * (SQUARE + 7),
        out_specs=[pl.BlockSpec(memory_space=VMEM)] * (SQUARE + 1),
        cost_estimate=pl.CostEstimate(
            flops=2 * rows * width * half * 6,
            bytes_accessed=6 * 2 * width * half + 4 * rows * width,
            transcendentals=2 * rows * half,
        ),
        compiler_params=pltpu.CompilerParams(vmem_limit_bytes=LARGE),
    )(
        *blocks,
        panels[0],
        far_panels[0],
        panels[1],
        far_panels[1],
        panels[2],
        far_panels[2],
        prior,
    )


def chosen(sel_ref, blocks):
    y = jnp.concatenate([block[...] for block in blocks], axis=0)
    return lax.dot_general(
        sel_ref[...], y, (((0,), (0,)), ((), ())), preferred_element_type=jnp.float32
    )


def merge_kernel(sel_ref, *refs):
    refs[SQUARE][...] = chosen(sel_ref, refs[:SQUARE]).astype(jnp.bfloat16)


def final_kernel(meta, sel_ref, weight_ref, back_ref, load_ref, load_far_ref, *refs):
    out_ref, slot_ref = refs[SQUARE], refs[SQUARE + 1]
    core = lax.axis_index("expert") % 2
    both = load_ref[...] + load_far_ref[...]
    row = lax.broadcasted_iota(jnp.int32, both.shape, 0)
    lane = lax.broadcasted_iota(jnp.int32, both.shape, 1)
    slot_ref[0] = jnp.sum(jnp.where((row == meta % 8) & (lane == core), both, 0))
    batches, tokens = weight_ref.shape
    total = chosen(sel_ref, refs[:SQUARE]) + back_ref[...].astype(jnp.float32)
    lane = lax.broadcasted_iota(jnp.int32, (tokens, tokens), 0)
    same = lane == lax.broadcasted_iota(jnp.int32, (tokens, tokens), 1)
    scale = jnp.concatenate(
        [
            jnp.sum(
                jnp.where(same, weight_ref[batch : batch + 1, :], 0.0), axis=1, keepdims=True
            )
            for batch in range(batches)
        ],
        axis=0,
    )
    out_ref[...] = (total * scale).astype(jnp.bfloat16)


def merge_rows(kernel, sel, others, blocks, loads):
    count = sel.shape[1]
    width = blocks[0].shape[1]
    shapes = [jax.ShapeDtypeStruct((count, width), jnp.bfloat16)]
    specs = [pl.BlockSpec(memory_space=VMEM)]
    if loads:
        shapes.append(jax.ShapeDtypeStruct((1,), jnp.int32))
        specs.append(pl.BlockSpec(memory_space=SMEM))
    return pl.pallas_call(
        kernel,
        out_shape=shapes,
        in_specs=[pl.BlockSpec(memory_space=VMEM)] * (SQUARE + 1 + len(others)),
        out_specs=specs,
        cost_estimate=pl.CostEstimate(
            flops=2 * sel.shape[0] * count * width,
            bytes_accessed=2 * (sel.shape[0] + count) * width,
            transcendentals=0,
        ),
        compiler_params=pltpu.CompilerParams(vmem_limit_bytes=SMALL),
    )(sel, *others, *blocks)


def swapped(size, bits):
    return [(index, index ^ bits) for index in range(size)]


def dispatched(
    activations,
    pick_weight,
    expert_ids,
    replica,
    old_home,
    new_expert,
    gate_panel,
    up_panel,
    down_panel,
):
    size = lax.axis_size("expert")
    batches, tokens, width = activations.shape
    rows = batches * tokens
    cap = min(CAP * REPL, tokens)
    meta = batches * cap
    distant = 2 * SQUARE

    def swap(value, bits):
        return lax.ppermute(value, "expert", swapped(size, bits))

    def around(blocks):
        return [blocks[0]] + [swap(blocks[q], 2 * q) for q in range(1, SQUARE)]

    x = activations.reshape(rows, width)
    x_far = swap(x, distant)
    picks = jnp.concatenate(
        [expert_ids.reshape(batches, tokens), replica.reshape(batches, tokens)], axis=0
    )
    picks_far = swap(picks, distant)
    panels = (gate_panel, up_panel, down_panel)
    panels_far = [swap(panel, 1) for panel in panels]
    *blocks, sel, table = pick_own(cap, old_home, new_expert, x, picks)
    blocks = around(blocks)
    *blocks_far, sel_far = pick_far(cap, old_home.shape[0], table, x_far, picks_far)
    blocks_far = around(blocks_far)
    prior = jnp.zeros((8, LANES), jnp.int32)
    *results, load = run_expert(meta, blocks, panels, panels_far, prior)
    *results_far, load = run_expert(meta, blocks_far, panels, panels_far, load)
    results_far = around(results_far)
    results = around(results)
    load_far = swap(load, 1)
    (far,) = merge_rows(merge_kernel, sel_far, (), results_far, False)
    back = swap(far, distant)
    weight = pick_weight.reshape(batches, tokens)
    output, slot_load = merge_rows(
        functools.partial(final_kernel, meta),
        sel,
        (weight, back, load, load_far),
        results,
        True,
    )
    return output.reshape(batches, tokens, width), slot_load


def solution(mesh):
    chips = mesh.shape["expert"] // 2

    def per_device(*args):
        if direct(args):
            return dispatched(*args)
        return gathered(*args)

    def direct(args):
        return chips == 2 * SQUARE and args[2].shape[2] == 1

    return jax.shard_map(
        per_device,
        mesh=mesh,
        in_specs=(
            P(None, ("groups", "expert"), None),
            P(None, ("groups", "expert"), None),
            P(None, ("groups", "expert"), None),
            P(None, ("groups", "expert"), None),
            P(),
            P("groups"),
            P("expert", None, None),
            P("expert", None, None),
            P("expert", None, None),
        ),
        out_specs=(P(None, ("groups", "expert"), None), P(("groups", "expert"))),
        check_vma=False,
    )
```

profile of v0, /device:TPU:0, one launch (start us, length us, event | category | flops | bytes accessed | tf_op | source)
XLA Modules:
  0.0 55.8 jit_solution(7450731611529909877)
XLA Ops:
  1.7 3.7 %collective-permute-start = (bf16[32,2048]{1,0:T(8,128)(2,1)}, bf16[32,2048]{1,0:T(8,128)(2,1)S(1)}, u32[]{:S(2)}, u32[]{:S(2)}) collective-permute-start(bf16[32,2048]{1,0:T(8,128)(2,1)} %bitcast.5), channel_id=1, source_target_pairs={{0,8},{1,9},{2,10},{3,11},{4,12},{5,13},{6,14},{7,15},{8,0},{9,1},... | collective-permute-start | bytes 393224 | tf_op jit(solution)/shard_map/ppermute | solution.py:358
  5.4 0.7 %pad_add_fusion.picks_ref = s32[4,16]{1,0:T(4,128)S(1)} fusion(s32[2,16]{1,0:T(2,128)} %bitcast.8, s32[2,16]{1,0:T(2,128)} %bitcast.9), kind=kLoop, calls=%fused_computation | loop fusion | flops 64 | bytes 512 | tf_op jit(solution)/shard_map/concatenate | solution.py:365
  6.1 0.9 %copy-done.6 = bf16[2,16,2048]{2,1,0:T(8,128)(2,1)S(1)} copy-done((bf16[2,16,2048]{2,1,0:T(8,128)(2,1)S(1)}, bf16[2,16,2048]{2,1,0:T(8,128)(2,1)}, u32[]{:S(2)}) %copy-start.6) | copy-done | bytes 131096
  7.0 0.7 %copy-done.8 = s32[8]{0:T(128)S(1)} copy-done((s32[8]{0:T(128)S(1)}, s32[8]{0:T(128)}, u32[]{:S(2)}) %copy-start.8) | copy-done | bytes 56
  7.6 0.7 %copy-done.9 = s32[16]{0:T(128)S(1)} copy-done((s32[16]{0:T(128)S(1)}, s32[16]{0:T(128)}, u32[]{:S(2)}) %copy-start.9) | copy-done | bytes 88
  8.3 1.3 %shard_map.104 = (bf16[24,2048]{1,0:T(8,128)(2,1)S(1)}, bf16[24,2048]{1,0:T(8,128)(2,1)S(1)}, bf16[24,2048]{1,0:T(8,128)(2,1)S(1)}, bf16[24,2048]{1,0:T(8,128)(2...) custom-call(s32[8]{0:T(128)S(1)} %copy-done.8, s32[16]{0:T(128)S(1)} %copy-done.9, ...), custom_call_target="tpu_custom_call" | custom-call | flops 12582912 | bytes 16777216 | tf_op jit(solution)/shard_map/pallas_call | solution.py:197
  9.6 3.0 %collective-permute-done.1.picks_ref = s32[4,16]{1,0:T(4,128)S(1)} collective-permute-done((s32[4,16]{1,0:T(4,128)S(1)}, s32[4,16]{1,0:T(4,128)S(1)}, u32[]{:S(2)}, u32[]{:S(2)}) %collective-permute-start.1) | collective-permute-done | bytes 288 | tf_op jit(solution)/shard_map/ppermute | solution.py:358
  12.5 1.5 %collective-permute-start.8 = (bf16[24,2048]{1,0:T(8,128)(2,1)S(1)}, bf16[24,2048]{1,0:T(8,128)(2,1)S(1)}, u32[]{:S(2)}, u32[]{:S(2)}) collective-permute-start(bf16[24,2048]{1,0:T(8,128)(2,1)S(1)} %get-tuple-element.33), channel_id=1, source_target_pairs={{0,2},{1,3},{2,0},{3,1},{4,6},{5,7},{6,4},{7,5},{8,10},{9,11},{10,... | collective-permute-start | bytes 294920 | tf_op jit(solution)/shard_map/ppermute | solution.py:358
  14.1 3.1 %collective-permute-done.8.refs_1_ = bf16[24,2048]{1,0:T(8,128)(2,1)S(1)} collective-permute-done((bf16[24,2048]{1,0:T(8,128)(2,1)S(1)}, bf16[24,2048]{1,0:T(8,128)(2,1)S(1)}, u32[]{:S(2)}, u32[]{:S(2)}) %collective-permute-start.8) | collective-permute-done | bytes 98336 | tf_op jit(solution)/shard_map/ppermute | solution.py:358
  17.2 0.9 %collective-permute-start.9 = (bf16[24,2048]{1,0:T(8,128)(2,1)S(1)}, bf16[24,2048]{1,0:T(8,128)(2,1)S(1)}, u32[]{:S(2)}, u32[]{:S(2)}) collective-permute-start(bf16[24,2048]{1,0:T(8,128)(2,1)S(1)} %get-tuple-element.34), channel_id=1, source_target_pairs={{0,4},{1,5},{2,6},{3,7},{4,0},{5,1},{6,2},{7,3},{8,12},{9,13},{10,... | collective-permute-start | bytes 294920 | tf_op jit(solution)/shard_map/ppermute | solution.py:358
  18.1 2.1 %collective-permute-start.10 = (bf16[24,2048]{1,0:T(8,128)(2,1)S(1)}, bf16[24,2048]{1,0:T(8,128)(2,1)S(1)}, u32[]{:S(2)}, u32[]{:S(2)}) collective-permute-start(bf16[24,2048]{1,0:T(8,128)(2,1)S(1)} %get-tuple-element.35), channel_id=1, source_target_pairs={{0,6},{1,7},{2,4},{3,5},{4,2},{5,3},{6,0},{7,1},{8,14},{9,15},{10,... | collective-permute-start | bytes 294920 | tf_op jit(solution)/shard_map/ppermute | solution.py:358
  20.7 1.9 %collective-permute-done.9.refs_2_ = bf16[24,2048]{1,0:T(8,128)(2,1)S(1)} collective-permute-done((bf16[24,2048]{1,0:T(8,128)(2,1)S(1)}, bf16[24,2048]{1,0:T(8,128)(2,1)S(1)}, u32[]{:S(2)}, u32[]{:S(2)}) %collective-permute-start.9) | collective-permute-done | bytes 98336 | tf_op jit(solution)/shard_map/ppermute | solution.py:358
  22.6 0.7 %collective-permute-start.2 = (bf16[24,2048]{1,0:T(8,128)(2,1)S(1)}, bf16[24,2048]{1,0:T(8,128)(2,1)S(1)}, u32[]{:S(2)}, u32[]{:S(2)}) collective-permute-start(bf16[24,2048]{1,0:T(8,128)(2,1)S(1)} %get-tuple-element.29), channel_id=1, source_target_pairs={{0,2},{1,3},{2,0},{3,1},{4,6},{5,7},{6,4},{7,5},{8,10},{9,11},{10,... | collective-permute-start | bytes 294920 | tf_op jit(solution)/shard_map/ppermute | solution.py:358
  23.3 0.6 %collective-permute-done.10.refs_3_ = bf16[24,2048]{1,0:T(8,128)(2,1)S(1)} collective-permute-done((bf16[24,2048]{1,0:T(8,128)(2,1)S(1)}, bf16[24,2048]{1,0:T(8,128)(2,1)S(1)}, u32[]{:S(2)}, u32[]{:S(2)}) %collective-permute-start.10) | collective-permute-done | bytes 98336 | tf_op jit(solution)/shard_map/ppermute | solution.py:358
  23.9 1.2 %collective-permute-start.3 = (bf16[24,2048]{1,0:T(8,128)(2,1)S(1)}, bf16[24,2048]{1,0:T(8,128)(2,1)S(1)}, u32[]{:S(2)}, u32[]{:S(2)}) collective-permute-start(bf16[24,2048]{1,0:T(8,128)(2,1)S(1)} %get-tuple-element.30), channel_id=1, source_target_pairs={{0,4},{1,5},{2,6},{3,7},{4,0},{5,1},{6,2},{7,3},{8,12},{9,13},{10,... | collective-permute-start | bytes 294920 | tf_op jit(solution)/shard_map/ppermute | solution.py:358
  25.1 1.6 %collective-permute-start.4 = (bf16[24,2048]{1,0:T(8,128)(2,1)S(1)}, bf16[24,2048]{1,0:T(8,128)(2,1)S(1)}, u32[]{:S(2)}, u32[]{:S(2)}) collective-permute-start(bf16[24,2048]{1,0:T(8,128)(2,1)S(1)} %get-tuple-element.31), channel_id=1, source_target_pairs={{0,6},{1,7},{2,4},{3,5},{4,2},{5,3},{6,0},{7,1},{8,14},{9,15},{10,... | collective-permute-start | bytes 294920 | tf_op jit(solution)/shard_map/ppermute | solution.py:358
  26.7 1.4 %copy-done = bf16[1,2048,384]{2,1,0:T(8,128)(2,1)S(1)} copy-done((bf16[1,2048,384]{2,1,0:T(8,128)(2,1)S(1)}, bf16[1,2048,384]{2,1,0:T(8,128)(2,1)}, u32[]{:S(2)}) %copy-start) | copy-done | bytes 1572888
  28.1 1.4 %copy-done.2 = bf16[1,2048,384]{2,1,0:T(8,128)(2,1)S(1)} copy-done((bf16[1,2048,384]{2,1,0:T(8,128)(2,1)S(1)}, bf16[1,2048,384]{2,1,0:T(8,128)(2,1)}, u32[]{:S(2)}) %copy-start.2) | copy-done | bytes 1572888
  29.6 1.4 %copy-done.4 = bf16[1,2048,384]{2,1,0:T(8,128)(2,1)S(1)} copy-done((bf16[1,2048,384]{2,1,0:T(8,128)(2,1)S(1)}, bf16[1,2048,384]{2,1,0:T(8,128)(2,1)}, u32[]{:S(2)}) %copy-start.4) | copy-done | bytes 1572888
  31.0 2.2 %shard_map.106 = (bf16[24,2048]{1,0:T(8,128)(2,1)S(1)}, bf16[24,2048]{1,0:T(8,128)(2,1)S(1)}, bf16[24,2048]{1,0:T(8,128)(2,1)S(1)}, bf16[24,2048]{1,0:T(8,128)(2,1)S(1)}, s32[8,128]{1,0:T(8,128)S(1)}) custom-call(bf16[24,2048]{1,0:T(8,128)(2,1)S(1)} %get-tuple-element.32.refs_0_, bf16[24,2048]{1,0:T(8,128)(2,1)S(1)} %collective-permute-done.8.refs_1_, ...), custom_call_target="tpu_custom_call" | custom-call | flops 905969664 | bytes 10223616 | tf_op jit(solution)/shard_map/pallas_call | solution.py:255
  33.3 2.2 %shard_map.107 = (bf16[24,2048]{1,0:T(8,128)(2,1)S(1)}, bf16[24,2048]{1,0:T(8,128)(2,1)S(1)}, bf16[24,2048]{1,0:T(8,128)(2,1)S(1)}, bf16[24,2048]{1,0:T(8,128)(2,1)S(1)}, s32[8,128]{1,0:T(8,128)S(1)}) custom-call(bf16[24,2048]{1,0:T(8,128)(2,1)S(1)} %get-tuple-element.28.refs_0_, bf16[24,2048]{1,0:T(8,128)(2,1)S(1)} %collective-permute-done.2.refs_1_, ...), custom_call_target="tpu_custom_call" | custom-call | flops 905969664 | bytes 10223616 | tf_op jit(solution)/shard_map/pallas_call | solution.py:255
  35.6 0.8 %collective-permute-start.11 = (bf16[24,2048]{1,0:T(8,128)(2,1)S(1)}, bf16[24,2048]{1,0:T(8,128)(2,1)S(1)}, u32[]{:S(2)}, u32[]{:S(2)}) collective-permute-start(bf16[24,2048]{1,0:T(8,128)(2,1)S(1)} %get-tuple-element.38), channel_id=1, source_target_pairs={{0,2},{1,3},{2,0},{3,1},{4,6},{5,7},{6,4},{7,5},{8,10},{9,11},{10,... | collective-permute-start | bytes 294920 | tf_op jit(solution)/shard_map/ppermute | solution.py:358
  36.3 1.2 %collective-permute-start.12 = (bf16[24,2048]{1,0:T(8,128)(2,1)S(1)}, bf16[24,2048]{1,0:T(8,128)(2,1)S(1)}, u32[]{:S(2)}, u32[]{:S(2)}) collective-permute-start(bf16[24,2048]{1,0:T(8,128)(2,1)S(1)} %get-tuple-element.39), channel_id=1, source_target_pairs={{0,4},{1,5},{2,6},{3,7},{4,0},{5,1},{6,2},{7,3},{8,12},{9,13},{10,... | collective-permute-start | bytes 294920 | tf_op jit(solution)/shard_map/ppermute | solution.py:358
  37.5 1.6 %collective-permute-start.13 = (bf16[24,2048]{1,0:T(8,128)(2,1)S(1)}, bf16[24,2048]{1,0:T(8,128)(2,1)S(1)}, u32[]{:S(2)}, u32[]{:S(2)}) collective-permute-start(bf16[24,2048]{1,0:T(8,128)(2,1)S(1)} %get-tuple-element.40), channel_id=1, source_target_pairs={{0,6},{1,7},{2,4},{3,5},{4,2},{5,3},{6,0},{7,1},{8,14},{9,15},{10,... | collective-permute-start | bytes 294920 | tf_op jit(solution)/shard_map/ppermute | solution.py:358
  39.1 1.4 %collective-permute-done.11.refs_1_ = bf16[24,2048]{1,0:T(8,128)(2,1)S(1)} collective-permute-done((bf16[24,2048]{1,0:T(8,128)(2,1)S(1)}, bf16[24,2048]{1,0:T(8,128)(2,1)S(1)}, u32[]{:S(2)}, u32[]{:S(2)}) %collective-permute-start.11) | collective-permute-done | bytes 98336 | tf_op jit(solution)/shard_map/ppermute | solution.py:358
  40.9 2.1 %collective-permute-done.13.refs_3_ = bf16[24,2048]{1,0:T(8,128)(2,1)S(1)} collective-permute-done((bf16[24,2048]{1,0:T(8,128)(2,1)S(1)}, bf16[24,2048]{1,0:T(8,128)(2,1)S(1)}, u32[]{:S(2)}, u32[]{:S(2)}) %collective-permute-start.13) | collective-permute-done | bytes 98336 | tf_op jit(solution)/shard_map/ppermute | solution.py:358
  43.3 4.5 %collective-permute-start.14 = (bf16[32,2048]{1,0:T(8,128)(2,1)S(1)}, bf16[32,2048]{1,0:T(8,128)(2,1)S(1)}, u32[]{:S(2)}, u32[]{:S(2)}) collective-permute-start(bf16[32,2048]{1,0:T(8,128)(2,1)S(1)} %shard_map.108), channel_id=1, source_target_pairs={{0,8},{1,9},{2,10},{3,11},{4,12},{5,13},{6,14},{7,15},{8,0},{9,1},... | collective-permute-start | bytes 393224 | tf_op jit(solution)/shard_map/ppermute | solution.py:358
  48.0 1.1 %collective-permute-start.17 = (bf16[24,2048]{1,0:T(8,128)(2,1)S(1)}, bf16[24,2048]{1,0:T(8,128)(2,1)S(1)}, u32[]{:S(2)}, u32[]{:S(2)}) collective-permute-start(bf16[24,2048]{1,0:T(8,128)(2,1)S(1)} %get-tuple-element.44), channel_id=1, source_target_pairs={{0,4},{1,5},{2,6},{3,7},{4,0},{5,1},{6,2},{7,3},{8,12},{9,13},{10,... | collective-permute-start | bytes 294920 | tf_op jit(solution)/shard_map/ppermute | solution.py:358
  49.1 2.2 %collective-permute-start.18 = (bf16[24,2048]{1,0:T(8,128)(2,1)S(1)}, bf16[24,2048]{1,0:T(8,128)(2,1)S(1)}, u32[]{:S(2)}, u32[]{:S(2)}) collective-permute-start(bf16[24,2048]{1,0:T(8,128)(2,1)S(1)} %get-tuple-element.45), channel_id=1, source_target_pairs={{0,6},{1,7},{2,4},{3,5},{4,2},{5,3},{6,0},{7,1},{8,14},{9,15},{10,... | collective-permute-start | bytes 294920 | tf_op jit(solution)/shard_map/ppermute | solution.py:358
  51.2 1.2 %collective-permute-done.15.load_far_ref = s32[8,128]{1,0:T(8,128)S(1)} collective-permute-done((s32[8,128]{1,0:T(8,128)S(1)}, s32[8,128]{1,0:T(8,128)S(1)}, u32[]{:S(2)}, u32[]{:S(2)}) %collective-permute-start.15) | collective-permute-done | bytes 4128 | tf_op jit(solution)/shard_map/ppermute | solution.py:358
  52.6 2.3 %collective-permute-done.18.refs_3_ = bf16[24,2048]{1,0:T(8,128)(2,1)S(1)} collective-permute-done((bf16[24,2048]{1,0:T(8,128)(2,1)S(1)}, bf16[24,2048]{1,0:T(8,128)(2,1)S(1)}, u32[]{:S(2)}, u32[]{:S(2)}) %collective-permute-start.18) | collective-permute-done | bytes 98336 | tf_op jit(solution)/shard_map/ppermute | solution.py:358
  54.9 0.9 %shard_map.109 = (bf16[32,2048]{1,0:T(8,128)(2,1)}, s32[1]{0:T(128)}) custom-call(bf16[96,32]{1,0:T(8,128)(2,1)S(1)} %get-tuple-element.25.sel_ref, f32[2,16]{1,0:T(2,128)S(1)} %bitcast.7, bf16[32,2048]{1,0:T(8,128)(2,1)S(1)} %collective-permute-done.14.back_ref, s32[8,128]{1,0:T(8,128)S(1)} %get-tuple-element.41.load_ref, ...), custom_call_target="tpu_custom_call" | custom-call | flops 12582912 | bytes 524288 | tf_op jit(solution)/shard_map/pallas_call | solution.py:321
  (34 shorter events, 2.9 us)
Async XLA Ops:
  0.6 24.5 %collective-permute-start.5 = (bf16[1,2048,384]{2,1,0:T(8,128)(2,1)}, bf16[1,2048,384]{2,1,0:T(8,128)(2,1)S(1)}, u32[]{:S(2)}, u32[]{:S(2)}) collective-permute-start(bf16[1,2048,384]{2,1,0:T(8,128)(2,1)} %refs_4_.3), channel_id=1, source_target_pairs={{0,1},{1,0},{2,3},{3,2},{4,5},{5,4},{6,7},{7,6},{8,9},{9,8},{10,11... | collective-permute-start | bytes 4718600 | tf_op jit(solution)/shard_map/ppermute | solution.py:358
  1.2 25.5 %collective-permute-start.6 = (bf16[1,2048,384]{2,1,0:T(8,128)(2,1)}, bf16[1,2048,384]{2,1,0:T(8,128)(2,1)S(1)}, u32[]{:S(2)}, u32[]{:S(2)}) collective-permute-start(bf16[1,2048,384]{2,1,0:T(8,128)(2,1)} %refs_6_.3), channel_id=1, source_target_pairs={{0,1},{1,0},{2,3},{3,2},{4,5},{5,4},{6,7},{7,6},{8,9},{9,8},{10,11... | collective-permute-start | bytes 4718600 | tf_op jit(solution)/shard_map/ppermute | solution.py:358
  1.3 25.5 %collective-permute-start.7 = (bf16[1,2048,384]{2,1,0:T(8,128)(2,1)}, bf16[1,2048,384]{2,1,0:T(8,128)(2,1)S(1)}, u32[]{:S(2)}, u32[]{:S(2)}) collective-permute-start(bf16[1,2048,384]{2,1,0:T(8,128)(2,1)} %refs_8_.3), channel_id=1, source_target_pairs={{0,1},{1,0},{2,3},{3,2},{4,5},{5,4},{6,7},{7,6},{8,9},{9,8},{10,11... | collective-permute-start | bytes 4718600 | tf_op jit(solution)/shard_map/ppermute | solution.py:358
  1.7 16.4 %collective-permute-start = (bf16[32,2048]{1,0:T(8,128)(2,1)}, bf16[32,2048]{1,0:T(8,128)(2,1)S(1)}, u32[]{:S(2)}, u32[]{:S(2)}) collective-permute-start(bf16[32,2048]{1,0:T(8,128)(2,1)} %bitcast.5), channel_id=1, source_target_pairs={{0,8},{1,9},{2,10},{3,11},{4,12},{5,13},{6,14},{7,15},{8,0},{9,1},... | collective-permute-start | bytes 393224 | tf_op jit(solution)/shard_map/ppermute | solution.py:358
  6.1 6.5 %collective-permute-start.1 = (s32[4,16]{1,0:T(4,128)S(1)}, s32[4,16]{1,0:T(4,128)S(1)}, u32[]{:S(2)}, u32[]{:S(2)}) collective-permute-start(s32[4,16]{1,0:T(4,128)S(1)} %pad_add_fusion.picks_ref), channel_id=1, source_target_pairs={{0,8},{1,9},{2,10},{3,11},{4,12},{5,13},{6,14},{7,15},{8,0},{9,1},... | collective-permute-start | bytes 776 | tf_op jit(solution)/shard_map/ppermute | solution.py:358
  6.1 0.9 %copy-start.6 = (bf16[2,16,2048]{2,1,0:T(8,128)(2,1)S(1)}, bf16[2,16,2048]{2,1,0:T(8,128)(2,1)}, u32[]{:S(2)}) copy-start(bf16[2,16,2048]{2,1,0:T(8,128)(2,1)} %param.9) | copy-start | bytes 393220
  7.0 0.7 %copy-start.8 = (s32[8]{0:T(128)S(1)}, s32[8]{0:T(128)}, u32[]{:S(2)}) copy-start(s32[8]{0:T(128)} %home_hbm.1) | copy-start | bytes 100
  7.6 0.7 %copy-start.9 = (s32[16]{0:T(128)S(1)}, s32[16]{0:T(128)}, u32[]{:S(2)}) copy-start(s32[16]{0:T(128)} %new_hbm.1) | copy-start | bytes 196
  12.5 4.6 %collective-permute-start.8 = (bf16[24,2048]{1,0:T(8,128)(2,1)S(1)}, bf16[24,2048]{1,0:T(8,128)(2,1)S(1)}, u32[]{:S(2)}, u32[]{:S(2)}) collective-permute-start(bf16[24,2048]{1,0:T(8,128)(2,1)S(1)} %get-tuple-element.33), channel_id=1, source_target_pairs={{0,2},{1,3},{2,0},{3,1},{4,6},{5,7},{6,4},{7,5},{8,10},{9,11},{10,... | collective-permute-start | bytes 294920 | tf_op jit(solution)/shard_map/ppermute | solution.py:358
  17.2 5.5 %collective-permute-start.9 = (bf16[24,2048]{1,0:T(8,128)(2,1)S(1)}, bf16[24,2048]{1,0:T(8,128)(2,1)S(1)}, u32[]{:S(2)}, u32[]{:S(2)}) collective-permute-start(bf16[24,2048]{1,0:T(8,128)(2,1)S(1)} %get-tuple-element.34), channel_id=1, source_target_pairs={{0,4},{1,5},{2,6},{3,7},{4,0},{5,1},{6,2},{7,3},{8,12},{9,13},{10,... | collective-permute-start | bytes 294920 | tf_op jit(solution)/shard_map/ppermute | solution.py:358
  18.1 5.8 %collective-permute-start.10 = (bf16[24,2048]{1,0:T(8,128)(2,1)S(1)}, bf16[24,2048]{1,0:T(8,128)(2,1)S(1)}, u32[]{:S(2)}, u32[]{:S(2)}) collective-permute-start(bf16[24,2048]{1,0:T(8,128)(2,1)S(1)} %get-tuple-element.35), channel_id=1, source_target_pairs={{0,6},{1,7},{2,4},{3,5},{4,2},{5,3},{6,0},{7,1},{8,14},{9,15},{10,... | collective-permute-start | bytes 294920 | tf_op jit(solution)/shard_map/ppermute | solution.py:358
  22.6 10.5 %collective-permute-start.2 = (bf16[24,2048]{1,0:T(8,128)(2,1)S(1)}, bf16[24,2048]{1,0:T(8,128)(2,1)S(1)}, u32[]{:S(2)}, u32[]{:S(2)}) collective-permute-start(bf16[24,2048]{1,0:T(8,128)(2,1)S(1)} %get-tuple-element.29), channel_id=1, source_target_pairs={{0,2},{1,3},{2,0},{3,1},{4,6},{5,7},{6,4},{7,5},{8,10},{9,11},{10,... | collective-permute-start | bytes 294920 | tf_op jit(solution)/shard_map/ppermute | solution.py:358
  23.9 9.3 %collective-permute-start.3 = (bf16[24,2048]{1,0:T(8,128)(2,1)S(1)}, bf16[24,2048]{1,0:T(8,128)(2,1)S(1)}, u32[]{:S(2)}, u32[]{:S(2)}) collective-permute-start(bf16[24,2048]{1,0:T(8,128)(2,1)S(1)} %get-tuple-element.30), channel_id=1, source_target_pairs={{0,4},{1,5},{2,6},{3,7},{4,0},{5,1},{6,2},{7,3},{8,12},{9,13},{10,... | collective-permute-start | bytes 294920 | tf_op jit(solution)/shard_map/ppermute | solution.py:358
  25.1 8.1 %collective-permute-start.4 = (bf16[24,2048]{1,0:T(8,128)(2,1)S(1)}, bf16[24,2048]{1,0:T(8,128)(2,1)S(1)}, u32[]{:S(2)}, u32[]{:S(2)}) collective-permute-start(bf16[24,2048]{1,0:T(8,128)(2,1)S(1)} %get-tuple-element.31), channel_id=1, source_target_pairs={{0,6},{1,7},{2,4},{3,5},{4,2},{5,3},{6,0},{7,1},{8,14},{9,15},{10,... | collective-permute-start | bytes 294920 | tf_op jit(solution)/shard_map/ppermute | solution.py:358
  26.7 1.4 %copy-start = (bf16[1,2048,384]{2,1,0:T(8,128)(2,1)S(1)}, bf16[1,2048,384]{2,1,0:T(8,128)(2,1)}, u32[]{:S(2)}) copy-start(bf16[1,2048,384]{2,1,0:T(8,128)(2,1)} %refs_4_.3) | copy-start | bytes 4718596
  28.1 1.4 %copy-start.2 = (bf16[1,2048,384]{2,1,0:T(8,128)(2,1)S(1)}, bf16[1,2048,384]{2,1,0:T(8,128)(2,1)}, u32[]{:S(2)}) copy-start(bf16[1,2048,384]{2,1,0:T(8,128)(2,1)} %refs_6_.3) | copy-start | bytes 4718596
  29.6 1.4 %copy-start.4 = (bf16[1,2048,384]{2,1,0:T(8,128)(2,1)S(1)}, bf16[1,2048,384]{2,1,0:T(8,128)(2,1)}, u32[]{:S(2)}) copy-start(bf16[1,2048,384]{2,1,0:T(8,128)(2,1)} %refs_8_.3) | copy-start | bytes 4718596
  31.0 2.2 %copy-start.1 = (bf16[1,2048,384]{2,1,0:T(8,128)(2,1)S(1)}, bf16[1,2048,384]{2,1,0:T(8,128)(2,1)}, u32[]{:S(2)}) copy-start(bf16[1,2048,384]{2,1,0:T(8,128)(2,1)} %refs_4_.3) | copy-start | bytes 4718596
  31.0 2.3 %copy-start.3 = (bf16[1,2048,384]{2,1,0:T(8,128)(2,1)S(1)}, bf16[1,2048,384]{2,1,0:T(8,128)(2,1)}, u32[]{:S(2)}) copy-start(bf16[1,2048,384]{2,1,0:T(8,128)(2,1)} %refs_6_.3) | copy-start | bytes 4718596
  31.0 2.4 %copy-start.5 = (bf16[1,2048,384]{2,1,0:T(8,128)(2,1)S(1)}, bf16[1,2048,384]{2,1,0:T(8,128)(2,1)}, u32[]{:S(2)}) copy-start(bf16[1,2048,384]{2,1,0:T(8,128)(2,1)} %refs_8_.3) | copy-start | bytes 4718596
  33.3 21.5 %copy-start.7 = (f32[2,16,1]{1,2,0:T(1,128)S(1)}, f32[2,16,1]{1,2,0:T(1,128)}, u32[]{:S(2)}) copy-start(f32[2,16,1]{1,2,0:T(1,128)} %param.10) | copy-start | bytes 388
  35.6 4.9 %collective-permute-start.11 = (bf16[24,2048]{1,0:T(8,128)(2,1)S(1)}, bf16[24,2048]{1,0:T(8,128)(2,1)S(1)}, u32[]{:S(2)}, u32[]{:S(2)}) collective-permute-start(bf16[24,2048]{1,0:T(8,128)(2,1)S(1)} %get-tuple-element.38), channel_id=1, source_target_pairs={{0,2},{1,3},{2,0},{3,1},{4,6},{5,7},{6,4},{7,5},{8,10},{9,11},{10,... | collective-permute-start | bytes 294920 | tf_op jit(solution)/shard_map/ppermute | solution.py:358
  36.3 4.6 %collective-permute-start.12 = (bf16[24,2048]{1,0:T(8,128)(2,1)S(1)}, bf16[24,2048]{1,0:T(8,128)(2,1)S(1)}, u32[]{:S(2)}, u32[]{:S(2)}) collective-permute-start(bf16[24,2048]{1,0:T(8,128)(2,1)S(1)} %get-tuple-element.39), channel_id=1, source_target_pairs={{0,4},{1,5},{2,6},{3,7},{4,0},{5,1},{6,2},{7,3},{8,12},{9,13},{10,... | collective-permute-start | bytes 294920 | tf_op jit(solution)/shard_map/ppermute | solution.py:358
  37.5 5.5 %collective-permute-start.13 = (bf16[24,2048]{1,0:T(8,128)(2,1)S(1)}, bf16[24,2048]{1,0:T(8,128)(2,1)S(1)}, u32[]{:S(2)}, u32[]{:S(2)}) collective-permute-start(bf16[24,2048]{1,0:T(8,128)(2,1)S(1)} %get-tuple-element.40), channel_id=1, source_target_pairs={{0,6},{1,7},{2,4},{3,5},{4,2},{5,3},{6,0},{7,1},{8,14},{9,15},{10,... | collective-permute-start | bytes 294920 | tf_op jit(solution)/shard_map/ppermute | solution.py:358
  43.3 11.6 %collective-permute-start.14 = (bf16[32,2048]{1,0:T(8,128)(2,1)S(1)}, bf16[32,2048]{1,0:T(8,128)(2,1)S(1)}, u32[]{:S(2)}, u32[]{:S(2)}) collective-permute-start(bf16[32,2048]{1,0:T(8,128)(2,1)S(1)} %shard_map.108), channel_id=1, source_target_pairs={{0,8},{1,9},{2,10},{3,11},{4,12},{5,13},{6,14},{7,15},{8,0},{9,1},... | collective-permute-start | bytes 393224 | tf_op jit(solution)/shard_map/ppermute | solution.py:358
  47.7 4.7 %collective-permute-start.16 = (bf16[24,2048]{1,0:T(8,128)(2,1)S(1)}, bf16[24,2048]{1,0:T(8,128)(2,1)S(1)}, u32[]{:S(2)}, u32[]{:S(2)}) collective-permute-start(bf16[24,2048]{1,0:T(8,128)(2,1)S(1)} %get-tuple-element.43), channel_id=1, source_target_pairs={{0,2},{1,3},{2,0},{3,1},{4,6},{5,7},{6,4},{7,5},{8,10},{9,11},{10,... | collective-permute-start | bytes 294920 | tf_op jit(solution)/shard_map/ppermute | solution.py:358
  48.0 4.6 %collective-permute-start.17 = (bf16[24,2048]{1,0:T(8,128)(2,1)S(1)}, bf16[24,2048]{1,0:T(8,128)(2,1)S(1)}, u32[]{:S(2)}, u32[]{:S(2)}) collective-permute-start(bf16[24,2048]{1,0:T(8,128)(2,1)S(1)} %get-tuple-element.44), channel_id=1, source_target_pairs={{0,4},{1,5},{2,6},{3,7},{4,0},{5,1},{6,2},{7,3},{8,12},{9,13},{10,... | collective-permute-start | bytes 294920 | tf_op jit(solution)/shard_map/ppermute | solution.py:358
  49.1 5.8 %collective-permute-start.18 = (bf16[24,2048]{1,0:T(8,128)(2,1)S(1)}, bf16[24,2048]{1,0:T(8,128)(2,1)S(1)}, u32[]{:S(2)}, u32[]{:S(2)}) collective-permute-start(bf16[24,2048]{1,0:T(8,128)(2,1)S(1)} %get-tuple-element.45), channel_id=1, source_target_pairs={{0,6},{1,7},{2,4},{3,5},{4,2},{5,3},{6,0},{7,1},{8,14},{9,15},{10,... | collective-permute-start | bytes 294920 | tf_op jit(solution)/shard_map/ppermute | solution.py:358
  51.2 1.2 %collective-permute-start.15 = (s32[8,128]{1,0:T(8,128)S(1)}, s32[8,128]{1,0:T(8,128)S(1)}, u32[]{:S(2)}, u32[]{:S(2)}) collective-permute-start(s32[8,128]{1,0:T(8,128)S(1)} %get-tuple-element.41.load_ref), channel_id=1, source_target_pairs={{0,1},{1,0},{2,3},{3,2},{4,5},{5,4},{6,7},{7,6},{8,9},{9,8},{10,11... | collective-permute-start | bytes 12296 | tf_op jit(solution)/shard_map/ppermute | solution.py:358
where the time goes:
time: 56 us; the launch traced here: 55.8 us
  starting transfers between devices  24.3 us (43%)
  waiting for transfers between devices  16.1 us (29%)
  Pallas kernels  7.41 us (13%)
  local copies, waits for them, and re-layouts  6.53 us (12%)
  between operations  0.74 us (1%)
  other arithmetic  0.7 us (1%)
    ppermute x19, starting transfers between devices, swap(): return lax.ppermute(value, 'expert', swapped(size, bits))  24.3 us
    ppermute x19, waiting for transfers between devices, swap(): return lax.ppermute(value, 'expert', swapped(size, bits))  16.1 us
    unnamed x20, local copies, waits for them, and re-layouts  6.53 us
    pallas_call x2, Pallas kernels, run_expert(): pl.pallas_call(functools.partial(expert_kernel, meta), out_shape=[jax.Sha...  4.44 us
    pallas_call x1, Pallas kernels, pick_own(): pl.pallas_call(functools.partial(pick_own_kernel, cap), out_shape=shapes...  1.3 us
    pallas_call x2, Pallas kernels, merge_rows(): pl.pallas_call(kernel, out_shape=shapes, in_specs=[pl.BlockSpec(memory_sp...  1.14 us
  transfers between devices with their start and end apart: 19, of which 10 were waited for; matrix products, arithmetic and copies ran while one was open for 1% of the time, Pallas kernels for 7%

commit v1 on v0

--- a/solution.py
+++ b/solution.py
@@ -17,7 +17,6 @@
 VMEM = pltpu.VMEM
 SMEM = pltpu.SMEM
 HBM = pltpu.MemorySpace.HBM
-FETCH = 16 << 20
 
 
 def slot_rank(new_expert, me):
@@ -187,7 +186,9 @@
     block = jax.ShapeDtypeStruct((high, width), jnp.bfloat16)
     sel = jax.ShapeDtypeStruct((SQUARE * high, count), jnp.bfloat16)
     cost = pl.CostEstimate(
-        flops=2 * SQUARE * high * count * width, bytes_accessed=FETCH, transcendentals=0
+        flops=2 * SQUARE * high * count * width,
+        bytes_accessed=4 * SQUARE * high * width,
+        transcendentals=0,
     )
     return [block] * SQUARE + [sel], cost
 
@@ -207,7 +208,7 @@
         ],
         cost_estimate=cost,
         compiler_params=pltpu.CompilerParams(vmem_limit_bytes=SMALL),
-    )(home, new, x, picks)
+    )(*(pltpu.with_memory_space_constraint(value, HBM) for value in (home, new, x)), picks)
 
 
 def pick_far(cap, experts, table, x, picks):
@@ -222,58 +223,64 @@
     )(table, x, picks)
 
 
-def expert_kernel(meta, *refs):
-    blocks, refs = refs[:SQUARE], refs[SQUARE:]
-    gates, ups, downs, prior_ref = refs[:2], refs[2:4], refs[4:6], refs[6]
-    outs, load_ref = refs[7 : 7 + SQUARE], refs[7 + SQUARE]
+def expert_kernel(meta, count, *refs):
+    blocks, refs = refs[:count], refs[count:]
+    panels_hbm, panels_far, refs = refs[:3], refs[3:6], refs[6:]
+    outs, load_ref, panels, sem = refs[:count], refs[count], refs[count + 1 : count + 4], refs[count + 4]
+    copies = [
+        pltpu.make_async_copy(source, target, sem.at[index])
+        for index, (source, target) in enumerate(zip(panels_hbm, panels))
+    ]
+    for copy in copies:
+        copy.start()
     high = blocks[0].shape[0]
     x = jnp.concatenate([block[...] for block in blocks], axis=0)
     contract = (((1,), (1,)), ((), ()))
-    total = None
-    for half in range(2):
-        gate = jnp.dot(x, gates[half][0], preferred_element_type=jnp.float32)
-        up = jnp.dot(x, ups[half][0], preferred_element_type=jnp.float32)
+    start = meta - meta % 8
+    load = jnp.zeros(load_ref.shape, jnp.float32)
+    for block in blocks:
+        load = load + block[start : start + 8, :LANES].astype(jnp.float32)
+    load_ref[...] = load.astype(jnp.int32)
+
+    def half(gate_ref, up_ref, down_ref, ready):
+        ready(0)
+        ready(1)
+        gate = jnp.dot(x, gate_ref[0], preferred_element_type=jnp.float32)
+        up = jnp.dot(x, up_ref[0], preferred_element_type=jnp.float32)
         hidden = (gate / (1.0 + jnp.exp(-gate)) * up).astype(jnp.bfloat16)
-        part = lax.dot_general(
-            hidden, downs[half][0], contract, preferred_element_type=jnp.float32
-        )
-        total = part if half == 0 else total + part
+        ready(2)
+        return lax.dot_general(hidden, down_ref[0], contract, preferred_element_type=jnp.float32)
+
+    total = half(*panels_far, lambda index: None)
+    total = total + half(*panels, lambda index: copies[index].wait())
     total = total.astype(jnp.bfloat16)
-    for q in range(SQUARE):
+    for q in range(count):
         outs[q][...] = total[q * high : (q + 1) * high]
-    load = prior_ref[...]
-    start = meta - meta % 8
-    for block in blocks:
-        load = load + block[start : start + 8, :LANES].astype(jnp.int32)
-    load_ref[...] = load
-
-
-def run_expert(meta, blocks, panels, far_panels, prior):
+
+
+def run_expert(meta, blocks, panels, panels_far):
     high, width = blocks[0].shape
     half = panels[0].shape[2]
-    rows = SQUARE * high
+    count = len(blocks)
+    rows = count * high
+    held = [pltpu.with_memory_space_constraint(panel, HBM) for panel in panels]
     return pl.pallas_call(
-        functools.partial(expert_kernel, meta),
-        out_shape=[jax.ShapeDtypeStruct((high, width), jnp.bfloat16)] * SQUARE
-        + [jax.ShapeDtypeStruct(prior.shape, jnp.int32)],
-        in_specs=[pl.BlockSpec(memory_space=VMEM)] * (SQUARE + 7),
-        out_specs=[pl.BlockSpec(memory_space=VMEM)] * (SQUARE + 1),
+        functools.partial(expert_kernel, meta, count),
+        out_shape=[jax.ShapeDtypeStruct((high, width), jnp.bfloat16)] * count
+        + [jax.ShapeDtypeStruct((8, LANES), jnp.int32)],
+        in_specs=[pl.BlockSpec(memory_space=VMEM)] * count
+        + [pl.BlockSpec(memory_space=HBM)] * 3
+        + [pl.BlockSpec(memory_space=VMEM)] * 3,
+        out_specs=[pl.BlockSpec(memory_space=VMEM)] * (count + 1),
+        scratch_shapes=[VMEM(panel.shape, panel.dtype) for panel in panels]
+        + [pltpu.SemaphoreType.DMA((3,))],
         cost_estimate=pl.CostEstimate(
             flops=2 * rows * width * half * 6,
             bytes_accessed=6 * 2 * width * half + 4 * rows * width,
             transcendentals=2 * rows * half,
         ),
         compiler_params=pltpu.CompilerParams(vmem_limit_bytes=LARGE),
-    )(
-        *blocks,
-        panels[0],
-        far_panels[0],
-        panels[1],
-        far_panels[1],
-        panels[2],
-        far_panels[2],
-        prior,
-    )
+    )(*blocks, *held, *panels_far)
 
 
 def chosen(sel_ref, blocks):
@@ -372,9 +379,8 @@
     blocks = around(blocks)
     *blocks_far, sel_far = pick_far(cap, old_home.shape[0], table, x_far, picks_far)
     blocks_far = around(blocks_far)
-    prior = jnp.zeros((8, LANES), jnp.int32)
-    *results, load = run_expert(meta, blocks, panels, panels_far, prior)
-    *results_far, load = run_expert(meta, blocks_far, panels, panels_far, load)
+    *results, load = run_expert(meta, blocks + blocks_far, panels, panels_far)
+    results, results_far = results[:SQUARE], results[SQUARE:]
     results_far = around(results_far)
     results = around(results)
     load_far = swap(load, 1)

time: 56 us -> 54.6 us (0.975)
  local copies, waits for them, and re-layouts: 6.53 us -> 0.01 us
  waiting for transfers between devices: 16.1 us -> 22.1 us
  starting transfers between devices: 24.3 us -> 22.8 us
  Pallas kernels: 7.41 us -> 8.04 us
    unnamed x20 -> x2, local copies, waits for them, and re-layouts: 6.53 us -> 0.01 us
    ppermute x19, waiting for transfers between devices: 16.1 us -> 22.1 us  [swap(): return lax.ppermute(value, 'expert', swapped(size, bits))]
    ppermute x19, starting transfers between devices: 24.3 us -> 22.8 us  [swap(): return lax.ppermute(value, 'expert', swapped(size, bits))]
    pallas_call x2 -> x1, Pallas kernels: 4.44 us -> 4.94 us  [run_expert(): pl.pallas_call(functools.partial(expert_kernel, meta, count), out_shape=[...]
  transfers between devices with their start and end apart: 19 -> 19, of which waited for: 10 -> 11; matrix products, arithmetic and copies ran while one was open for 1% -> 1% of each run, Pallas kernels for 7% -> 4%
where the time goes in v1:
time: 54.6 us; the launch traced here: 54.4 us
  starting transfers between devices  22.8 us (42%)
  waiting for transfers between devices  22.1 us (40%)
  Pallas kernels  8.04 us (15%)
  other arithmetic  0.7 us (1%)
  between operations  0.69 us (1%)
    ppermute x19, starting transfers between devices, swap(): return lax.ppermute(value, 'expert', swapped(size, bits))  22.8 us
    ppermute x19, waiting for transfers between devices, swap(): return lax.ppermute(value, 'expert', swapped(size, bits))  22.1 us
    pallas_call x1, Pallas kernels, run_expert(): pl.pallas_call(functools.partial(expert_kernel, meta, count), out_shape=[...  4.94 us
    pallas_call x1, Pallas kernels, pick_own(): pl.pallas_call(functools.partial(pick_own_kernel, cap), out_shape=shapes...  1.43 us
    pallas_call x2, Pallas kernels, merge_rows(): pl.pallas_call(kernel, out_shape=shapes, in_specs=[pl.BlockSpec(memory_sp...  1.14 us
  transfers between devices with their start and end apart: 19, of which 11 were waited for; matrix products, arithmetic and copies ran while one was open for 1% of the time, Pallas kernels for 4%

profile of v1, /device:TPU:0, one launch (start us, length us, event | category | flops | bytes accessed | tf_op | source)
XLA Modules:
  0.0 54.4 jit_solution(14670427991088900307)
XLA Ops:
  0.6 0.6 %collective-permute-start.8 = (bf16[1,2048,384]{2,1,0:T(8,128)(2,1)}, bf16[1,2048,384]{2,1,0:T(8,128)(2,1)S(1)}, u32[]{:S(2)}, u32[]{:S(2)}) collective-permute-start(bf16[1,2048,384]{2,1,0:T(8,128)(2,1)} %refs_8_.1), channel_id=1, source_target_pairs={{0,1},{1,0},{2,3},{3,2},{4,5},{5,4},{6,7},{7,6},{8,9},{9,8},{10,11... | collective-permute-start | bytes 4718600 | tf_op jit(solution)/shard_map/ppermute | solution.py:365
  1.3 0.4 collective-permute-start.10
  1.7 3.7 %collective-permute-start = (bf16[32,2048]{1,0:T(8,128)(2,1)}, bf16[32,2048]{1,0:T(8,128)(2,1)S(1)}, u32[]{:S(2)}, u32[]{:S(2)}) collective-permute-start(bf16[32,2048]{1,0:T(8,128)(2,1)} %bitcast.6), channel_id=1, source_target_pairs={{0,8},{1,9},{2,10},{3,11},{4,12},{5,13},{6,14},{7,15},{8,0},{9,1},... | collective-permute-start | bytes 393224 | tf_op jit(solution)/shard_map/ppermute | solution.py:365
  5.4 0.7 %pad_add_fusion.picks_ref = s32[4,16]{1,0:T(4,128)S(1)} fusion(s32[2,16]{1,0:T(2,128)} %bitcast.8, s32[2,16]{1,0:T(2,128)} %bitcast.9), kind=kLoop, calls=%fused_computation | loop fusion | flops 64 | bytes 512 | tf_op jit(solution)/shard_map/concatenate | solution.py:372
  6.1 1.4 %shard_map.104 = (bf16[24,2048]{1,0:T(8,128)(2,1)S(1)}, bf16[24,2048]{1,0:T(8,128)(2,1)S(1)}, bf16[24,2048]{1,0:T(8,128)(2,1)S(1)}, bf16[24,2048]{1,0:T(8,128)(2...) custom-call(s32[8]{0:T(128)} %home_hbm.1, s32[16]{0:T(128)} %new_hbm.1, bf16[32,2048]{1,0:T(8,128)(2,1)} %bitcast.7, ...), custom_call_target="tpu_custom_call" | custom-call | flops 12582912 | bytes 786432 | tf_op jit(solution)/shard_map/pallas_call | solution.py:198
  7.5 5.0 %collective-permute-done.1.picks_ref = s32[4,16]{1,0:T(4,128)S(1)} collective-permute-done((s32[4,16]{1,0:T(4,128)S(1)}, s32[4,16]{1,0:T(4,128)S(1)}, u32[]{:S(2)}, u32[]{:S(2)}) %collective-permute-start.1) | collective-permute-done | bytes 288 | tf_op jit(solution)/shard_map/ppermute | solution.py:365
  12.5 1.5 %collective-permute-start.2 = (bf16[24,2048]{1,0:T(8,128)(2,1)S(1)}, bf16[24,2048]{1,0:T(8,128)(2,1)S(1)}, u32[]{:S(2)}, u32[]{:S(2)}) collective-permute-start(bf16[24,2048]{1,0:T(8,128)(2,1)S(1)} %get-tuple-element.28), channel_id=1, source_target_pairs={{0,2},{1,3},{2,0},{3,1},{4,6},{5,7},{6,4},{7,5},{8,10},{9,11},{10,... | collective-permute-start | bytes 294920 | tf_op jit(solution)/shard_map/ppermute | solution.py:365
  14.1 0.8 %collective-permute-start.3 = (bf16[24,2048]{1,0:T(8,128)(2,1)S(1)}, bf16[24,2048]{1,0:T(8,128)(2,1)S(1)}, u32[]{:S(2)}, u32[]{:S(2)}) collective-permute-start(bf16[24,2048]{1,0:T(8,128)(2,1)S(1)} %get-tuple-element.29), channel_id=1, source_target_pairs={{0,4},{1,5},{2,6},{3,7},{4,0},{5,1},{6,2},{7,3},{8,12},{9,13},{10,... | collective-permute-start | bytes 294920 | tf_op jit(solution)/shard_map/ppermute | solution.py:365
  14.9 0.5 shard_map.105
  15.4 1.8 %collective-permute-done.2.refs_1_ = bf16[24,2048]{1,0:T(8,128)(2,1)S(1)} collective-permute-done((bf16[24,2048]{1,0:T(8,128)(2,1)S(1)}, bf16[24,2048]{1,0:T(8,128)(2,1)S(1)}, u32[]{:S(2)}, u32[]{:S(2)}) %collective-permute-start.2) | collective-permute-done | bytes 98336 | tf_op jit(solution)/shard_map/ppermute | solution.py:365
  17.2 1.9 %collective-permute-start.4 = (bf16[24,2048]{1,0:T(8,128)(2,1)S(1)}, bf16[24,2048]{1,0:T(8,128)(2,1)S(1)}, u32[]{:S(2)}, u32[]{:S(2)}) collective-permute-start(bf16[24,2048]{1,0:T(8,128)(2,1)S(1)} %get-tuple-element.30), channel_id=1, source_target_pairs={{0,6},{1,7},{2,4},{3,5},{4,2},{5,3},{6,0},{7,1},{8,14},{9,15},{10,... | collective-permute-start | bytes 294920 | tf_op jit(solution)/shard_map/ppermute | solution.py:365
  19.0 0.5 collective-permute-start.5
  19.6 3.1 %collective-permute-done.4.refs_3_ = bf16[24,2048]{1,0:T(8,128)(2,1)S(1)} collective-permute-done((bf16[24,2048]{1,0:T(8,128)(2,1)S(1)}, bf16[24,2048]{1,0:T(8,128)(2,1)S(1)}, u32[]{:S(2)}, u32[]{:S(2)}) %collective-permute-start.4) | collective-permute-done | bytes 98336 | tf_op jit(solution)/shard_map/ppermute | solution.py:365
  22.7 1.0 %collective-permute-start.6 = (bf16[24,2048]{1,0:T(8,128)(2,1)S(1)}, bf16[24,2048]{1,0:T(8,128)(2,1)S(1)}, u32[]{:S(2)}, u32[]{:S(2)}) collective-permute-start(bf16[24,2048]{1,0:T(8,128)(2,1)S(1)} %get-tuple-element.33), channel_id=1, source_target_pairs={{0,4},{1,5},{2,6},{3,7},{4,0},{5,1},{6,2},{7,3},{8,12},{9,13},{10,... | collective-permute-start | bytes 294920 | tf_op jit(solution)/shard_map/ppermute | solution.py:365
  23.7 2.1 %collective-permute-start.7 = (bf16[24,2048]{1,0:T(8,128)(2,1)S(1)}, bf16[24,2048]{1,0:T(8,128)(2,1)S(1)}, u32[]{:S(2)}, u32[]{:S(2)}) collective-permute-start(bf16[24,2048]{1,0:T(8,128)(2,1)S(1)} %get-tuple-element.34), channel_id=1, source_target_pairs={{0,6},{1,7},{2,4},{3,5},{4,2},{5,3},{6,0},{7,1},{8,14},{9,15},{10,... | collective-permute-start | bytes 294920 | tf_op jit(solution)/shard_map/ppermute | solution.py:365
  25.8 1.5 %collective-permute-done.6.refs_6_ = bf16[24,2048]{1,0:T(8,128)(2,1)S(1)} collective-permute-done((bf16[24,2048]{1,0:T(8,128)(2,1)S(1)}, bf16[24,2048]{1,0:T(8,128)(2,1)S(1)}, u32[]{:S(2)}, u32[]{:S(2)}) %collective-permute-start.6) | collective-permute-done | bytes 98336 | tf_op jit(solution)/shard_map/ppermute | solution.py:365
  27.3 2.1 %collective-permute-done.7.refs_7_ = bf16[24,2048]{1,0:T(8,128)(2,1)S(1)} collective-permute-done((bf16[24,2048]{1,0:T(8,128)(2,1)S(1)}, bf16[24,2048]{1,0:T(8,128)(2,1)S(1)}, u32[]{:S(2)}, u32[]{:S(2)}) %collective-permute-start.7) | collective-permute-done | bytes 98336 | tf_op jit(solution)/shard_map/ppermute | solution.py:365
  29.5 4.9 %shard_map.106 = (bf16[24,2048]{1,0:T(8,128)(2,1)S(1)}, bf16[24,2048]{1,0:T(8,128)(2,1)S(1)}, bf16[24,2048]{1,0:T(8,128)(2,1)S(1)}, bf16[24,2048]{1,0:T(8,128)(2...) custom-call(bf16[24,2048]{1,0:T(8,128)(2,1)S(1)} %get-tuple-element., ...), custom_call_target="tpu_custom_call" | custom-call | flops 1811939328 | bytes 11010048 | tf_op jit(solution)/shard_map/pallas_call | solution.py:267
  34.4 1.4 %collective-permute-start.11 = (bf16[24,2048]{1,0:T(8,128)(2,1)S(1)}, bf16[24,2048]{1,0:T(8,128)(2,1)S(1)}, u32[]{:S(2)}, u32[]{:S(2)}) collective-permute-start(bf16[24,2048]{1,0:T(8,128)(2,1)S(1)} %get-tuple-element.36), channel_id=1, source_target_pairs={{0,2},{1,3},{2,0},{3,1},{4,6},{5,7},{6,4},{7,5},{8,10},{9,11},{10,... | collective-permute-start | bytes 294920 | tf_op jit(solution)/shard_map/ppermute | solution.py:365
  35.8 1.1 %collective-permute-start.12 = (bf16[24,2048]{1,0:T(8,128)(2,1)S(1)}, bf16[24,2048]{1,0:T(8,128)(2,1)S(1)}, u32[]{:S(2)}, u32[]{:S(2)}) collective-permute-start(bf16[24,2048]{1,0:T(8,128)(2,1)S(1)} %get-tuple-element.37), channel_id=1, source_target_pairs={{0,4},{1,5},{2,6},{3,7},{4,0},{5,1},{6,2},{7,3},{8,12},{9,13},{10,... | collective-permute-start | bytes 294920 | tf_op jit(solution)/shard_map/ppermute | solution.py:365
  36.9 1.1 %collective-permute-start.13 = (bf16[24,2048]{1,0:T(8,128)(2,1)S(1)}, bf16[24,2048]{1,0:T(8,128)(2,1)S(1)}, u32[]{:S(2)}, u32[]{:S(2)}) collective-permute-start(bf16[24,2048]{1,0:T(8,128)(2,1)S(1)} %get-tuple-element.38), channel_id=1, source_target_pairs={{0,6},{1,7},{2,4},{3,5},{4,2},{5,3},{6,0},{7,1},{8,14},{9,15},{10,... | collective-permute-start | bytes 294920 | tf_op jit(solution)/shard_map/ppermute | solution.py:365
  38.0 1.7 %collective-permute-done.11.refs_1_ = bf16[24,2048]{1,0:T(8,128)(2,1)S(1)} collective-permute-done((bf16[24,2048]{1,0:T(8,128)(2,1)S(1)}, bf16[24,2048]{1,0:T(8,128)(2,1)S(1)}, u32[]{:S(2)}, u32[]{:S(2)}) %collective-permute-start.11) | collective-permute-done | bytes 98336 | tf_op jit(solution)/shard_map/ppermute | solution.py:365
  39.7 0.7 %collective-permute-done.12.refs_2_ = bf16[24,2048]{1,0:T(8,128)(2,1)S(1)} collective-permute-done((bf16[24,2048]{1,0:T(8,128)(2,1)S(1)}, bf16[24,2048]{1,0:T(8,128)(2,1)S(1)}, u32[]{:S(2)}, u32[]{:S(2)}) %collective-permute-start.12) | collective-permute-done | bytes 98336 | tf_op jit(solution)/shard_map/ppermute | solution.py:365
  40.4 2.0 %collective-permute-done.13.refs_3_ = bf16[24,2048]{1,0:T(8,128)(2,1)S(1)} collective-permute-done((bf16[24,2048]{1,0:T(8,128)(2,1)S(1)}, bf16[24,2048]{1,0:T(8,128)(2,1)S(1)}, u32[]{:S(2)}, u32[]{:S(2)}) %collective-permute-start.13) | collective-permute-done | bytes 98336 | tf_op jit(solution)/shard_map/ppermute | solution.py:365
  42.4 0.2 shard_map.107
  42.7 2.7 %collective-permute-start.14 = (bf16[32,2048]{1,0:T(8,128)(2,1)S(1)}, bf16[32,2048]{1,0:T(8,128)(2,1)S(1)}, u32[]{:S(2)}, u32[]{:S(2)}) collective-permute-start(bf16[32,2048]{1,0:T(8,128)(2,1)S(1)} %shard_map.107), channel_id=1, source_target_pairs={{0,8},{1,9},{2,10},{3,11},{4,12},{5,13},{6,14},{7,15},{8,0},{9,1},... | collective-permute-start | bytes 393224 | tf_op jit(solution)/shard_map/ppermute | solution.py:365
  45.4 2.6 %collective-permute-start.16 = (bf16[24,2048]{1,0:T(8,128)(2,1)S(1)}, bf16[24,2048]{1,0:T(8,128)(2,1)S(1)}, u32[]{:S(2)}, u32[]{:S(2)}) collective-permute-start(bf16[24,2048]{1,0:T(8,128)(2,1)S(1)} %get-tuple-element.41), channel_id=1, source_target_pairs={{0,2},{1,3},{2,0},{3,1},{4,6},{5,7},{6,4},{7,5},{8,10},{9,11},{10,... | collective-permute-start | bytes 294920 | tf_op jit(solution)/shard_map/ppermute | solution.py:365
  48.0 1.5 %collective-permute-start.18 = (bf16[24,2048]{1,0:T(8,128)(2,1)S(1)}, bf16[24,2048]{1,0:T(8,128)(2,1)S(1)}, u32[]{:S(2)}, u32[]{:S(2)}) collective-permute-start(bf16[24,2048]{1,0:T(8,128)(2,1)S(1)} %get-tuple-element.43), channel_id=1, source_target_pairs={{0,6},{1,7},{2,4},{3,5},{4,2},{5,3},{6,0},{7,1},{8,14},{9,15},{10,... | collective-permute-start | bytes 294920 | tf_op jit(solution)/shard_map/ppermute | solution.py:365
  49.4 1.2 %collective-permute-done.15.load_far_ref = s32[8,128]{1,0:T(8,128)S(1)} collective-permute-done((s32[8,128]{1,0:T(8,128)S(1)}, s32[8,128]{1,0:T(8,128)S(1)}, u32[]{:S(2)}, u32[]{:S(2)}) %collective-permute-start.15) | collective-permute-done | bytes 4128 | tf_op jit(solution)/shard_map/ppermute | solution.py:365
  50.6 2.0 %collective-permute-done.17.refs_2_ = bf16[24,2048]{1,0:T(8,128)(2,1)S(1)} collective-permute-done((bf16[24,2048]{1,0:T(8,128)(2,1)S(1)}, bf16[24,2048]{1,0:T(8,128)(2,1)S(1)}, u32[]{:S(2)}, u32[]{:S(2)}) %collective-permute-start.17) | collective-permute-done | bytes 98336 | tf_op jit(solution)/shard_map/ppermute | solution.py:365
  52.6 0.9 %collective-permute-done.18.refs_3_ = bf16[24,2048]{1,0:T(8,128)(2,1)S(1)} collective-permute-done((bf16[24,2048]{1,0:T(8,128)(2,1)S(1)}, bf16[24,2048]{1,0:T(8,128)(2,1)S(1)}, u32[]{:S(2)}, u32[]{:S(2)}) %collective-permute-start.18) | collective-permute-done | bytes 98336 | tf_op jit(solution)/shard_map/ppermute | solution.py:365
  53.5 0.9 %shard_map.108 = (bf16[32,2048]{1,0:T(8,128)(2,1)}, s32[1]{0:T(128)}) custom-call(bf16[96,32]{1,0:T(8,128)(2,1)S(1)} %get-tuple-element.24.sel_ref, f32[2,16]{1,0:T(2,128)S(1)} %bitcast.5, bf16[32,2048]{1,0:T(8,128)(2,1)S(1)} %collective-permute-done.14.back_ref, s32[8,128]{1,0:T(8,128)S(1)} %get-tuple-element.39.load_ref, ...), custom_call_target="tpu_custom_call" | custom-call | flops 12582912 | bytes 524288 | tf_op jit(solution)/shard_map/pallas_call | solution.py:328
  (14 shorter events, 0.1 us)
Async XLA Ops:
  0.6 28.8 %collective-permute-start.8 = (bf16[1,2048,384]{2,1,0:T(8,128)(2,1)}, bf16[1,2048,384]{2,1,0:T(8,128)(2,1)S(1)}, u32[]{:S(2)}, u32[]{:S(2)}) collective-permute-start(bf16[1,2048,384]{2,1,0:T(8,128)(2,1)} %refs_8_.1), channel_id=1, source_target_pairs={{0,1},{1,0},{2,3},{3,2},{4,5},{5,4},{6,7},{7,6},{8,9},{9,8},{10,11... | collective-permute-start | bytes 4718600 | tf_op jit(solution)/shard_map/ppermute | solution.py:365
  1.2 28.3 %collective-permute-start.9 = (bf16[1,2048,384]{2,1,0:T(8,128)(2,1)}, bf16[1,2048,384]{2,1,0:T(8,128)(2,1)S(1)}, u32[]{:S(2)}, u32[]{:S(2)}) collective-permute-start(bf16[1,2048,384]{2,1,0:T(8,128)(2,1)} %refs_9_.1), channel_id=1, source_target_pairs={{0,1},{1,0},{2,3},{3,2},{4,5},{5,4},{6,7},{7,6},{8,9},{9,8},{10,11... | collective-permute-start | bytes 4718600 | tf_op jit(solution)/shard_map/ppermute | solution.py:365
  1.3 28.2 %collective-permute-start.10 = (bf16[1,2048,384]{2,1,0:T(8,128)(2,1)}, bf16[1,2048,384]{2,1,0:T(8,128)(2,1)S(1)}, u32[]{:S(2)}, u32[]{:S(2)}) collective-permute-start(bf16[1,2048,384]{2,1,0:T(8,128)(2,1)} %refs_10_.1), channel_id=1, source_target_pairs={{0,1},{1,0},{2,3},{3,2},{4,5},{5,4},{6,7},{7,6},{8,9},{9,8},{10,11... | collective-permute-start | bytes 4718600 | tf_op jit(solution)/shard_map/ppermute | solution.py:365
  1.7 12.4 %collective-permute-start = (bf16[32,2048]{1,0:T(8,128)(2,1)}, bf16[32,2048]{1,0:T(8,128)(2,1)S(1)}, u32[]{:S(2)}, u32[]{:S(2)}) collective-permute-start(bf16[32,2048]{1,0:T(8,128)(2,1)} %bitcast.6), channel_id=1, source_target_pairs={{0,8},{1,9},{2,10},{3,11},{4,12},{5,13},{6,14},{7,15},{8,0},{9,1},... | collective-permute-start | bytes 393224 | tf_op jit(solution)/shard_map/ppermute | solution.py:365
  6.1 6.5 %collective-permute-start.1 = (s32[4,16]{1,0:T(4,128)S(1)}, s32[4,16]{1,0:T(4,128)S(1)}, u32[]{:S(2)}, u32[]{:S(2)}) collective-permute-start(s32[4,16]{1,0:T(4,128)S(1)} %pad_add_fusion.picks_ref), channel_id=1, source_target_pairs={{0,8},{1,9},{2,10},{3,11},{4,12},{5,13},{6,14},{7,15},{8,0},{9,1},... | collective-permute-start | bytes 776 | tf_op jit(solution)/shard_map/ppermute | solution.py:365
  12.5 4.6 %collective-permute-start.2 = (bf16[24,2048]{1,0:T(8,128)(2,1)S(1)}, bf16[24,2048]{1,0:T(8,128)(2,1)S(1)}, u32[]{:S(2)}, u32[]{:S(2)}) collective-permute-start(bf16[24,2048]{1,0:T(8,128)(2,1)S(1)} %get-tuple-element.28), channel_id=1, source_target_pairs={{0,2},{1,3},{2,0},{3,1},{4,6},{5,7},{6,4},{7,5},{8,10},{9,11},{10,... | collective-permute-start | bytes 294920 | tf_op jit(solution)/shard_map/ppermute | solution.py:365
  14.1 4.9 %collective-permute-start.3 = (bf16[24,2048]{1,0:T(8,128)(2,1)S(1)}, bf16[24,2048]{1,0:T(8,128)(2,1)S(1)}, u32[]{:S(2)}, u32[]{:S(2)}) collective-permute-start(bf16[24,2048]{1,0:T(8,128)(2,1)S(1)} %get-tuple-element.29), channel_id=1, source_target_pairs={{0,4},{1,5},{2,6},{3,7},{4,0},{5,1},{6,2},{7,3},{8,12},{9,13},{10,... | collective-permute-start | bytes 294920 | tf_op jit(solution)/shard_map/ppermute | solution.py:365
  17.2 5.5 %collective-permute-start.4 = (bf16[24,2048]{1,0:T(8,128)(2,1)S(1)}, bf16[24,2048]{1,0:T(8,128)(2,1)S(1)}, u32[]{:S(2)}, u32[]{:S(2)}) collective-permute-start(bf16[24,2048]{1,0:T(8,128)(2,1)S(1)} %get-tuple-element.30), channel_id=1, source_target_pairs={{0,6},{1,7},{2,4},{3,5},{4,2},{5,3},{6,0},{7,1},{8,14},{9,15},{10,... | collective-permute-start | bytes 294920 | tf_op jit(solution)/shard_map/ppermute | solution.py:365
  19.0 4.7 %collective-permute-start.5 = (bf16[24,2048]{1,0:T(8,128)(2,1)S(1)}, bf16[24,2048]{1,0:T(8,128)(2,1)S(1)}, u32[]{:S(2)}, u32[]{:S(2)}) collective-permute-start(bf16[24,2048]{1,0:T(8,128)(2,1)S(1)} %get-tuple-element.32), channel_id=1, source_target_pairs={{0,2},{1,3},{2,0},{3,1},{4,6},{5,7},{6,4},{7,5},{8,10},{9,11},{10,... | collective-permute-start | bytes 294920 | tf_op jit(solution)/shard_map/ppermute | solution.py:365
  22.7 4.6 %collective-permute-start.6 = (bf16[24,2048]{1,0:T(8,128)(2,1)S(1)}, bf16[24,2048]{1,0:T(8,128)(2,1)S(1)}, u32[]{:S(2)}, u32[]{:S(2)}) collective-permute-start(bf16[24,2048]{1,0:T(8,128)(2,1)S(1)} %get-tuple-element.33), channel_id=1, source_target_pairs={{0,4},{1,5},{2,6},{3,7},{4,0},{5,1},{6,2},{7,3},{8,12},{9,13},{10,... | collective-permute-start | bytes 294920 | tf_op jit(solution)/shard_map/ppermute | solution.py:365
  23.7 5.7 %collective-permute-start.7 = (bf16[24,2048]{1,0:T(8,128)(2,1)S(1)}, bf16[24,2048]{1,0:T(8,128)(2,1)S(1)}, u32[]{:S(2)}, u32[]{:S(2)}) collective-permute-start(bf16[24,2048]{1,0:T(8,128)(2,1)S(1)} %get-tuple-element.34), channel_id=1, source_target_pairs={{0,6},{1,7},{2,4},{3,5},{4,2},{5,3},{6,0},{7,1},{8,14},{9,15},{10,... | collective-permute-start | bytes 294920 | tf_op jit(solution)/shard_map/ppermute | solution.py:365
  29.4 24.0 %copy-start = (f32[2,16,1]{1,2,0:T(1,128)S(1)}, f32[2,16,1]{1,2,0:T(1,128)}, u32[]{:S(2)}) copy-start(f32[2,16,1]{1,2,0:T(1,128)} %param.10) | copy-start | bytes 388
  34.4 5.3 %collective-permute-start.11 = (bf16[24,2048]{1,0:T(8,128)(2,1)S(1)}, bf16[24,2048]{1,0:T(8,128)(2,1)S(1)}, u32[]{:S(2)}, u32[]{:S(2)}) collective-permute-start(bf16[24,2048]{1,0:T(8,128)(2,1)S(1)} %get-tuple-element.36), channel_id=1, source_target_pairs={{0,2},{1,3},{2,0},{3,1},{4,6},{5,7},{6,4},{7,5},{8,10},{9,11},{10,... | collective-permute-start | bytes 294920 | tf_op jit(solution)/shard_map/ppermute | solution.py:365
  35.8 4.6 %collective-permute-start.12 = (bf16[24,2048]{1,0:T(8,128)(2,1)S(1)}, bf16[24,2048]{1,0:T(8,128)(2,1)S(1)}, u32[]{:S(2)}, u32[]{:S(2)}) collective-permute-start(bf16[24,2048]{1,0:T(8,128)(2,1)S(1)} %get-tuple-element.37), channel_id=1, source_target_pairs={{0,4},{1,5},{2,6},{3,7},{4,0},{5,1},{6,2},{7,3},{8,12},{9,13},{10,... | collective-permute-start | bytes 294920 | tf_op jit(solution)/shard_map/ppermute | solution.py:365
  36.9 5.5 %collective-permute-start.13 = (bf16[24,2048]{1,0:T(8,128)(2,1)S(1)}, bf16[24,2048]{1,0:T(8,128)(2,1)S(1)}, u32[]{:S(2)}, u32[]{:S(2)}) collective-permute-start(bf16[24,2048]{1,0:T(8,128)(2,1)S(1)} %get-tuple-element.38), channel_id=1, source_target_pairs={{0,6},{1,7},{2,4},{3,5},{4,2},{5,3},{6,0},{7,1},{8,14},{9,15},{10,... | collective-permute-start | bytes 294920 | tf_op jit(solution)/shard_map/ppermute | solution.py:365
  42.7 10.8 %collective-permute-start.14 = (bf16[32,2048]{1,0:T(8,128)(2,1)S(1)}, bf16[32,2048]{1,0:T(8,128)(2,1)S(1)}, u32[]{:S(2)}, u32[]{:S(2)}) collective-permute-start(bf16[32,2048]{1,0:T(8,128)(2,1)S(1)} %shard_map.107), channel_id=1, source_target_pairs={{0,8},{1,9},{2,10},{3,11},{4,12},{5,13},{6,14},{7,15},{8,0},{9,1},... | collective-permute-start | bytes 393224 | tf_op jit(solution)/shard_map/ppermute | solution.py:365
  45.4 5.2 %collective-permute-start.16 = (bf16[24,2048]{1,0:T(8,128)(2,1)S(1)}, bf16[24,2048]{1,0:T(8,128)(2,1)S(1)}, u32[]{:S(2)}, u32[]{:S(2)}) collective-permute-start(bf16[24,2048]{1,0:T(8,128)(2,1)S(1)} %get-tuple-element.41), channel_id=1, source_target_pairs={{0,2},{1,3},{2,0},{3,1},{4,6},{5,7},{6,4},{7,5},{8,10},{9,11},{10,... | collective-permute-start | bytes 294920 | tf_op jit(solution)/shard_map/ppermute | solution.py:365
  48.0 4.6 %collective-permute-start.17 = (bf16[24,2048]{1,0:T(8,128)(2,1)S(1)}, bf16[24,2048]{1,0:T(8,128)(2,1)S(1)}, u32[]{:S(2)}, u32[]{:S(2)}) collective-permute-start(bf16[24,2048]{1,0:T(8,128)(2,1)S(1)} %get-tuple-element.42), channel_id=1, source_target_pairs={{0,4},{1,5},{2,6},{3,7},{4,0},{5,1},{6,2},{7,3},{8,12},{9,13},{10,... | collective-permute-start | bytes 294920 | tf_op jit(solution)/shard_map/ppermute | solution.py:365
  48.0 5.5 %collective-permute-start.18 = (bf16[24,2048]{1,0:T(8,128)(2,1)S(1)}, bf16[24,2048]{1,0:T(8,128)(2,1)S(1)}, u32[]{:S(2)}, u32[]{:S(2)}) collective-permute-start(bf16[24,2048]{1,0:T(8,128)(2,1)S(1)} %get-tuple-element.43), channel_id=1, source_target_pairs={{0,6},{1,7},{2,4},{3,5},{4,2},{5,3},{6,0},{7,1},{8,14},{9,15},{10,... | collective-permute-start | bytes 294920 | tf_op jit(solution)/shard_map/ppermute | solution.py:365
  49.4 1.2 %collective-permute-start.15 = (s32[8,128]{1,0:T(8,128)S(1)}, s32[8,128]{1,0:T(8,128)S(1)}, u32[]{:S(2)}, u32[]{:S(2)}) collective-permute-start(s32[8,128]{1,0:T(8,128)S(1)} %get-tuple-element.39.load_ref), channel_id=1, source_target_pairs={{0,1},{1,0},{2,3},{3,2},{4,5},{5,4},{6,7},{7,6},{8,9},{9,8},{10,11... | collective-permute-start | bytes 12296 | tf_op jit(solution)/shard_map/ppermute | solution.py:365

commit v2 on v1

--- a/solution.py
+++ b/solution.py
@@ -136,22 +136,25 @@
         blocks[q][:, :LANES] = (part[:, :LANES] + meta).astype(jnp.bfloat16)
 
 
-def pick_own_kernel(cap, home_hbm, new_hbm, x_hbm, picks_ref, *refs):
-    blocks, sel_ref, table_ref = refs[:SQUARE], refs[SQUARE], refs[SQUARE + 1]
-    home_ref, new_ref, x_ref, sem = refs[SQUARE + 2 :]
+def pick_own_kernel(cap, home_hbm, new_hbm, x_hbm, ids_hbm, reps_hbm, *refs):
+    blocks, (sel_ref, table_ref, picks_ref, zero_ref) = refs[:SQUARE], refs[SQUARE : SQUARE + 4]
+    home_ref, new_ref, x_ref, ids_ref, reps_ref, sem = refs[SQUARE + 4 :]
+    sources = (home_hbm, new_hbm, ids_hbm, reps_hbm, x_hbm)
+    targets = (home_ref, new_ref, ids_ref, reps_ref, x_ref)
     copies = [
         pltpu.make_async_copy(source, target, sem.at[index])
-        for index, (source, target) in enumerate(
-            ((home_hbm, home_ref), (new_hbm, new_ref), (x_hbm, x_ref))
-        )
+        for index, (source, target) in enumerate(zip(sources, targets))
     ]
     for copy in copies:
         copy.start()
+    zero_ref[...] = jnp.zeros(zero_ref.shape, zero_ref.dtype)
     chip = lax.axis_index("expert") // 2
     slots = new_ref.shape[0]
     experts = home_ref.shape[0]
-    copies[0].wait()
-    copies[1].wait()
+    for copy in copies[:-1]:
+        copy.wait()
+    picks = jnp.concatenate([ids_ref[...], reps_ref[...]], axis=0)
+    picks_ref[...] = picks
     row = lax.broadcasted_iota(jnp.int32, table_ref.shape, 0)
     lane = lax.broadcasted_iota(jnp.int32, table_ref.shape, 1)
     table = jnp.zeros(table_ref.shape, jnp.int32)
@@ -168,10 +171,10 @@
     table_ref[...] = table
 
     def rows():
-        copies[2].wait()
+        copies[-1].wait()
         return x_ref[...]
 
-    pick(cap, table, picks_ref[...], rows, blocks, sel_ref, experts)
+    pick(cap, table, picks, rows, blocks, sel_ref, experts)
 
 
 def pick_far_kernel(cap, experts, table_ref, x_ref, picks_ref, *refs):
@@ -179,8 +182,7 @@
     pick(cap, table_ref[...], picks_ref[...], lambda: x_ref[...], blocks, sel_ref, experts)
 
 
-def pick_shapes(cap, x, picks):
-    batches = picks.shape[0] // 2
+def pick_shapes(cap, x, batches):
     high = block_rows(batches, cap)
     count, width = x.shape
     block = jax.ShapeDtypeStruct((high, width), jnp.bfloat16)
@@ -193,26 +195,34 @@
     return [block] * SQUARE + [sel], cost
 
 
-def pick_own(cap, home, new, x, picks):
-    shapes, cost = pick_shapes(cap, x, picks)
+def pick_own(cap, home, new, x, ids, reps):
+    batches, tokens = ids.shape
+    shapes, cost = pick_shapes(cap, x, batches)
+    shapes += [
+        jax.ShapeDtypeStruct((8, LANES), jnp.int32),
+        jax.ShapeDtypeStruct((2 * batches, tokens), jnp.int32),
+        jax.ShapeDtypeStruct((8, LANES), jnp.float32),
+    ]
     return pl.pallas_call(
         functools.partial(pick_own_kernel, cap),
-        out_shape=shapes + [jax.ShapeDtypeStruct((8, LANES), jnp.int32)],
-        in_specs=[pl.BlockSpec(memory_space=HBM)] * 3 + [pl.BlockSpec(memory_space=VMEM)],
-        out_specs=[pl.BlockSpec(memory_space=VMEM)] * (SQUARE + 2),
+        out_shape=shapes,
+        in_specs=[pl.BlockSpec(memory_space=HBM)] * 5,
+        out_specs=[pl.BlockSpec(memory_space=VMEM)] * len(shapes),
         scratch_shapes=[
             SMEM(home.shape, jnp.int32),
             SMEM(new.shape, jnp.int32),
             VMEM(x.shape, x.dtype),
-            pltpu.SemaphoreType.DMA((3,)),
+            VMEM(ids.shape, ids.dtype),
+            VMEM(reps.shape, reps.dtype),
+            pltpu.SemaphoreType.DMA((5,)),
         ],
         cost_estimate=cost,
         compiler_params=pltpu.CompilerParams(vmem_limit_bytes=SMALL),
-    )(*(pltpu.with_memory_space_constraint(value, HBM) for value in (home, new, x)), picks)
+    )(*(pltpu.with_memory_space_constraint(value, HBM) for value in (home, new, x, ids, reps)))
 
 
 def pick_far(cap, experts, table, x, picks):
-    shapes, cost = pick_shapes(cap, x, picks)
+    shapes, cost = pick_shapes(cap, x, picks.shape[0] // 2)
     return pl.pallas_call(
         functools.partial(pick_far_kernel, cap, experts),
         out_shape=shapes,
@@ -223,64 +233,74 @@
     )(table, x, picks)
 
 
-def expert_kernel(meta, count, *refs):
-    blocks, refs = refs[:count], refs[count:]
-    panels_hbm, panels_far, refs = refs[:3], refs[3:6], refs[6:]
-    outs, load_ref, panels, sem = refs[:count], refs[count], refs[count + 1 : count + 4], refs[count + 4]
+def fetch_kernel(*refs):
+    count = len(refs) // 2
+    sources, targets, sem = refs[:count], refs[count : 2 * count], refs[2 * count]
     copies = [
         pltpu.make_async_copy(source, target, sem.at[index])
-        for index, (source, target) in enumerate(zip(panels_hbm, panels))
+        for index, (source, target) in enumerate(zip(sources, targets))
     ]
     for copy in copies:
         copy.start()
+    for copy in copies:
+        copy.wait()
+
+
+def fetched(values):
+    count = len(values)
+    return pl.pallas_call(
+        fetch_kernel,
+        out_shape=[jax.ShapeDtypeStruct(value.shape, value.dtype) for value in values],
+        in_specs=[pl.BlockSpec(memory_space=HBM)] * count,
+        out_specs=[pl.BlockSpec(memory_space=VMEM)] * count,
+        scratch_shapes=[pltpu.SemaphoreType.DMA((count,))],
+        cost_estimate=pl.CostEstimate(
+            flops=0, bytes_accessed=4 * sum(value.size for value in values), transcendentals=0
+        ),
+        compiler_params=pltpu.CompilerParams(vmem_limit_bytes=LARGE),
+    )(*(pltpu.with_memory_space_constraint(value, HBM) for value in values))
+
+
+def expert_kernel(meta, *refs):
+    blocks, panels, prior_ref = refs[:SQUARE], refs[SQUARE : SQUARE + 6], refs[SQUARE + 6]
+    outs, load_ref = refs[SQUARE + 7 : 2 * SQUARE + 7], refs[2 * SQUARE + 7]
     high = blocks[0].shape[0]
     x = jnp.concatenate([block[...] for block in blocks], axis=0)
     contract = (((1,), (1,)), ((), ()))
     start = meta - meta % 8
-    load = jnp.zeros(load_ref.shape, jnp.float32)
+    load = prior_ref[...]
     for block in blocks:
         load = load + block[start : start + 8, :LANES].astype(jnp.float32)
-    load_ref[...] = load.astype(jnp.int32)
-
-    def half(gate_ref, up_ref, down_ref, ready):
-        ready(0)
-        ready(1)
+    load_ref[...] = load
+    total = None
+    for gate_ref, up_ref, down_ref in (panels[:3], panels[3:]):
         gate = jnp.dot(x, gate_ref[0], preferred_element_type=jnp.float32)
         up = jnp.dot(x, up_ref[0], preferred_element_type=jnp.float32)
         hidden = (gate / (1.0 + jnp.exp(-gate)) * up).astype(jnp.bfloat16)
-        ready(2)
-        return lax.dot_general(hidden, down_ref[0], contract, preferred_element_type=jnp.float32)
-
-    total = half(*panels_far, lambda index: None)
-    total = total + half(*panels, lambda index: copies[index].wait())
+        part = lax.dot_general(hidden, down_ref[0], contract, preferred_element_type=jnp.float32)
+        total = part if total is None else total + part
     total = total.astype(jnp.bfloat16)
-    for q in range(count):
+    for q in range(SQUARE):
         outs[q][...] = total[q * high : (q + 1) * high]
 
 
-def run_expert(meta, blocks, panels, panels_far):
+def run_expert(meta, blocks, panels, panels_far, prior):
     high, width = blocks[0].shape
     half = panels[0].shape[2]
-    count = len(blocks)
-    rows = count * high
-    held = [pltpu.with_memory_space_constraint(panel, HBM) for panel in panels]
+    rows = SQUARE * high
     return pl.pallas_call(
-        functools.partial(expert_kernel, meta, count),
-        out_shape=[jax.ShapeDtypeStruct((high, width), jnp.bfloat16)] * count
-        + [jax.ShapeDtypeStruct((8, LANES), jnp.int32)],
-        in_specs=[pl.BlockSpec(memory_space=VMEM)] * count
-        + [pl.BlockSpec(memory_space=HBM)] * 3
-        + [pl.BlockSpec(memory_space=VMEM)] * 3,
-        out_specs=[pl.BlockSpec(memory_space=VMEM)] * (count + 1),
-        scratch_shapes=[VMEM(panel.shape, panel.dtype) for panel in panels]
-        + [pltpu.SemaphoreType.DMA((3,))],
+        functools.partial(expert_kernel, meta),
+        out_shape=[jax.ShapeDtypeStruct((high, width), jnp.bfloat16)] * SQUARE
+        + [jax.ShapeDtypeStruct(prior.shape, prior.dtype)],
+        in_specs=[pl.BlockSpec(memory_space=VMEM)] * (SQUARE + 7),
+        out_specs=[pl.BlockSpec(memory_space=VMEM)] * (SQUARE + 1),
         cost_estimate=pl.CostEstimate(
             flops=2 * rows * width * half * 6,
             bytes_accessed=6 * 2 * width * half + 4 * rows * width,
             transcendentals=2 * rows * half,
         ),
         compiler_params=pltpu.CompilerParams(vmem_limit_bytes=LARGE),
-    )(*blocks, *held, *panels_far)
+    )(*blocks, *panels, *panels_far, prior)
 
 
 def chosen(sel_ref, blocks):
@@ -300,7 +320,9 @@
     both = load_ref[...] + load_far_ref[...]
     row = lax.broadcasted_iota(jnp.int32, both.shape, 0)
     lane = lax.broadcasted_iota(jnp.int32, both.shape, 1)
-    slot_ref[0] = jnp.sum(jnp.where((row == meta % 8) & (lane == core), both, 0))
+    slot_ref[0] = jnp.sum(jnp.where((row == meta % 8) & (lane == core), both, 0.0)).astype(
+        jnp.int32
+    )
     batches, tokens = weight_ref.shape
     total = chosen(sel_ref, refs[:SQUARE]) + back_ref[...].astype(jnp.float32)
     lane = lax.broadcasted_iota(jnp.int32, (tokens, tokens), 0)
@@ -369,18 +391,23 @@
 
     x = activations.reshape(rows, width)
     x_far = swap(x, distant)
-    picks = jnp.concatenate(
-        [expert_ids.reshape(batches, tokens), replica.reshape(batches, tokens)], axis=0
-    )
-    picks_far = swap(picks, distant)
     panels = (gate_panel, up_panel, down_panel)
     panels_far = [swap(panel, 1) for panel in panels]
-    *blocks, sel, table = pick_own(cap, old_home, new_expert, x, picks)
+    *blocks, sel, table, picks, zero = pick_own(
+        cap,
+        old_home,
+        new_expert,
+        x,
+        expert_ids.reshape(batches, tokens),
+        replica.reshape(batches, tokens),
+    )
+    picks_far = swap(picks, distant)
     blocks = around(blocks)
     *blocks_far, sel_far = pick_far(cap, old_home.shape[0], table, x_far, picks_far)
     blocks_far = around(blocks_far)
-    *results, load = run_expert(meta, blocks + blocks_far, panels, panels_far)
-    results, results_far = results[:SQUARE], results[SQUARE:]
+    panels = fetched(panels)
+    *results, load = run_expert(meta, blocks, panels, panels_far, zero)
+    *results_far, load = run_expert(meta, blocks_far, panels, panels_far, load)
     results_far = around(results_far)
     results = around(results)
     load_far = swap(load, 1)

time: 54.6 us -> 54 us (0.989)
  waiting for transfers between devices: 22.1 us -> 18.8 us
  Pallas kernels: 8.04 us -> 9.94 us
  starting transfers between devices: 22.8 us -> 24.3 us
  other arithmetic: 0.7 us -> 0 us
    ppermute x19, waiting for transfers between devices: 22.1 us -> 18.8 us  [swap(): return lax.ppermute(value, 'expert', swapped(size, bits))]
    pallas_call x2 -> x4, Pallas kernels: 6.37 us -> 8.28 us  [the longest x2 4.43 us: run_expert(): pl.pallas_call(functools.partial(expert_kernel, meta), out_shape=[jax.Sha...]
    ppermute x19, starting transfers between devices: 22.8 us -> 24.3 us  [swap(): return lax.ppermute(value, 'expert', swapped(size, bits))]
    concatenate x1 -> x0, other arithmetic: 0.7 us -> none  [dispatched(): jnp.concatenate([expert_ids.reshape(batches, tokens), replica.reshape(bat...]
  transfers between devices with their start and end apart: 19 -> 19, of which waited for: 11 -> 10; matrix products, arithmetic and copies ran while one was open for 1% -> 0% of each run, Pallas kernels for 4% -> 12%
where the time goes in v2:
time: 54 us; the launch traced here: 53.8 us
  starting transfers between devices  24.3 us (45%)
  waiting for transfers between devices  18.8 us (35%)
  Pallas kernels  9.94 us (18%)
  between operations  0.73 us (1%)
    ppermute x19, starting transfers between devices, swap(): return lax.ppermute(value, 'expert', swapped(size, bits))  24.3 us
    ppermute x19, waiting for transfers between devices, swap(): return lax.ppermute(value, 'expert', swapped(size, bits))  18.8 us
    pallas_call x2, Pallas kernels, run_expert(): pl.pallas_call(functools.partial(expert_kernel, meta), out_shape=[jax.Sha...  4.43 us
    pallas_call x1, Pallas kernels, fetched(): pl.pallas_call(fetch_kernel, out_shape=[jax.ShapeDtypeStruct(value.shape,...  2.38 us
    pallas_call x1, Pallas kernels, pick_own(): pl.pallas_call(functools.partial(pick_own_kernel, cap), out_shape=shapes,...  1.47 us
    pallas_call x2, Pallas kernels, merge_rows(): pl.pallas_call(kernel, out_shape=shapes, in_specs=[pl.BlockSpec(memory_sp...  1.14 us
  transfers between devices with their start and end apart: 19, of which 10 were waited for; matrix products, arithmetic and copies ran while one was open for 0% of the time, Pallas kernels for 12%

profile of v2, /device:TPU:0, one launch (start us, length us, event | category | flops | bytes accessed | tf_op | source)
XLA Modules:
  0.0 53.8 jit_solution(11984477306074867526)
XLA Ops:
  0.6 0.6 %collective-permute-start.5 = (bf16[1,2048,384]{2,1,0:T(8,128)(2,1)}, bf16[1,2048,384]{2,1,0:T(8,128)(2,1)S(1)}, u32[]{:S(2)}, u32[]{:S(2)}) collective-permute-start(bf16[1,2048,384]{2,1,0:T(8,128)(2,1)} %refs_0_.1), channel_id=1, source_target_pairs={{0,1},{1,0},{2,3},{3,2},{4,5},{5,4},{6,7},{7,6},{8,9},{9,8},{10,11... | collective-permute-start | bytes 4718600 | tf_op jit(solution)/shard_map/ppermute | solution.py:387
  1.3 0.4 collective-permute-start.7
  1.7 3.7 %collective-permute-start = (bf16[32,2048]{1,0:T(8,128)(2,1)}, bf16[32,2048]{1,0:T(8,128)(2,1)S(1)}, u32[]{:S(2)}, u32[]{:S(2)}) collective-permute-start(bf16[32,2048]{1,0:T(8,128)(2,1)} %bitcast.6), channel_id=1, source_target_pairs={{0,8},{1,9},{2,10},{3,11},{4,12},{5,13},{6,14},{7,15},{8,0},{9,1},... | collective-permute-start | bytes 393224 | tf_op jit(solution)/shard_map/ppermute | solution.py:387
  5.4 1.5 %shard_map.104 = (bf16[24,2048]{1,0:T(8,128)(2,1)S(1)}, bf16[24,2048]{1,0:T(8,128)(2,1)S(1)}, bf16[24,2048]{1,0:T(8,128)(2,1)S(1)}, bf16[24,2048]{1,0:T(8,128)(2...) custom-call(s32[8]{0:T(128)} %home_hbm.1, ...), custom_call_target="tpu_custom_call" | custom-call | flops 12582912 | bytes 786432 | tf_op jit(solution)/shard_map/pallas_call | solution.py:206
  6.9 5.6 %collective-permute-done.1.picks_ref = s32[4,16]{1,0:T(4,128)S(1)} collective-permute-done((s32[4,16]{1,0:T(4,128)S(1)}, s32[4,16]{1,0:T(4,128)S(1)}, u32[]{:S(2)}, u32[]{:S(2)}) %collective-permute-start.1) | collective-permute-done | bytes 288 | tf_op jit(solution)/shard_map/ppermute | solution.py:387
  12.5 1.5 %collective-permute-start.8 = (bf16[24,2048]{1,0:T(8,128)(2,1)S(1)}, bf16[24,2048]{1,0:T(8,128)(2,1)S(1)}, u32[]{:S(2)}, u32[]{:S(2)}) collective-permute-start(bf16[24,2048]{1,0:T(8,128)(2,1)S(1)} %get-tuple-element.42), channel_id=1, source_target_pairs={{0,2},{1,3},{2,0},{3,1},{4,6},{5,7},{6,4},{7,5},{8,10},{9,11},{10,... | collective-permute-start | bytes 294920 | tf_op jit(solution)/shard_map/ppermute | solution.py:387
  14.1 3.1 %collective-permute-done.8.refs_1_ = bf16[24,2048]{1,0:T(8,128)(2,1)S(1)} collective-permute-done((bf16[24,2048]{1,0:T(8,128)(2,1)S(1)}, bf16[24,2048]{1,0:T(8,128)(2,1)S(1)}, u32[]{:S(2)}, u32[]{:S(2)}) %collective-permute-start.8) | collective-permute-done | bytes 98336 | tf_op jit(solution)/shard_map/ppermute | solution.py:387
  17.2 0.9 %collective-permute-start.9 = (bf16[24,2048]{1,0:T(8,128)(2,1)S(1)}, bf16[24,2048]{1,0:T(8,128)(2,1)S(1)}, u32[]{:S(2)}, u32[]{:S(2)}) collective-permute-start(bf16[24,2048]{1,0:T(8,128)(2,1)S(1)} %get-tuple-element.43), channel_id=1, source_target_pairs={{0,4},{1,5},{2,6},{3,7},{4,0},{5,1},{6,2},{7,3},{8,12},{9,13},{10,... | collective-permute-start | bytes 294920 | tf_op jit(solution)/shard_map/ppermute | solution.py:387
  18.1 2.1 %collective-permute-start.10 = (bf16[24,2048]{1,0:T(8,128)(2,1)S(1)}, bf16[24,2048]{1,0:T(8,128)(2,1)S(1)}, u32[]{:S(2)}, u32[]{:S(2)}) collective-permute-start(bf16[24,2048]{1,0:T(8,128)(2,1)S(1)} %get-tuple-element.44), channel_id=1, source_target_pairs={{0,6},{1,7},{2,4},{3,5},{4,2},{5,3},{6,0},{7,1},{8,14},{9,15},{10,... | collective-permute-start | bytes 294920 | tf_op jit(solution)/shard_map/ppermute | solution.py:387
  20.2 0.5 shard_map.105
  20.7 1.9 %collective-permute-done.9.refs_2_ = bf16[24,2048]{1,0:T(8,128)(2,1)S(1)} collective-permute-done((bf16[24,2048]{1,0:T(8,128)(2,1)S(1)}, bf16[24,2048]{1,0:T(8,128)(2,1)S(1)}, u32[]{:S(2)}, u32[]{:S(2)}) %collective-permute-start.9) | collective-permute-done | bytes 98336 | tf_op jit(solution)/shard_map/ppermute | solution.py:387
  22.6 0.7 %collective-permute-start.2 = (bf16[24,2048]{1,0:T(8,128)(2,1)S(1)}, bf16[24,2048]{1,0:T(8,128)(2,1)S(1)}, u32[]{:S(2)}, u32[]{:S(2)}) collective-permute-start(bf16[24,2048]{1,0:T(8,128)(2,1)S(1)} %get-tuple-element.35), channel_id=1, source_target_pairs={{0,2},{1,3},{2,0},{3,1},{4,6},{5,7},{6,4},{7,5},{8,10},{9,11},{10,... | collective-permute-start | bytes 294920 | tf_op jit(solution)/shard_map/ppermute | solution.py:387
  23.3 0.6 %collective-permute-done.10.refs_3_ = bf16[24,2048]{1,0:T(8,128)(2,1)S(1)} collective-permute-done((bf16[24,2048]{1,0:T(8,128)(2,1)S(1)}, bf16[24,2048]{1,0:T(8,128)(2,1)S(1)}, u32[]{:S(2)}, u32[]{:S(2)}) %collective-permute-start.10) | collective-permute-done | bytes 98336 | tf_op jit(solution)/shard_map/ppermute | solution.py:387
  23.9 1.2 %collective-permute-start.3 = (bf16[24,2048]{1,0:T(8,128)(2,1)S(1)}, bf16[24,2048]{1,0:T(8,128)(2,1)S(1)}, u32[]{:S(2)}, u32[]{:S(2)}) collective-permute-start(bf16[24,2048]{1,0:T(8,128)(2,1)S(1)} %get-tuple-element.36), channel_id=1, source_target_pairs={{0,4},{1,5},{2,6},{3,7},{4,0},{5,1},{6,2},{7,3},{8,12},{9,13},{10,... | collective-permute-start | bytes 294920 | tf_op jit(solution)/shard_map/ppermute | solution.py:387
  25.1 1.6 %collective-permute-start.4 = (bf16[24,2048]{1,0:T(8,128)(2,1)S(1)}, bf16[24,2048]{1,0:T(8,128)(2,1)S(1)}, u32[]{:S(2)}, u32[]{:S(2)}) collective-permute-start(bf16[24,2048]{1,0:T(8,128)(2,1)S(1)} %get-tuple-element.37), channel_id=1, source_target_pairs={{0,6},{1,7},{2,4},{3,5},{4,2},{5,3},{6,0},{7,1},{8,14},{9,15},{10,... | collective-permute-start | bytes 294920 | tf_op jit(solution)/shard_map/ppermute | solution.py:387
  26.7 2.4 %shard_map.106 = (bf16[1,2048,384]{2,1,0:T(8,128)(2,1)S(1)}, bf16[1,2048,384]{2,1,0:T(8,128)(2,1)S(1)}, bf16[1,2048,384]{2,1,0:T(8,128)(2,1)S(1)}) custom-call(bf16[1,2048,384]{2,1,0:T(8,128)(2,1)} %refs_0_.1, bf16[1,2048,384]{2,1,0:T(8,128)(2,1)} %refs_1_.1, bf16[1,2048,384]{2,1,0:T(8,128)(2,1)} %refs_2_.1), custom_call_target="tpu_custom_call" | custom-call | bytes 9437184 | tf_op jit(solution)/shard_map/pallas_call | solution.py:251
  29.1 2.2 %shard_map.107 = (bf16[24,2048]{1,0:T(8,128)(2,1)S(1)}, bf16[24,2048]{1,0:T(8,128)(2,1)S(1)}, bf16[24,2048]{1,0:T(8,128)(2,1)S(1)}, bf16[24,2048]{1,0:T(8,128)(2,1)S(1)}, f32[8,128]{1,0:T(8,128)S(1)}) custom-call(bf16[24,2048]{1,0:T(8,128)(2,1)S(1)} %get-tuple-element.41.refs_0_, bf16[24,2048]{1,0:T(8,128)(2,1)S(1)} %collective-permute-done.8.refs_1_, ...), custom_call_target="tpu_custom_call" | custom-call | flops 905969664 | bytes 10223616 | tf_op jit(solution)/shard_map/pallas_call | solution.py:291
  31.4 2.2 %shard_map.108 = (bf16[24,2048]{1,0:T(8,128)(2,1)S(1)}, bf16[24,2048]{1,0:T(8,128)(2,1)S(1)}, bf16[24,2048]{1,0:T(8,128)(2,1)S(1)}, bf16[24,2048]{1,0:T(8,128)(2,1)S(1)}, f32[8,128]{1,0:T(8,128)S(1)}) custom-call(bf16[24,2048]{1,0:T(8,128)(2,1)S(1)} %get-tuple-element.34.refs_0_, bf16[24,2048]{1,0:T(8,128)(2,1)S(1)} %collective-permute-done.2.refs_1_, ...), custom_call_target="tpu_custom_call" | custom-call | flops 905969664 | bytes 10223616 | tf_op jit(solution)/shard_map/pallas_call | solution.py:291
  33.6 0.8 %collective-permute-start.11 = (bf16[24,2048]{1,0:T(8,128)(2,1)S(1)}, bf16[24,2048]{1,0:T(8,128)(2,1)S(1)}, u32[]{:S(2)}, u32[]{:S(2)}) collective-permute-start(bf16[24,2048]{1,0:T(8,128)(2,1)S(1)} %get-tuple-element.48), channel_id=1, source_target_pairs={{0,2},{1,3},{2,0},{3,1},{4,6},{5,7},{6,4},{7,5},{8,10},{9,11},{10,... | collective-permute-start | bytes 294920 | tf_op jit(solution)/shard_map/ppermute | solution.py:387
  34.4 1.2 %collective-permute-start.12 = (bf16[24,2048]{1,0:T(8,128)(2,1)S(1)}, bf16[24,2048]{1,0:T(8,128)(2,1)S(1)}, u32[]{:S(2)}, u32[]{:S(2)}) collective-permute-start(bf16[24,2048]{1,0:T(8,128)(2,1)S(1)} %get-tuple-element.49), channel_id=1, source_target_pairs={{0,4},{1,5},{2,6},{3,7},{4,0},{5,1},{6,2},{7,3},{8,12},{9,13},{10,... | collective-permute-start | bytes 294920 | tf_op jit(solution)/shard_map/ppermute | solution.py:387
  35.6 1.6 %collective-permute-start.13 = (bf16[24,2048]{1,0:T(8,128)(2,1)S(1)}, bf16[24,2048]{1,0:T(8,128)(2,1)S(1)}, u32[]{:S(2)}, u32[]{:S(2)}) collective-permute-start(bf16[24,2048]{1,0:T(8,128)(2,1)S(1)} %get-tuple-element.50), channel_id=1, source_target_pairs={{0,6},{1,7},{2,4},{3,5},{4,2},{5,3},{6,0},{7,1},{8,14},{9,15},{10,... | collective-permute-start | bytes 294920 | tf_op jit(solution)/shard_map/ppermute | solution.py:387
  37.2 1.4 %collective-permute-done.11.refs_1_ = bf16[24,2048]{1,0:T(8,128)(2,1)S(1)} collective-permute-done((bf16[24,2048]{1,0:T(8,128)(2,1)S(1)}, bf16[24,2048]{1,0:T(8,128)(2,1)S(1)}, u32[]{:S(2)}, u32[]{:S(2)}) %collective-permute-start.11) | collective-permute-done | bytes 98336 | tf_op jit(solution)/shard_map/ppermute | solution.py:387
  38.5 0.5 collective-permute-done.12.refs_2_
  39.0 2.1 %collective-permute-done.13.refs_3_ = bf16[24,2048]{1,0:T(8,128)(2,1)S(1)} collective-permute-done((bf16[24,2048]{1,0:T(8,128)(2,1)S(1)}, bf16[24,2048]{1,0:T(8,128)(2,1)S(1)}, u32[]{:S(2)}, u32[]{:S(2)}) %collective-permute-start.13) | collective-permute-done | bytes 98336 | tf_op jit(solution)/shard_map/ppermute | solution.py:387
  41.3 4.5 %collective-permute-start.14 = (bf16[32,2048]{1,0:T(8,128)(2,1)S(1)}, bf16[32,2048]{1,0:T(8,128)(2,1)S(1)}, u32[]{:S(2)}, u32[]{:S(2)}) collective-permute-start(bf16[32,2048]{1,0:T(8,128)(2,1)S(1)} %shard_map.109), channel_id=1, source_target_pairs={{0,8},{1,9},{2,10},{3,11},{4,12},{5,13},{6,14},{7,15},{8,0},{9,1},... | collective-permute-start | bytes 393224 | tf_op jit(solution)/shard_map/ppermute | solution.py:387
  45.8 0.3 collective-permute-start.16
  46.0 1.1 %collective-permute-start.17 = (bf16[24,2048]{1,0:T(8,128)(2,1)S(1)}, bf16[24,2048]{1,0:T(8,128)(2,1)S(1)}, u32[]{:S(2)}, u32[]{:S(2)}) collective-permute-start(bf16[24,2048]{1,0:T(8,128)(2,1)S(1)} %get-tuple-element.54), channel_id=1, source_target_pairs={{0,4},{1,5},{2,6},{3,7},{4,0},{5,1},{6,2},{7,3},{8,12},{9,13},{10,... | collective-permute-start | bytes 294920 | tf_op jit(solution)/shard_map/ppermute | solution.py:387
  47.1 2.1 %collective-permute-start.18 = (bf16[24,2048]{1,0:T(8,128)(2,1)S(1)}, bf16[24,2048]{1,0:T(8,128)(2,1)S(1)}, u32[]{:S(2)}, u32[]{:S(2)}) collective-permute-start(bf16[24,2048]{1,0:T(8,128)(2,1)S(1)} %get-tuple-element.55), channel_id=1, source_target_pairs={{0,6},{1,7},{2,4},{3,5},{4,2},{5,3},{6,0},{7,1},{8,14},{9,15},{10,... | collective-permute-start | bytes 294920 | tf_op jit(solution)/shard_map/ppermute | solution.py:387
  49.3 1.2 %collective-permute-done.15.load_far_ref = f32[8,128]{1,0:T(8,128)S(1)} collective-permute-done((f32[8,128]{1,0:T(8,128)S(1)}, f32[8,128]{1,0:T(8,128)S(1)}, u32[]{:S(2)}, u32[]{:S(2)}) %collective-permute-start.15) | collective-permute-done | bytes 4128 | tf_op jit(solution)/shard_map/ppermute | solution.py:387
  50.4 0.2 collective-permute-done.17.refs_2_
  50.7 2.2 %collective-permute-done.18.refs_3_ = bf16[24,2048]{1,0:T(8,128)(2,1)S(1)} collective-permute-done((bf16[24,2048]{1,0:T(8,128)(2,1)S(1)}, bf16[24,2048]{1,0:T(8,128)(2,1)S(1)}, u32[]{:S(2)}, u32[]{:S(2)}) %collective-permute-start.18) | collective-permute-done | bytes 98336 | tf_op jit(solution)/shard_map/ppermute | solution.py:387
  52.9 0.9 %shard_map.110 = (bf16[32,2048]{1,0:T(8,128)(2,1)}, s32[1]{0:T(128)}) custom-call(bf16[96,32]{1,0:T(8,128)(2,1)S(1)} %get-tuple-element.30.sel_ref, f32[2,16]{1,0:T(2,128)S(1)} %bitcast.5, bf16[32,2048]{1,0:T(8,128)(2,1)S(1)} %collective-permute-done.14.back_ref, f32[8,128]{1,0:T(8,128)S(1)} %get-tuple-element.51.load_ref, ...), custom_call_target="tpu_custom_call" | custom-call | flops 12582912 | bytes 524288 | tf_op jit(solution)/shard_map/pallas_call | solution.py:350
  (15 shorter events, 0.4 us)
Async XLA Ops:
  0.6 24.5 %collective-permute-start.5 = (bf16[1,2048,384]{2,1,0:T(8,128)(2,1)}, bf16[1,2048,384]{2,1,0:T(8,128)(2,1)S(1)}, u32[]{:S(2)}, u32[]{:S(2)}) collective-permute-start(bf16[1,2048,384]{2,1,0:T(8,128)(2,1)} %refs_0_.1), channel_id=1, source_target_pairs={{0,1},{1,0},{2,3},{3,2},{4,5},{5,4},{6,7},{7,6},{8,9},{9,8},{10,11... | collective-permute-start | bytes 4718600 | tf_op jit(solution)/shard_map/ppermute | solution.py:387
  1.2 27.9 %collective-permute-start.6 = (bf16[1,2048,384]{2,1,0:T(8,128)(2,1)}, bf16[1,2048,384]{2,1,0:T(8,128)(2,1)S(1)}, u32[]{:S(2)}, u32[]{:S(2)}) collective-permute-start(bf16[1,2048,384]{2,1,0:T(8,128)(2,1)} %refs_1_.1), channel_id=1, source_target_pairs={{0,1},{1,0},{2,3},{3,2},{4,5},{5,4},{6,7},{7,6},{8,9},{9,8},{10,11... | collective-permute-start | bytes 4718600 | tf_op jit(solution)/shard_map/ppermute | solution.py:387
  1.3 27.9 %collective-permute-start.7 = (bf16[1,2048,384]{2,1,0:T(8,128)(2,1)}, bf16[1,2048,384]{2,1,0:T(8,128)(2,1)S(1)}, u32[]{:S(2)}, u32[]{:S(2)}) collective-permute-start(bf16[1,2048,384]{2,1,0:T(8,128)(2,1)} %refs_2_.1), channel_id=1, source_target_pairs={{0,1},{1,0},{2,3},{3,2},{4,5},{5,4},{6,7},{7,6},{8,9},{9,8},{10,11... | collective-permute-start | bytes 4718600 | tf_op jit(solution)/shard_map/ppermute | solution.py:387
  1.7 16.4 %collective-permute-start = (bf16[32,2048]{1,0:T(8,128)(2,1)}, bf16[32,2048]{1,0:T(8,128)(2,1)S(1)}, u32[]{:S(2)}, u32[]{:S(2)}) collective-permute-start(bf16[32,2048]{1,0:T(8,128)(2,1)} %bitcast.6), channel_id=1, source_target_pairs={{0,8},{1,9},{2,10},{3,11},{4,12},{5,13},{6,14},{7,15},{8,0},{9,1},... | collective-permute-start | bytes 393224 | tf_op jit(solution)/shard_map/ppermute | solution.py:387
  6.8 5.7 %collective-permute-start.1 = (s32[4,16]{1,0:T(4,128)S(1)}, s32[4,16]{1,0:T(4,128)S(1)}, u32[]{:S(2)}, u32[]{:S(2)}) collective-permute-start(s32[4,16]{1,0:T(4,128)S(1)} %get-tuple-element.32), channel_id=1, source_target_pairs={{0,8},{1,9},{2,10},{3,11},{4,12},{5,13},{6,14},{7,15},{8,0},{9,1},... | collective-permute-start | bytes 776 | tf_op jit(solution)/shard_map/ppermute | solution.py:387
  12.5 4.6 %collective-permute-start.8 = (bf16[24,2048]{1,0:T(8,128)(2,1)S(1)}, bf16[24,2048]{1,0:T(8,128)(2,1)S(1)}, u32[]{:S(2)}, u32[]{:S(2)}) collective-permute-start(bf16[24,2048]{1,0:T(8,128)(2,1)S(1)} %get-tuple-element.42), channel_id=1, source_target_pairs={{0,2},{1,3},{2,0},{3,1},{4,6},{5,7},{6,4},{7,5},{8,10},{9,11},{10,... | collective-permute-start | bytes 294920 | tf_op jit(solution)/shard_map/ppermute | solution.py:387
  17.2 5.5 %collective-permute-start.9 = (bf16[24,2048]{1,0:T(8,128)(2,1)S(1)}, bf16[24,2048]{1,0:T(8,128)(2,1)S(1)}, u32[]{:S(2)}, u32[]{:S(2)}) collective-permute-start(bf16[24,2048]{1,0:T(8,128)(2,1)S(1)} %get-tuple-element.43), channel_id=1, source_target_pairs={{0,4},{1,5},{2,6},{3,7},{4,0},{5,1},{6,2},{7,3},{8,12},{9,13},{10,... | collective-permute-start | bytes 294920 | tf_op jit(solution)/shard_map/ppermute | solution.py:387
  18.1 5.8 %collective-permute-start.10 = (bf16[24,2048]{1,0:T(8,128)(2,1)S(1)}, bf16[24,2048]{1,0:T(8,128)(2,1)S(1)}, u32[]{:S(2)}, u32[]{:S(2)}) collective-permute-start(bf16[24,2048]{1,0:T(8,128)(2,1)S(1)} %get-tuple-element.44), channel_id=1, source_target_pairs={{0,6},{1,7},{2,4},{3,5},{4,2},{5,3},{6,0},{7,1},{8,14},{9,15},{10,... | collective-permute-start | bytes 294920 | tf_op jit(solution)/shard_map/ppermute | solution.py:387
  22.6 8.7 %collective-permute-start.2 = (bf16[24,2048]{1,0:T(8,128)(2,1)S(1)}, bf16[24,2048]{1,0:T(8,128)(2,1)S(1)}, u32[]{:S(2)}, u32[]{:S(2)}) collective-permute-start(bf16[24,2048]{1,0:T(8,128)(2,1)S(1)} %get-tuple-element.35), channel_id=1, source_target_pairs={{0,2},{1,3},{2,0},{3,1},{4,6},{5,7},{6,4},{7,5},{8,10},{9,11},{10,... | collective-permute-start | bytes 294920 | tf_op jit(solution)/shard_map/ppermute | solution.py:387
  23.9 7.5 %collective-permute-start.3 = (bf16[24,2048]{1,0:T(8,128)(2,1)S(1)}, bf16[24,2048]{1,0:T(8,128)(2,1)S(1)}, u32[]{:S(2)}, u32[]{:S(2)}) collective-permute-start(bf16[24,2048]{1,0:T(8,128)(2,1)S(1)} %get-tuple-element.36), channel_id=1, source_target_pairs={{0,4},{1,5},{2,6},{3,7},{4,0},{5,1},{6,2},{7,3},{8,12},{9,13},{10,... | collective-permute-start | bytes 294920 | tf_op jit(solution)/shard_map/ppermute | solution.py:387
  25.1 6.2 %collective-permute-start.4 = (bf16[24,2048]{1,0:T(8,128)(2,1)S(1)}, bf16[24,2048]{1,0:T(8,128)(2,1)S(1)}, u32[]{:S(2)}, u32[]{:S(2)}) collective-permute-start(bf16[24,2048]{1,0:T(8,128)(2,1)S(1)} %get-tuple-element.37), channel_id=1, source_target_pairs={{0,6},{1,7},{2,4},{3,5},{4,2},{5,3},{6,0},{7,1},{8,14},{9,15},{10,... | collective-permute-start | bytes 294920 | tf_op jit(solution)/shard_map/ppermute | solution.py:387
  31.4 21.5 %copy-start = (f32[2,16,1]{1,2,0:T(1,128)S(1)}, f32[2,16,1]{1,2,0:T(1,128)}, u32[]{:S(2)}) copy-start(f32[2,16,1]{1,2,0:T(1,128)} %param.10) | copy-start | bytes 388
  33.6 4.9 %collective-permute-start.11 = (bf16[24,2048]{1,0:T(8,128)(2,1)S(1)}, bf16[24,2048]{1,0:T(8,128)(2,1)S(1)}, u32[]{:S(2)}, u32[]{:S(2)}) collective-permute-start(bf16[24,2048]{1,0:T(8,128)(2,1)S(1)} %get-tuple-element.48), channel_id=1, source_target_pairs={{0,2},{1,3},{2,0},{3,1},{4,6},{5,7},{6,4},{7,5},{8,10},{9,11},{10,... | collective-permute-start | bytes 294920 | tf_op jit(solution)/shard_map/ppermute | solution.py:387
  34.4 4.6 %collective-permute-start.12 = (bf16[24,2048]{1,0:T(8,128)(2,1)S(1)}, bf16[24,2048]{1,0:T(8,128)(2,1)S(1)}, u32[]{:S(2)}, u32[]{:S(2)}) collective-permute-start(bf16[24,2048]{1,0:T(8,128)(2,1)S(1)} %get-tuple-element.49), channel_id=1, source_target_pairs={{0,4},{1,5},{2,6},{3,7},{4,0},{5,1},{6,2},{7,3},{8,12},{9,13},{10,... | collective-permute-start | bytes 294920 | tf_op jit(solution)/shard_map/ppermute | solution.py:387
  35.6 5.5 %collective-permute-start.13 = (bf16[24,2048]{1,0:T(8,128)(2,1)S(1)}, bf16[24,2048]{1,0:T(8,128)(2,1)S(1)}, u32[]{:S(2)}, u32[]{:S(2)}) collective-permute-start(bf16[24,2048]{1,0:T(8,128)(2,1)S(1)} %get-tuple-element.50), channel_id=1, source_target_pairs={{0,6},{1,7},{2,4},{3,5},{4,2},{5,3},{6,0},{7,1},{8,14},{9,15},{10,... | collective-permute-start | bytes 294920 | tf_op jit(solution)/shard_map/ppermute | solution.py:387
  41.3 11.6 %collective-permute-start.14 = (bf16[32,2048]{1,0:T(8,128)(2,1)S(1)}, bf16[32,2048]{1,0:T(8,128)(2,1)S(1)}, u32[]{:S(2)}, u32[]{:S(2)}) collective-permute-start(bf16[32,2048]{1,0:T(8,128)(2,1)S(1)} %shard_map.109), channel_id=1, source_target_pairs={{0,8},{1,9},{2,10},{3,11},{4,12},{5,13},{6,14},{7,15},{8,0},{9,1},... | collective-permute-start | bytes 393224 | tf_op jit(solution)/shard_map/ppermute | solution.py:387
  45.8 4.7 %collective-permute-start.16 = (bf16[24,2048]{1,0:T(8,128)(2,1)S(1)}, bf16[24,2048]{1,0:T(8,128)(2,1)S(1)}, u32[]{:S(2)}, u32[]{:S(2)}) collective-permute-start(bf16[24,2048]{1,0:T(8,128)(2,1)S(1)} %get-tuple-element.53), channel_id=1, source_target_pairs={{0,2},{1,3},{2,0},{3,1},{4,6},{5,7},{6,4},{7,5},{8,10},{9,11},{10,... | collective-permute-start | bytes 294920 | tf_op jit(solution)/shard_map/ppermute | solution.py:387
  46.0 4.6 %collective-permute-start.17 = (bf16[24,2048]{1,0:T(8,128)(2,1)S(1)}, bf16[24,2048]{1,0:T(8,128)(2,1)S(1)}, u32[]{:S(2)}, u32[]{:S(2)}) collective-permute-start(bf16[24,2048]{1,0:T(8,128)(2,1)S(1)} %get-tuple-element.54), channel_id=1, source_target_pairs={{0,4},{1,5},{2,6},{3,7},{4,0},{5,1},{6,2},{7,3},{8,12},{9,13},{10,... | collective-permute-start | bytes 294920 | tf_op jit(solution)/shard_map/ppermute | solution.py:387
  47.1 5.8 %collective-permute-start.18 = (bf16[24,2048]{1,0:T(8,128)(2,1)S(1)}, bf16[24,2048]{1,0:T(8,128)(2,1)S(1)}, u32[]{:S(2)}, u32[]{:S(2)}) collective-permute-start(bf16[24,2048]{1,0:T(8,128)(2,1)S(1)} %get-tuple-element.55), channel_id=1, source_target_pairs={{0,6},{1,7},{2,4},{3,5},{4,2},{5,3},{6,0},{7,1},{8,14},{9,15},{10,... | collective-permute-start | bytes 294920 | tf_op jit(solution)/shard_map/ppermute | solution.py:387
  49.3 1.2 %collective-permute-start.15 = (f32[8,128]{1,0:T(8,128)S(1)}, f32[8,128]{1,0:T(8,128)S(1)}, u32[]{:S(2)}, u32[]{:S(2)}) collective-permute-start(f32[8,128]{1,0:T(8,128)S(1)} %get-tuple-element.51.load_ref), channel_id=1, source_target_pairs={{0,1},{1,0},{2,3},{3,2},{4,5},{5,4},{6,7},{7,6},{8,9},{9,8},{10,11... | collective-permute-start | bytes 12296 | tf_op jit(solution)/shard_map/ppermute | solution.py:387

commit v3 on v2

--- a/solution.py
+++ b/solution.py
@@ -314,8 +314,21 @@
     refs[SQUARE][...] = chosen(sel_ref, refs[:SQUARE]).astype(jnp.bfloat16)
 
 
-def final_kernel(meta, sel_ref, weight_ref, back_ref, load_ref, load_far_ref, *refs):
-    out_ref, slot_ref = refs[SQUARE], refs[SQUARE + 1]
+def merge_own_kernel(sel_ref, weight_ref, *refs):
+    out_ref, scale_ref = refs[SQUARE:]
+    out_ref[...] = chosen(sel_ref, refs[:SQUARE]).astype(jnp.bfloat16)
+    batches, tokens = weight_ref.shape
+    lane = lax.broadcasted_iota(jnp.int32, (tokens, tokens), 0)
+    same = lane == lax.broadcasted_iota(jnp.int32, (tokens, tokens), 1)
+    for batch in range(batches):
+        column = jnp.where(same, weight_ref[batch : batch + 1, :], 0.0)
+        column = jnp.sum(column, axis=1, keepdims=True)
+        scale_ref[batch * tokens : (batch + 1) * tokens, :] = jnp.broadcast_to(
+            column, (tokens, LANES)
+        )
+
+
+def final_kernel(meta, own_ref, scale_ref, load_ref, load_far_ref, back_ref, out_ref, slot_ref):
     core = lax.axis_index("expert") % 2
     both = load_ref[...] + load_far_ref[...]
     row = lax.broadcasted_iota(jnp.int32, both.shape, 0)
@@ -323,42 +336,27 @@
     slot_ref[0] = jnp.sum(jnp.where((row == meta % 8) & (lane == core), both, 0.0)).astype(
         jnp.int32
     )
-    batches, tokens = weight_ref.shape
-    total = chosen(sel_ref, refs[:SQUARE]) + back_ref[...].astype(jnp.float32)
-    lane = lax.broadcasted_iota(jnp.int32, (tokens, tokens), 0)
-    same = lane == lax.broadcasted_iota(jnp.int32, (tokens, tokens), 1)
-    scale = jnp.concatenate(
-        [
-            jnp.sum(
-                jnp.where(same, weight_ref[batch : batch + 1, :], 0.0), axis=1, keepdims=True
-            )
-            for batch in range(batches)
-        ],
-        axis=0,
-    )
-    out_ref[...] = (total * scale).astype(jnp.bfloat16)
-
-
-def merge_rows(kernel, sel, others, blocks, loads):
-    count = sel.shape[1]
-    width = blocks[0].shape[1]
-    shapes = [jax.ShapeDtypeStruct((count, width), jnp.bfloat16)]
-    specs = [pl.BlockSpec(memory_space=VMEM)]
-    if loads:
-        shapes.append(jax.ShapeDtypeStruct((1,), jnp.int32))
-        specs.append(pl.BlockSpec(memory_space=SMEM))
+    total = own_ref[...].astype(jnp.float32) + back_ref[...].astype(jnp.float32)
+    out_ref[...] = (total * scale_ref[:, :1]).astype(jnp.bfloat16)
+
+
+def small_call(kernel, shapes, *operands, slot=False):
+    specs = [pl.BlockSpec(memory_space=VMEM)] * len(shapes)
+    if slot:
+        shapes = shapes + [jax.ShapeDtypeStruct((1,), jnp.int32)]
+        specs = specs + [pl.BlockSpec(memory_space=SMEM)]
     return pl.pallas_call(
         kernel,
         out_shape=shapes,
-        in_specs=[pl.BlockSpec(memory_space=VMEM)] * (SQUARE + 1 + len(others)),
+        in_specs=[pl.BlockSpec(memory_space=VMEM)] * len(operands),
         out_specs=specs,
         cost_estimate=pl.CostEstimate(
-            flops=2 * sel.shape[0] * count * width,
-            bytes_accessed=2 * (sel.shape[0] + count) * width,
+            flops=2 * sum(shape.size for shape in shapes) * LANES,
+            bytes_accessed=2 * sum(operand.size for operand in operands),
             transcendentals=0,
         ),
         compiler_params=pltpu.CompilerParams(vmem_limit_bytes=SMALL),
-    )(sel, *others, *blocks)
+    )(*operands)
 
 
 def swapped(size, bits):
@@ -411,15 +409,26 @@
     results_far = around(results_far)
     results = around(results)
     load_far = swap(load, 1)
-    (far,) = merge_rows(merge_kernel, sel_far, (), results_far, False)
+    whole = jax.ShapeDtypeStruct((rows, width), jnp.bfloat16)
+    (far,) = small_call(merge_kernel, [whole], sel_far, *results_far)
     back = swap(far, distant)
     weight = pick_weight.reshape(batches, tokens)
-    output, slot_load = merge_rows(
+    own, scale = small_call(
+        merge_own_kernel,
+        [whole, jax.ShapeDtypeStruct((rows, LANES), jnp.float32)],
+        sel,
+        weight,
+        *results,
+    )
+    output, slot_load = small_call(
         functools.partial(final_kernel, meta),
-        sel,
-        (weight, back, load, load_far),
-        results,
-        True,
+        [whole],
+        own,
+        scale,
+        load,
+        load_far,
+        back,
+        slot=True,
     )
     return output.reshape(batches, tokens, width), slot_load
 

time: 54 us -> 54.1 us (level)
    pallas_call x2 -> x3, Pallas kernels: 1.14 us -> 1.21 us  [small_call(): pl.pallas_call(kernel, out_shape=shapes, in_specs=[pl.BlockSpec(memory_sp...]
  transfers between devices with their start and end apart: 19 -> 19, of which waited for: 10 -> 10; matrix products, arithmetic and copies ran while one was open for 0% -> 0% of each run, Pallas kernels for 12% -> 13%
where the time goes in v3:
time: 54.1 us; the launch traced here: 53.9 us
  starting transfers between devices  24.3 us (45%)
  waiting for transfers between devices  18.8 us (35%)
  Pallas kernels  10 us (18%)
  between operations  0.75 us (1%)
    ppermute x19, starting transfers between devices, swap(): return lax.ppermute(value, 'expert', swapped(size, bits))  24.3 us
    ppermute x19, waiting for transfers between devices, swap(): return lax.ppermute(value, 'expert', swapped(size, bits))  18.8 us
    pallas_call x2, Pallas kernels, run_expert(): pl.pallas_call(functools.partial(expert_kernel, meta), out_shape=[jax.Sha...  4.43 us
    pallas_call x1, Pallas kernels, fetched(): pl.pallas_call(fetch_kernel, out_shape=[jax.ShapeDtypeStruct(value.shape,...  2.38 us
    pallas_call x1, Pallas kernels, pick_own(): pl.pallas_call(functools.partial(pick_own_kernel, cap), out_shape=shapes,...  1.47 us
    pallas_call x3, Pallas kernels, small_call(): pl.pallas_call(kernel, out_shape=shapes, in_specs=[pl.BlockSpec(memory_sp...  1.21 us
  transfers between devices with their start and end apart: 19, of which 10 were waited for; matrix products, arithmetic and copies ran while one was open for 0% of the time, Pallas kernels for 13%

profile of v3, /device:TPU:0, one launch (start us, length us, event | category | flops | bytes accessed | tf_op | source)
XLA Modules:
  0.0 53.9 jit_solution(18371885238633384325)
XLA Ops:
  0.6 0.6 %collective-permute-start.3 = (bf16[1,2048,384]{2,1,0:T(8,128)(2,1)}, bf16[1,2048,384]{2,1,0:T(8,128)(2,1)S(1)}, u32[]{:S(2)}, u32[]{:S(2)}) collective-permute-start(bf16[1,2048,384]{2,1,0:T(8,128)(2,1)} %refs_0_.1), channel_id=1, source_target_pairs={{0,1},{1,0},{2,3},{3,2},{4,5},{5,4},{6,7},{7,6},{8,9},{9,8},{10,11... | collective-permute-start | bytes 4718600 | tf_op jit(solution)/shard_map/ppermute | solution.py:385
  1.3 0.4 collective-permute-start.5
  1.7 3.7 %collective-permute-start.9 = (bf16[32,2048]{1,0:T(8,128)(2,1)}, bf16[32,2048]{1,0:T(8,128)(2,1)S(1)}, u32[]{:S(2)}, u32[]{:S(2)}) collective-permute-start(bf16[32,2048]{1,0:T(8,128)(2,1)} %bitcast.6), channel_id=1, source_target_pairs={{0,8},{1,9},{2,10},{3,11},{4,12},{5,13},{6,14},{7,15},{8,0},{9,1},... | collective-permute-start | bytes 393224 | tf_op jit(solution)/shard_map/ppermute | solution.py:385
  5.4 1.5 %shard_map.104 = (bf16[24,2048]{1,0:T(8,128)(2,1)S(1)}, bf16[24,2048]{1,0:T(8,128)(2,1)S(1)}, bf16[24,2048]{1,0:T(8,128)(2,1)S(1)}, bf16[24,2048]{1,0:T(8,128)(2...) custom-call(s32[8]{0:T(128)} %home_hbm.1, ...), custom_call_target="tpu_custom_call" | custom-call | flops 12582912 | bytes 786432 | tf_op jit(solution)/shard_map/pallas_call | solution.py:206
  6.9 5.6 %collective-permute-done.10.picks_ref = s32[4,16]{1,0:T(4,128)S(1)} collective-permute-done((s32[4,16]{1,0:T(4,128)S(1)}, s32[4,16]{1,0:T(4,128)S(1)}, u32[]{:S(2)}, u32[]{:S(2)}) %collective-permute-start.10) | collective-permute-done | bytes 288 | tf_op jit(solution)/shard_map/ppermute | solution.py:385
  12.5 1.5 %collective-permute-start = (bf16[24,2048]{1,0:T(8,128)(2,1)S(1)}, bf16[24,2048]{1,0:T(8,128)(2,1)S(1)}, u32[]{:S(2)}, u32[]{:S(2)}) collective-permute-start(bf16[24,2048]{1,0:T(8,128)(2,1)S(1)} %get-tuple-element.34), channel_id=1, source_target_pairs={{0,2},{1,3},{2,0},{3,1},{4,6},{5,7},{6,4},{7,5},{8,10},{9,11},{10,... | collective-permute-start | bytes 294920 | tf_op jit(solution)/shard_map/ppermute | solution.py:385
  14.1 3.1 %collective-permute-done.refs_1_ = bf16[24,2048]{1,0:T(8,128)(2,1)S(1)} collective-permute-done((bf16[24,2048]{1,0:T(8,128)(2,1)S(1)}, bf16[24,2048]{1,0:T(8,128)(2,1)S(1)}, u32[]{:S(2)}, u32[]{:S(2)}) %collective-permute-start) | collective-permute-done | bytes 98336 | tf_op jit(solution)/shard_map/ppermute | solution.py:385
  17.2 0.9 %collective-permute-start.1 = (bf16[24,2048]{1,0:T(8,128)(2,1)S(1)}, bf16[24,2048]{1,0:T(8,128)(2,1)S(1)}, u32[]{:S(2)}, u32[]{:S(2)}) collective-permute-start(bf16[24,2048]{1,0:T(8,128)(2,1)S(1)} %get-tuple-element.35), channel_id=1, source_target_pairs={{0,4},{1,5},{2,6},{3,7},{4,0},{5,1},{6,2},{7,3},{8,12},{9,13},{10,... | collective-permute-start | bytes 294920 | tf_op jit(solution)/shard_map/ppermute | solution.py:385
  18.1 2.1 %collective-permute-start.2 = (bf16[24,2048]{1,0:T(8,128)(2,1)S(1)}, bf16[24,2048]{1,0:T(8,128)(2,1)S(1)}, u32[]{:S(2)}, u32[]{:S(2)}) collective-permute-start(bf16[24,2048]{1,0:T(8,128)(2,1)S(1)} %get-tuple-element.36), channel_id=1, source_target_pairs={{0,6},{1,7},{2,4},{3,5},{4,2},{5,3},{6,0},{7,1},{8,14},{9,15},{10,... | collective-permute-start | bytes 294920 | tf_op jit(solution)/shard_map/ppermute | solution.py:385
  20.2 0.5 shard_map.108
  20.7 1.9 %collective-permute-done.1.refs_2_ = bf16[24,2048]{1,0:T(8,128)(2,1)S(1)} collective-permute-done((bf16[24,2048]{1,0:T(8,128)(2,1)S(1)}, bf16[24,2048]{1,0:T(8,128)(2,1)S(1)}, u32[]{:S(2)}, u32[]{:S(2)}) %collective-permute-start.1) | collective-permute-done | bytes 98336 | tf_op jit(solution)/shard_map/ppermute | solution.py:385
  22.6 0.7 %collective-permute-start.11 = (bf16[24,2048]{1,0:T(8,128)(2,1)S(1)}, bf16[24,2048]{1,0:T(8,128)(2,1)S(1)}, u32[]{:S(2)}, u32[]{:S(2)}) collective-permute-start(bf16[24,2048]{1,0:T(8,128)(2,1)S(1)} %get-tuple-element.50), channel_id=1, source_target_pairs={{0,2},{1,3},{2,0},{3,1},{4,6},{5,7},{6,4},{7,5},{8,10},{9,11},{10,... | collective-permute-start | bytes 294920 | tf_op jit(solution)/shard_map/ppermute | solution.py:385
  23.3 0.6 %collective-permute-done.2.refs_3_ = bf16[24,2048]{1,0:T(8,128)(2,1)S(1)} collective-permute-done((bf16[24,2048]{1,0:T(8,128)(2,1)S(1)}, bf16[24,2048]{1,0:T(8,128)(2,1)S(1)}, u32[]{:S(2)}, u32[]{:S(2)}) %collective-permute-start.2) | collective-permute-done | bytes 98336 | tf_op jit(solution)/shard_map/ppermute | solution.py:385
  23.9 1.2 %collective-permute-start.12 = (bf16[24,2048]{1,0:T(8,128)(2,1)S(1)}, bf16[24,2048]{1,0:T(8,128)(2,1)S(1)}, u32[]{:S(2)}, u32[]{:S(2)}) collective-permute-start(bf16[24,2048]{1,0:T(8,128)(2,1)S(1)} %get-tuple-element.51), channel_id=1, source_target_pairs={{0,4},{1,5},{2,6},{3,7},{4,0},{5,1},{6,2},{7,3},{8,12},{9,13},{10,... | collective-permute-start | bytes 294920 | tf_op jit(solution)/shard_map/ppermute | solution.py:385
  25.1 1.6 %collective-permute-start.13 = (bf16[24,2048]{1,0:T(8,128)(2,1)S(1)}, bf16[24,2048]{1,0:T(8,128)(2,1)S(1)}, u32[]{:S(2)}, u32[]{:S(2)}) collective-permute-start(bf16[24,2048]{1,0:T(8,128)(2,1)S(1)} %get-tuple-element.52), channel_id=1, source_target_pairs={{0,6},{1,7},{2,4},{3,5},{4,2},{5,3},{6,0},{7,1},{8,14},{9,15},{10,... | collective-permute-start | bytes 294920 | tf_op jit(solution)/shard_map/ppermute | solution.py:385
  26.7 2.4 %shard_map.105 = (bf16[1,2048,384]{2,1,0:T(8,128)(2,1)S(1)}, bf16[1,2048,384]{2,1,0:T(8,128)(2,1)S(1)}, bf16[1,2048,384]{2,1,0:T(8,128)(2,1)S(1)}) custom-call(bf16[1,2048,384]{2,1,0:T(8,128)(2,1)} %refs_0_.1, bf16[1,2048,384]{2,1,0:T(8,128)(2,1)} %refs_1_.1, bf16[1,2048,384]{2,1,0:T(8,128)(2,1)} %refs_2_.1), custom_call_target="tpu_custom_call" | custom-call | bytes 9437184 | tf_op jit(solution)/shard_map/pallas_call | solution.py:251
  29.1 2.2 %shard_map.106 = (bf16[24,2048]{1,0:T(8,128)(2,1)S(1)}, bf16[24,2048]{1,0:T(8,128)(2,1)S(1)}, bf16[24,2048]{1,0:T(8,128)(2,1)S(1)}, bf16[24,2048]{1,0:T(8,128)(2,1)S(1)}, f32[8,128]{1,0:T(8,128)S(1)}) custom-call(bf16[24,2048]{1,0:T(8,128)(2,1)S(1)} %get-tuple-element.33.refs_0_, bf16[24,2048]{1,0:T(8,128)(2,1)S(1)} %collective-permute-done.refs_1_, ...), custom_call_target="tpu_custom_call" | custom-call | flops 905969664 | bytes 10223616 | tf_op jit(solution)/shard_map/pallas_call | solution.py:291
  31.4 2.2 %shard_map.109 = (bf16[24,2048]{1,0:T(8,128)(2,1)S(1)}, bf16[24,2048]{1,0:T(8,128)(2,1)S(1)}, bf16[24,2048]{1,0:T(8,128)(2,1)S(1)}, bf16[24,2048]{1,0:T(8,128)(2,1)S(1)}, f32[8,128]{1,0:T(8,128)S(1)}) custom-call(bf16[24,2048]{1,0:T(8,128)(2,1)S(1)} %get-tuple-element.49.refs_0_, bf16[24,2048]{1,0:T(8,128)(2,1)S(1)} %collective-permute-done.11.refs_1_, ...), custom_call_target="tpu_custom_call" | custom-call | flops 905969664 | bytes 10223616 | tf_op jit(solution)/shard_map/pallas_call | solution.py:291
  33.6 0.8 %collective-permute-start.15 = (bf16[24,2048]{1,0:T(8,128)(2,1)S(1)}, bf16[24,2048]{1,0:T(8,128)(2,1)S(1)}, u32[]{:S(2)}, u32[]{:S(2)}) collective-permute-start(bf16[24,2048]{1,0:T(8,128)(2,1)S(1)} %get-tuple-element.57), channel_id=1, source_target_pairs={{0,2},{1,3},{2,0},{3,1},{4,6},{5,7},{6,4},{7,5},{8,10},{9,11},{10,... | collective-permute-start | bytes 294920 | tf_op jit(solution)/shard_map/ppermute | solution.py:385
  34.4 1.2 %collective-permute-start.16 = (bf16[24,2048]{1,0:T(8,128)(2,1)S(1)}, bf16[24,2048]{1,0:T(8,128)(2,1)S(1)}, u32[]{:S(2)}, u32[]{:S(2)}) collective-permute-start(bf16[24,2048]{1,0:T(8,128)(2,1)S(1)} %get-tuple-element.58), channel_id=1, source_target_pairs={{0,4},{1,5},{2,6},{3,7},{4,0},{5,1},{6,2},{7,3},{8,12},{9,13},{10,... | collective-permute-start | bytes 294920 | tf_op jit(solution)/shard_map/ppermute | solution.py:385
  35.6 1.6 %collective-permute-start.17 = (bf16[24,2048]{1,0:T(8,128)(2,1)S(1)}, bf16[24,2048]{1,0:T(8,128)(2,1)S(1)}, u32[]{:S(2)}, u32[]{:S(2)}) collective-permute-start(bf16[24,2048]{1,0:T(8,128)(2,1)S(1)} %get-tuple-element.59), channel_id=1, source_target_pairs={{0,6},{1,7},{2,4},{3,5},{4,2},{5,3},{6,0},{7,1},{8,14},{9,15},{10,... | collective-permute-start | bytes 294920 | tf_op jit(solution)/shard_map/ppermute | solution.py:385
  37.2 1.4 %collective-permute-done.15.refs_1_ = bf16[24,2048]{1,0:T(8,128)(2,1)S(1)} collective-permute-done((bf16[24,2048]{1,0:T(8,128)(2,1)S(1)}, bf16[24,2048]{1,0:T(8,128)(2,1)S(1)}, u32[]{:S(2)}, u32[]{:S(2)}) %collective-permute-start.15) | collective-permute-done | bytes 98336 | tf_op jit(solution)/shard_map/ppermute | solution.py:385
  38.5 0.5 collective-permute-done.16.refs_2_
  39.0 2.1 %collective-permute-done.17.refs_3_ = bf16[24,2048]{1,0:T(8,128)(2,1)S(1)} collective-permute-done((bf16[24,2048]{1,0:T(8,128)(2,1)S(1)}, bf16[24,2048]{1,0:T(8,128)(2,1)S(1)}, u32[]{:S(2)}, u32[]{:S(2)}) %collective-permute-start.17) | collective-permute-done | bytes 98336 | tf_op jit(solution)/shard_map/ppermute | solution.py:385
  41.3 4.5 %collective-permute-start.18 = (bf16[32,2048]{1,0:T(8,128)(2,1)S(1)}, bf16[32,2048]{1,0:T(8,128)(2,1)S(1)}, u32[]{:S(2)}, u32[]{:S(2)}) collective-permute-start(bf16[32,2048]{1,0:T(8,128)(2,1)S(1)} %shard_map.110), channel_id=1, source_target_pairs={{0,8},{1,9},{2,10},{3,11},{4,12},{5,13},{6,14},{7,15},{8,0},{9,1},... | collective-permute-start | bytes 393224 | tf_op jit(solution)/shard_map/ppermute | solution.py:385
  45.8 0.3 collective-permute-start.6
  46.0 1.1 %collective-permute-start.7 = (bf16[24,2048]{1,0:T(8,128)(2,1)S(1)}, bf16[24,2048]{1,0:T(8,128)(2,1)S(1)}, u32[]{:S(2)}, u32[]{:S(2)}) collective-permute-start(bf16[24,2048]{1,0:T(8,128)(2,1)S(1)} %get-tuple-element.43), channel_id=1, source_target_pairs={{0,4},{1,5},{2,6},{3,7},{4,0},{5,1},{6,2},{7,3},{8,12},{9,13},{10,... | collective-permute-start | bytes 294920 | tf_op jit(solution)/shard_map/ppermute | solution.py:385
  47.1 2.1 %collective-permute-start.8 = (bf16[24,2048]{1,0:T(8,128)(2,1)S(1)}, bf16[24,2048]{1,0:T(8,128)(2,1)S(1)}, u32[]{:S(2)}, u32[]{:S(2)}) collective-permute-start(bf16[24,2048]{1,0:T(8,128)(2,1)S(1)} %get-tuple-element.44), channel_id=1, source_target_pairs={{0,6},{1,7},{2,4},{3,5},{4,2},{5,3},{6,0},{7,1},{8,14},{9,15},{10,... | collective-permute-start | bytes 294920 | tf_op jit(solution)/shard_map/ppermute | solution.py:385
  49.3 1.1 %collective-permute-done.6.refs_1_ = bf16[24,2048]{1,0:T(8,128)(2,1)S(1)} collective-permute-done((bf16[24,2048]{1,0:T(8,128)(2,1)S(1)}, bf16[24,2048]{1,0:T(8,128)(2,1)S(1)}, u32[]{:S(2)}, u32[]{:S(2)}) %collective-permute-start.6) | collective-permute-done | bytes 98336 | tf_op jit(solution)/shard_map/ppermute | solution.py:385
  50.4 0.3 collective-permute-done.7.refs_2_
  50.7 2.2 %collective-permute-done.8.refs_3_ = bf16[24,2048]{1,0:T(8,128)(2,1)S(1)} collective-permute-done((bf16[24,2048]{1,0:T(8,128)(2,1)S(1)}, bf16[24,2048]{1,0:T(8,128)(2,1)S(1)}, u32[]{:S(2)}, u32[]{:S(2)}) %collective-permute-start.8) | collective-permute-done | bytes 98336 | tf_op jit(solution)/shard_map/ppermute | solution.py:385
  53.2 0.8 %shard_map.111 = (bf16[32,2048]{1,0:T(8,128)(2,1)}, s32[1]{0:T(128)}) custom-call(bf16[32,2048]{1,0:T(8,128)(2,1)S(1)} %get-tuple-element.45.own_ref, f32[32,128]{1,0:T(8,128)S(1)} %get-tuple-element.46.scale_ref, f32[8,128]{1,0:T(8,128)S(1)} %get-tuple-element.54.load_ref, f32[8,128]{1,0:T(8,128)S(1)} %collective-permute-done.14.load_far_ref, ...), custom_call_target="tpu_custom_call" | custom-call | flops 16777472 | bytes 274432 | tf_op jit(solution)/shard_map/pallas_call | solution.py:348
  (16 shorter events, 0.6 us)
Async XLA Ops:
  0.6 24.5 %collective-permute-start.3 = (bf16[1,2048,384]{2,1,0:T(8,128)(2,1)}, bf16[1,2048,384]{2,1,0:T(8,128)(2,1)S(1)}, u32[]{:S(2)}, u32[]{:S(2)}) collective-permute-start(bf16[1,2048,384]{2,1,0:T(8,128)(2,1)} %refs_0_.1), channel_id=1, source_target_pairs={{0,1},{1,0},{2,3},{3,2},{4,5},{5,4},{6,7},{7,6},{8,9},{9,8},{10,11... | collective-permute-start | bytes 4718600 | tf_op jit(solution)/shard_map/ppermute | solution.py:385
  1.2 27.9 %collective-permute-start.4 = (bf16[1,2048,384]{2,1,0:T(8,128)(2,1)}, bf16[1,2048,384]{2,1,0:T(8,128)(2,1)S(1)}, u32[]{:S(2)}, u32[]{:S(2)}) collective-permute-start(bf16[1,2048,384]{2,1,0:T(8,128)(2,1)} %refs_1_.1), channel_id=1, source_target_pairs={{0,1},{1,0},{2,3},{3,2},{4,5},{5,4},{6,7},{7,6},{8,9},{9,8},{10,11... | collective-permute-start | bytes 4718600 | tf_op jit(solution)/shard_map/ppermute | solution.py:385
  1.3 27.9 %collective-permute-start.5 = (bf16[1,2048,384]{2,1,0:T(8,128)(2,1)}, bf16[1,2048,384]{2,1,0:T(8,128)(2,1)S(1)}, u32[]{:S(2)}, u32[]{:S(2)}) collective-permute-start(bf16[1,2048,384]{2,1,0:T(8,128)(2,1)} %refs_2_.1), channel_id=1, source_target_pairs={{0,1},{1,0},{2,3},{3,2},{4,5},{5,4},{6,7},{7,6},{8,9},{9,8},{10,11... | collective-permute-start | bytes 4718600 | tf_op jit(solution)/shard_map/ppermute | solution.py:385
  1.7 16.4 %collective-permute-start.9 = (bf16[32,2048]{1,0:T(8,128)(2,1)}, bf16[32,2048]{1,0:T(8,128)(2,1)S(1)}, u32[]{:S(2)}, u32[]{:S(2)}) collective-permute-start(bf16[32,2048]{1,0:T(8,128)(2,1)} %bitcast.6), channel_id=1, source_target_pairs={{0,8},{1,9},{2,10},{3,11},{4,12},{5,13},{6,14},{7,15},{8,0},{9,1},... | collective-permute-start | bytes 393224 | tf_op jit(solution)/shard_map/ppermute | solution.py:385
  6.8 5.7 %collective-permute-start.10 = (s32[4,16]{1,0:T(4,128)S(1)}, s32[4,16]{1,0:T(4,128)S(1)}, u32[]{:S(2)}, u32[]{:S(2)}) collective-permute-start(s32[4,16]{1,0:T(4,128)S(1)} %get-tuple-element.48), channel_id=1, source_target_pairs={{0,8},{1,9},{2,10},{3,11},{4,12},{5,13},{6,14},{7,15},{8,0},{9,1},... | collective-permute-start | bytes 776 | tf_op jit(solution)/shard_map/ppermute | solution.py:385
  12.5 4.6 %collective-permute-start = (bf16[24,2048]{1,0:T(8,128)(2,1)S(1)}, bf16[24,2048]{1,0:T(8,128)(2,1)S(1)}, u32[]{:S(2)}, u32[]{:S(2)}) collective-permute-start(bf16[24,2048]{1,0:T(8,128)(2,1)S(1)} %get-tuple-element.34), channel_id=1, source_target_pairs={{0,2},{1,3},{2,0},{3,1},{4,6},{5,7},{6,4},{7,5},{8,10},{9,11},{10,... | collective-permute-start | bytes 294920 | tf_op jit(solution)/shard_map/ppermute | solution.py:385
  17.2 5.5 %collective-permute-start.1 = (bf16[24,2048]{1,0:T(8,128)(2,1)S(1)}, bf16[24,2048]{1,0:T(8,128)(2,1)S(1)}, u32[]{:S(2)}, u32[]{:S(2)}) collective-permute-start(bf16[24,2048]{1,0:T(8,128)(2,1)S(1)} %get-tuple-element.35), channel_id=1, source_target_pairs={{0,4},{1,5},{2,6},{3,7},{4,0},{5,1},{6,2},{7,3},{8,12},{9,13},{10,... | collective-permute-start | bytes 294920 | tf_op jit(solution)/shard_map/ppermute | solution.py:385
  18.1 5.8 %collective-permute-start.2 = (bf16[24,2048]{1,0:T(8,128)(2,1)S(1)}, bf16[24,2048]{1,0:T(8,128)(2,1)S(1)}, u32[]{:S(2)}, u32[]{:S(2)}) collective-permute-start(bf16[24,2048]{1,0:T(8,128)(2,1)S(1)} %get-tuple-element.36), channel_id=1, source_target_pairs={{0,6},{1,7},{2,4},{3,5},{4,2},{5,3},{6,0},{7,1},{8,14},{9,15},{10,... | collective-permute-start | bytes 294920 | tf_op jit(solution)/shard_map/ppermute | solution.py:385
  22.6 8.7 %collective-permute-start.11 = (bf16[24,2048]{1,0:T(8,128)(2,1)S(1)}, bf16[24,2048]{1,0:T(8,128)(2,1)S(1)}, u32[]{:S(2)}, u32[]{:S(2)}) collective-permute-start(bf16[24,2048]{1,0:T(8,128)(2,1)S(1)} %get-tuple-element.50), channel_id=1, source_target_pairs={{0,2},{1,3},{2,0},{3,1},{4,6},{5,7},{6,4},{7,5},{8,10},{9,11},{10,... | collective-permute-start | bytes 294920 | tf_op jit(solution)/shard_map/ppermute | solution.py:385
  23.9 7.5 %collective-permute-start.12 = (bf16[24,2048]{1,0:T(8,128)(2,1)S(1)}, bf16[24,2048]{1,0:T(8,128)(2,1)S(1)}, u32[]{:S(2)}, u32[]{:S(2)}) collective-permute-start(bf16[24,2048]{1,0:T(8,128)(2,1)S(1)} %get-tuple-element.51), channel_id=1, source_target_pairs={{0,4},{1,5},{2,6},{3,7},{4,0},{5,1},{6,2},{7,3},{8,12},{9,13},{10,... | collective-permute-start | bytes 294920 | tf_op jit(solution)/shard_map/ppermute | solution.py:385
  25.1 6.2 %collective-permute-start.13 = (bf16[24,2048]{1,0:T(8,128)(2,1)S(1)}, bf16[24,2048]{1,0:T(8,128)(2,1)S(1)}, u32[]{:S(2)}, u32[]{:S(2)}) collective-permute-start(bf16[24,2048]{1,0:T(8,128)(2,1)S(1)} %get-tuple-element.52), channel_id=1, source_target_pairs={{0,6},{1,7},{2,4},{3,5},{4,2},{5,3},{6,0},{7,1},{8,14},{9,15},{10,... | collective-permute-start | bytes 294920 | tf_op jit(solution)/shard_map/ppermute | solution.py:385
  31.4 21.5 %copy-start = (f32[2,16,1]{1,2,0:T(1,128)S(1)}, f32[2,16,1]{1,2,0:T(1,128)}, u32[]{:S(2)}) copy-start(f32[2,16,1]{1,2,0:T(1,128)} %param.10) | copy-start | bytes 388
  33.6 4.9 %collective-permute-start.15 = (bf16[24,2048]{1,0:T(8,128)(2,1)S(1)}, bf16[24,2048]{1,0:T(8,128)(2,1)S(1)}, u32[]{:S(2)}, u32[]{:S(2)}) collective-permute-start(bf16[24,2048]{1,0:T(8,128)(2,1)S(1)} %get-tuple-element.57), channel_id=1, source_target_pairs={{0,2},{1,3},{2,0},{3,1},{4,6},{5,7},{6,4},{7,5},{8,10},{9,11},{10,... | collective-permute-start | bytes 294920 | tf_op jit(solution)/shard_map/ppermute | solution.py:385
  34.4 4.6 %collective-permute-start.16 = (bf16[24,2048]{1,0:T(8,128)(2,1)S(1)}, bf16[24,2048]{1,0:T(8,128)(2,1)S(1)}, u32[]{:S(2)}, u32[]{:S(2)}) collective-permute-start(bf16[24,2048]{1,0:T(8,128)(2,1)S(1)} %get-tuple-element.58), channel_id=1, source_target_pairs={{0,4},{1,5},{2,6},{3,7},{4,0},{5,1},{6,2},{7,3},{8,12},{9,13},{10,... | collective-permute-start | bytes 294920 | tf_op jit(solution)/shard_map/ppermute | solution.py:385
  35.6 5.5 %collective-permute-start.17 = (bf16[24,2048]{1,0:T(8,128)(2,1)S(1)}, bf16[24,2048]{1,0:T(8,128)(2,1)S(1)}, u32[]{:S(2)}, u32[]{:S(2)}) collective-permute-start(bf16[24,2048]{1,0:T(8,128)(2,1)S(1)} %get-tuple-element.59), channel_id=1, source_target_pairs={{0,6},{1,7},{2,4},{3,5},{4,2},{5,3},{6,0},{7,1},{8,14},{9,15},{10,... | collective-permute-start | bytes 294920 | tf_op jit(solution)/shard_map/ppermute | solution.py:385
  41.3 11.8 %collective-permute-start.18 = (bf16[32,2048]{1,0:T(8,128)(2,1)S(1)}, bf16[32,2048]{1,0:T(8,128)(2,1)S(1)}, u32[]{:S(2)}, u32[]{:S(2)}) collective-permute-start(bf16[32,2048]{1,0:T(8,128)(2,1)S(1)} %shard_map.110), channel_id=1, source_target_pairs={{0,8},{1,9},{2,10},{3,11},{4,12},{5,13},{6,14},{7,15},{8,0},{9,1},... | collective-permute-start | bytes 393224 | tf_op jit(solution)/shard_map/ppermute | solution.py:385
  45.8 4.6 %collective-permute-start.6 = (bf16[24,2048]{1,0:T(8,128)(2,1)S(1)}, bf16[24,2048]{1,0:T(8,128)(2,1)S(1)}, u32[]{:S(2)}, u32[]{:S(2)}) collective-permute-start(bf16[24,2048]{1,0:T(8,128)(2,1)S(1)} %get-tuple-element.42), channel_id=1, source_target_pairs={{0,2},{1,3},{2,0},{3,1},{4,6},{5,7},{6,4},{7,5},{8,10},{9,11},{10,... | collective-permute-start | bytes 294920 | tf_op jit(solution)/shard_map/ppermute | solution.py:385
  46.0 4.6 %collective-permute-start.7 = (bf16[24,2048]{1,0:T(8,128)(2,1)S(1)}, bf16[24,2048]{1,0:T(8,128)(2,1)S(1)}, u32[]{:S(2)}, u32[]{:S(2)}) collective-permute-start(bf16[24,2048]{1,0:T(8,128)(2,1)S(1)} %get-tuple-element.43), channel_id=1, source_target_pairs={{0,4},{1,5},{2,6},{3,7},{4,0},{5,1},{6,2},{7,3},{8,12},{9,13},{10,... | collective-permute-start | bytes 294920 | tf_op jit(solution)/shard_map/ppermute | solution.py:385
  47.1 5.8 %collective-permute-start.8 = (bf16[24,2048]{1,0:T(8,128)(2,1)S(1)}, bf16[24,2048]{1,0:T(8,128)(2,1)S(1)}, u32[]{:S(2)}, u32[]{:S(2)}) collective-permute-start(bf16[24,2048]{1,0:T(8,128)(2,1)S(1)} %get-tuple-element.44), channel_id=1, source_target_pairs={{0,6},{1,7},{2,4},{3,5},{4,2},{5,3},{6,0},{7,1},{8,14},{9,15},{10,... | collective-permute-start | bytes 294920 | tf_op jit(solution)/shard_map/ppermute | solution.py:385
  49.3 3.9 %collective-permute-start.14 = (f32[8,128]{1,0:T(8,128)S(1)}, f32[8,128]{1,0:T(8,128)S(1)}, u32[]{:S(2)}, u32[]{:S(2)}) collective-permute-start(f32[8,128]{1,0:T(8,128)S(1)} %get-tuple-element.54.load_ref), channel_id=1, source_target_pairs={{0,1},{1,0},{2,3},{3,2},{4,5},{5,4},{6,7},{7,6},{8,9},{9,8},{10,11... | collective-permute-start | bytes 12296 | tf_op jit(solution)/shard_map/ppermute | solution.py:385

commit v4 on v3

--- a/solution.py
+++ b/solution.py
@@ -12,6 +12,8 @@
 REPL = 5
 LANES = 128
 SQUARE = 4
+TILE = 8
+PANELS = 2
 SMALL = 4 << 20
 LARGE = 20 << 20
 VMEM = pltpu.VMEM
@@ -72,8 +74,56 @@
     return whole
 
 
+def tiling(count):
+    full, rest = divmod(count, TILE)
+    fold = TILE // rest if rest and TILE % rest == 0 else 1
+    if rest and fold == 1:
+        full, rest = full + 1, 0
+    return full, rest, fold
+
+
 def block_rows(batches, cap):
-    return -(-(batches * cap + 1) // 8) * 8
+    return -(-batches * cap // TILE) * TILE
+
+
+def block_lanes(count, width):
+    full, rest, fold = tiling(count)
+    return full * width + (width // fold if rest else 0)
+
+
+def packed(count, rows, ref):
+    full, rest, fold = tiling(count)
+    width = rows.shape[1]
+    for tile in range(full):
+        part = rows[tile * TILE : (tile + 1) * TILE]
+        ref[:, tile * width : (tile + 1) * width] = part.astype(ref.dtype)
+    if rest:
+        tail = rows[full * TILE : (full + 1) * TILE]
+        piece = width // fold
+        turn = steps(lax.broadcasted_iota(jnp.int32, (TILE, piece), 0), rest, fold)
+        value = tail[:, :piece]
+        for index in range(1, fold):
+            moved = pltpu.roll(tail[:, index * piece : (index + 1) * piece], index * rest, axis=0)
+            value = jnp.where(turn == index, moved, value)
+        ref[:, full * width : full * width + piece] = value.astype(ref.dtype)
+
+
+def unpacked(count, width, ref):
+    full, rest, fold = tiling(count)
+    tiles = [ref[:, tile * width : (tile + 1) * width] for tile in range(full)]
+    if rest:
+        piece = width // fold
+        tail = ref[:, full * width : full * width + piece].astype(jnp.float32)
+        parts = [tail]
+        for index in range(1, fold):
+            parts.append(pltpu.roll(tail, TILE - index * rest, axis=0))
+        tiles.append(jnp.concatenate(parts, axis=1).astype(ref.dtype))
+    return tiles
+
+
+def stacked(count, width, refs):
+    tiles = [tile for ref in refs for tile in unpacked(count, width, ref)]
+    return jnp.concatenate(tiles, axis=0)
 
 
 def pick(cap, table, picks, x, blocks, sel_ref, experts):
@@ -121,26 +171,27 @@
     lane = batch_of(lax.broadcasted_iota(jnp.int32, (SQUARE * high, count), 1))
     sel = ((target == (peer ^ chip)) & (position == left) & (group == lane)).astype(jnp.bfloat16)
     sel_ref[...] = sel
-    meta_row = lax.broadcasted_iota(jnp.int32, (high, LANES), 0) == batches * cap
-    meta_lane = lax.broadcasted_iota(jnp.int32, (high, LANES), 1)
+    meta_lane = lax.broadcasted_iota(jnp.int32, (TILE, LANES), 1)
     x = x()
     for q in range(SQUARE):
         part = jnp.dot(sel[q * high : (q + 1) * high], x, preferred_element_type=jnp.float32)
-        meta = jnp.zeros((high, LANES), jnp.float32)
+        meta = jnp.zeros((TILE, LANES), jnp.float32)
         for core in range(2):
             at = 2 * q + core
             hits = (ids == table[1:2, at : at + 1]) & (reps == table[2:3, at : at + 1])
             load = jnp.sum(hits.astype(jnp.float32), axis=1, keepdims=True)
-            meta = jnp.where(meta_row & (meta_lane == core), load, meta)
-        blocks[q][...] = part.astype(jnp.bfloat16)
-        blocks[q][:, :LANES] = (part[:, :LANES] + meta).astype(jnp.bfloat16)
+            meta = jnp.where(meta_lane == core, load, meta)
+        packed(batches * cap, part, blocks[q])
+        blocks[q][:, blocks[q].shape[1] - LANES :] = meta.astype(jnp.bfloat16)
 
 
 def pick_own_kernel(cap, home_hbm, new_hbm, x_hbm, ids_hbm, reps_hbm, *refs):
+    panels_hbm, refs = refs[:PANELS], refs[PANELS:]
     blocks, (sel_ref, table_ref, picks_ref, zero_ref) = refs[:SQUARE], refs[SQUARE : SQUARE + 4]
-    home_ref, new_ref, x_ref, ids_ref, reps_ref, sem = refs[SQUARE + 4 :]
-    sources = (home_hbm, new_hbm, ids_hbm, reps_hbm, x_hbm)
-    targets = (home_ref, new_ref, ids_ref, reps_ref, x_ref)
+    panels, refs = refs[SQUARE + 4 : SQUARE + 4 + PANELS], refs[SQUARE + 4 + PANELS :]
+    home_ref, new_ref, x_ref, ids_ref, reps_ref, sem = refs
+    sources = (home_hbm, new_hbm, ids_hbm, reps_hbm, x_hbm, *panels_hbm)
+    targets = (home_ref, new_ref, ids_ref, reps_ref, x_ref, *panels)
     copies = [
         pltpu.make_async_copy(source, target, sem.at[index])
         for index, (source, target) in enumerate(zip(sources, targets))
@@ -151,7 +202,7 @@
     chip = lax.axis_index("expert") // 2
     slots = new_ref.shape[0]
     experts = home_ref.shape[0]
-    for copy in copies[:-1]:
+    for copy in copies[:4]:
         copy.wait()
     picks = jnp.concatenate([ids_ref[...], reps_ref[...]], axis=0)
     picks_ref[...] = picks
@@ -171,10 +222,12 @@
     table_ref[...] = table
 
     def rows():
-        copies[-1].wait()
+        copies[4].wait()
         return x_ref[...]
 
     pick(cap, table, picks, rows, blocks, sel_ref, experts)
+    for copy in copies[5:]:
+        copy.wait()
 
 
 def pick_far_kernel(cap, experts, table_ref, x_ref, picks_ref, *refs):
@@ -185,7 +238,8 @@
 def pick_shapes(cap, x, batches):
     high = block_rows(batches, cap)
     count, width = x.shape
-    block = jax.ShapeDtypeStruct((high, width), jnp.bfloat16)
+    lanes = block_lanes(batches * cap, width) + LANES
+    block = jax.ShapeDtypeStruct((TILE, lanes), jnp.bfloat16)
     sel = jax.ShapeDtypeStruct((SQUARE * high, count), jnp.bfloat16)
     cost = pl.CostEstimate(
         flops=2 * SQUARE * high * count * width,
@@ -195,7 +249,7 @@
     return [block] * SQUARE + [sel], cost
 
 
-def pick_own(cap, home, new, x, ids, reps):
+def pick_own(cap, home, new, x, ids, reps, panels):
     batches, tokens = ids.shape
     shapes, cost = pick_shapes(cap, x, batches)
     shapes += [
@@ -203,10 +257,11 @@
         jax.ShapeDtypeStruct((2 * batches, tokens), jnp.int32),
         jax.ShapeDtypeStruct((8, LANES), jnp.float32),
     ]
+    shapes += [jax.ShapeDtypeStruct(panel.shape, panel.dtype) for panel in panels]
     return pl.pallas_call(
         functools.partial(pick_own_kernel, cap),
         out_shape=shapes,
-        in_specs=[pl.BlockSpec(memory_space=HBM)] * 5,
+        in_specs=[pl.BlockSpec(memory_space=HBM)] * (5 + len(panels)),
         out_specs=[pl.BlockSpec(memory_space=VMEM)] * len(shapes),
         scratch_shapes=[
             SMEM(home.shape, jnp.int32),
@@ -214,11 +269,11 @@
             VMEM(x.shape, x.dtype),
             VMEM(ids.shape, ids.dtype),
             VMEM(reps.shape, reps.dtype),
-            pltpu.SemaphoreType.DMA((5,)),
+            pltpu.SemaphoreType.DMA((5 + len(panels),)),
         ],
         cost_estimate=cost,
-        compiler_params=pltpu.CompilerParams(vmem_limit_bytes=SMALL),
-    )(*(pltpu.with_memory_space_constraint(value, HBM) for value in (home, new, x, ids, reps)))
+        compiler_params=pltpu.CompilerParams(vmem_limit_bytes=LARGE),
+    )(*(pltpu.with_memory_space_constraint(value, HBM) for value in (home, new, x, ids, reps, *panels)))
 
 
 def pick_far(cap, experts, table, x, picks):
@@ -261,16 +316,15 @@
     )(*(pltpu.with_memory_space_constraint(value, HBM) for value in values))
 
 
-def expert_kernel(meta, *refs):
+def expert_kernel(count, *refs):
     blocks, panels, prior_ref = refs[:SQUARE], refs[SQUARE : SQUARE + 6], refs[SQUARE + 6]
     outs, load_ref = refs[SQUARE + 7 : 2 * SQUARE + 7], refs[2 * SQUARE + 7]
-    high = blocks[0].shape[0]
-    x = jnp.concatenate([block[...] for block in blocks], axis=0)
+    x = stacked(count, panels[0].shape[1], blocks)
+    high = x.shape[0] // SQUARE
     contract = (((1,), (1,)), ((), ()))
-    start = meta - meta % 8
     load = prior_ref[...]
     for block in blocks:
-        load = load + block[start : start + 8, :LANES].astype(jnp.float32)
+        load = load + block[:, block.shape[1] - LANES :].astype(jnp.float32)
     load_ref[...] = load
     total = None
     for gate_ref, up_ref, down_ref in (panels[:3], panels[3:]):
@@ -279,18 +333,17 @@
         hidden = (gate / (1.0 + jnp.exp(-gate)) * up).astype(jnp.bfloat16)
         part = lax.dot_general(hidden, down_ref[0], contract, preferred_element_type=jnp.float32)
         total = part if total is None else total + part
-    total = total.astype(jnp.bfloat16)
     for q in range(SQUARE):
-        outs[q][...] = total[q * high : (q + 1) * high]
-
-
-def run_expert(meta, blocks, panels, panels_far, prior):
-    high, width = blocks[0].shape
-    half = panels[0].shape[2]
-    rows = SQUARE * high
+        packed(count, total[q * high : (q + 1) * high], outs[q])
+
+
+def run_expert(count, blocks, panels, panels_far, prior):
+    width, half = panels[0].shape[1:]
+    rows = SQUARE * count
+    block = jax.ShapeDtypeStruct((TILE, block_lanes(count, width)), jnp.bfloat16)
     return pl.pallas_call(
-        functools.partial(expert_kernel, meta),
-        out_shape=[jax.ShapeDtypeStruct((high, width), jnp.bfloat16)] * SQUARE
+        functools.partial(expert_kernel, count),
+        out_shape=[block] * SQUARE
         + [jax.ShapeDtypeStruct(prior.shape, prior.dtype)],
         in_specs=[pl.BlockSpec(memory_space=VMEM)] * (SQUARE + 7),
         out_specs=[pl.BlockSpec(memory_space=VMEM)] * (SQUARE + 1),
@@ -303,20 +356,22 @@
     )(*blocks, *panels, *panels_far, prior)
 
 
-def chosen(sel_ref, blocks):
-    y = jnp.concatenate([block[...] for block in blocks], axis=0)
+def chosen(count, width, sel_ref, blocks):
+    y = stacked(count, width, blocks)
     return lax.dot_general(
         sel_ref[...], y, (((0,), (0,)), ((), ())), preferred_element_type=jnp.float32
     )
 
 
-def merge_kernel(sel_ref, *refs):
-    refs[SQUARE][...] = chosen(sel_ref, refs[:SQUARE]).astype(jnp.bfloat16)
-
-
-def merge_own_kernel(sel_ref, weight_ref, *refs):
+def merge_kernel(count, sel_ref, *refs):
+    width = refs[SQUARE].shape[1]
+    refs[SQUARE][...] = chosen(count, width, sel_ref, refs[:SQUARE]).astype(jnp.bfloat16)
+
+
+def merge_own_kernel(count, sel_ref, weight_ref, *refs):
     out_ref, scale_ref = refs[SQUARE:]
-    out_ref[...] = chosen(sel_ref, refs[:SQUARE]).astype(jnp.bfloat16)
+    width = out_ref.shape[1]
+    out_ref[...] = chosen(count, width, sel_ref, refs[:SQUARE]).astype(jnp.bfloat16)
     batches, tokens = weight_ref.shape
     lane = lax.broadcasted_iota(jnp.int32, (tokens, tokens), 0)
     same = lane == lax.broadcasted_iota(jnp.int32, (tokens, tokens), 1)
@@ -328,12 +383,12 @@
         )
 
 
-def final_kernel(meta, own_ref, scale_ref, load_ref, load_far_ref, back_ref, out_ref, slot_ref):
+def final_kernel(own_ref, scale_ref, load_ref, load_far_ref, back_ref, out_ref, slot_ref):
     core = lax.axis_index("expert") % 2
     both = load_ref[...] + load_far_ref[...]
     row = lax.broadcasted_iota(jnp.int32, both.shape, 0)
     lane = lax.broadcasted_iota(jnp.int32, both.shape, 1)
-    slot_ref[0] = jnp.sum(jnp.where((row == meta % 8) & (lane == core), both, 0.0)).astype(
+    slot_ref[0] = jnp.sum(jnp.where((row == 0) & (lane == core), both, 0.0)).astype(
         jnp.int32
     )
     total = own_ref[...].astype(jnp.float32) + back_ref[...].astype(jnp.float32)
@@ -378,7 +433,7 @@
     batches, tokens, width = activations.shape
     rows = batches * tokens
     cap = min(CAP * REPL, tokens)
-    meta = batches * cap
+    count = batches * cap
     distant = 2 * SQUARE
 
     def swap(value, bits):
@@ -391,37 +446,38 @@
     x_far = swap(x, distant)
     panels = (gate_panel, up_panel, down_panel)
     panels_far = [swap(panel, 1) for panel in panels]
-    *blocks, sel, table, picks, zero = pick_own(
+    *blocks, sel, table, picks, zero, gate_own, up_own = pick_own(
         cap,
         old_home,
         new_expert,
         x,
         expert_ids.reshape(batches, tokens),
         replica.reshape(batches, tokens),
+        panels[:PANELS],
     )
     picks_far = swap(picks, distant)
     blocks = around(blocks)
     *blocks_far, sel_far = pick_far(cap, old_home.shape[0], table, x_far, picks_far)
     blocks_far = around(blocks_far)
-    panels = fetched(panels)
-    *results, load = run_expert(meta, blocks, panels, panels_far, zero)
-    *results_far, load = run_expert(meta, blocks_far, panels, panels_far, load)
+    panels = (gate_own, up_own, *fetched(panels[PANELS:]))
+    *results, load = run_expert(count, blocks, panels, panels_far, zero)
+    *results_far, load = run_expert(count, blocks_far, panels, panels_far, load)
     results_far = around(results_far)
     results = around(results)
     load_far = swap(load, 1)
     whole = jax.ShapeDtypeStruct((rows, width), jnp.bfloat16)
-    (far,) = small_call(merge_kernel, [whole], sel_far, *results_far)
+    (far,) = small_call(functools.partial(merge_kernel, count), [whole], sel_far, *results_far)
     back = swap(far, distant)
     weight = pick_weight.reshape(batches, tokens)
     own, scale = small_call(
-        merge_own_kernel,
+        functools.partial(merge_own_kernel, count),
         [whole, jax.ShapeDtypeStruct((rows, LANES), jnp.float32)],
         sel,
         weight,
         *results,
     )
     output, slot_load = small_call(
-        functools.partial(final_kernel, meta),
+        final_kernel,
         [whole],
         own,
         scale,

time: 54.1 us -> 52.4 us (0.969)
  starting transfers between devices: 24.3 us -> 23.1 us
    ppermute x19, starting transfers between devices: 24.3 us -> 23.1 us  [swap(): return lax.ppermute(value, 'expert', swapped(size, bits))]
    pallas_call x1, Pallas kernels: 2.38 us -> 1.42 us  [fetched(): pl.pallas_call(fetch_kernel, out_shape=[jax.ShapeDtypeStruct(value.shape,...]
    pallas_call x1, Pallas kernels: 1.47 us -> 2.05 us  [pick_own(): pl.pallas_call(functools.partial(pick_own_kernel, cap), out_shape=shapes,...]
  transfers between devices with their start and end apart: 19 -> 19, of which waited for: 10 -> 10; matrix products, arithmetic and copies ran while one was open for 0% -> 0% of each run, Pallas kernels for 13% -> 12%
where the time goes in v4:
time: 52.4 us; the launch traced here: 52.3 us
  starting transfers between devices  23.1 us (44%)
  waiting for transfers between devices  18.7 us (36%)
  Pallas kernels  9.64 us (18%)
  between operations  0.75 us (1%)
    ppermute x19, starting transfers between devices, swap(): return lax.ppermute(value, 'expert', swapped(size, bits))  23.1 us
    ppermute x19, waiting for transfers between devices, swap(): return lax.ppermute(value, 'expert', swapped(size, bits))  18.7 us
    pallas_call x2, Pallas kernels, run_expert(): pl.pallas_call(functools.partial(expert_kernel, count), out_shape=[block]...  4.43 us
    pallas_call x1, Pallas kernels, pick_own(): pl.pallas_call(functools.partial(pick_own_kernel, cap), out_shape=shapes,...  2.05 us
    pallas_call x1, Pallas kernels, fetched(): pl.pallas_call(fetch_kernel, out_shape=[jax.ShapeDtypeStruct(value.shape,...  1.42 us
    pallas_call x3, Pallas kernels, small_call(): pl.pallas_call(kernel, out_shape=shapes, in_specs=[pl.BlockSpec(memory_sp...  1.21 us
  transfers between devices with their start and end apart: 19, of which 10 were waited for; matrix products, arithmetic and copies ran while one was open for 0% of the time, Pallas kernels for 12%

profile of v4, /device:TPU:0, one launch (start us, length us, event | category | flops | bytes accessed | tf_op | source)
XLA Modules:
  0.0 52.3 jit_solution(4964138601750660779)
XLA Ops:
  0.6 0.6 %collective-permute-start.3 = (bf16[1,2048,384]{2,1,0:T(8,128)(2,1)}, bf16[1,2048,384]{2,1,0:T(8,128)(2,1)S(1)}, u32[]{:S(2)}, u32[]{:S(2)}) collective-permute-start(bf16[1,2048,384]{2,1,0:T(8,128)(2,1)} %refs_0_.2), channel_id=1, source_target_pairs={{0,1},{1,0},{2,3},{3,2},{4,5},{5,4},{6,7},{7,6},{8,9},{9,8},{10,11... | collective-permute-start | bytes 4718600 | tf_op jit(solution)/shard_map/ppermute | solution.py:440
  1.3 0.4 collective-permute-start.5
  1.7 3.6 %collective-permute-start.9 = (bf16[32,2048]{1,0:T(8,128)(2,1)}, bf16[32,2048]{1,0:T(8,128)(2,1)S(1)}, u32[]{:S(2)}, u32[]{:S(2)}) collective-permute-start(bf16[32,2048]{1,0:T(8,128)(2,1)} %bitcast.6), channel_id=1, source_target_pairs={{0,8},{1,9},{2,10},{3,11},{4,12},{5,13},{6,14},{7,15},{8,0},{9,1},... | collective-permute-start | bytes 393224 | tf_op jit(solution)/shard_map/ppermute | solution.py:440
  5.4 2.1 %shard_map.104 = (bf16[8,5248]{1,0:T(8,128)(2,1)S(1)}, bf16[8,5248]{1,0:T(8,128)(2,1)S(1)}, bf16[8,5248]{1,0:T(8,128)(2,1)S(1)}, bf16[8,5248]{1,0:T(8,128)(2,1)S...) custom-call(s32[8]{0:T(128)} %home_hbm.1, ...), custom_call_target="tpu_custom_call" | custom-call | flops 12582912 | bytes 786432 | tf_op jit(solution)/shard_map/pallas_call | solution.py:261
  7.5 5.0 %collective-permute-done.10.picks_ref = s32[4,16]{1,0:T(4,128)S(1)} collective-permute-done((s32[4,16]{1,0:T(4,128)S(1)}, s32[4,16]{1,0:T(4,128)S(1)}, u32[]{:S(2)}, u32[]{:S(2)}) %collective-permute-start.10) | collective-permute-done | bytes 288 | tf_op jit(solution)/shard_map/ppermute | solution.py:440
  12.5 1.5 %collective-permute-start = (bf16[8,5248]{1,0:T(8,128)(2,1)S(1)}, bf16[8,5248]{1,0:T(8,128)(2,1)S(1)}, u32[]{:S(2)}, u32[]{:S(2)}) collective-permute-start(bf16[8,5248]{1,0:T(8,128)(2,1)S(1)} %get-tuple-element.33), channel_id=1, source_target_pairs={{0,2},{1,3},{2,0},{3,1},{4,6},{5,7},{6,4},{7,5},{8,10},{9,11},{10,... | collective-permute-start | bytes 251912 | tf_op jit(solution)/shard_map/ppermute | solution.py:440
  14.1 2.9 %collective-permute-done.refs_1_ = bf16[8,5248]{1,0:T(8,128)(2,1)S(1)} collective-permute-done((bf16[8,5248]{1,0:T(8,128)(2,1)S(1)}, bf16[8,5248]{1,0:T(8,128)(2,1)S(1)}, u32[]{:S(2)}, u32[]{:S(2)}) %collective-permute-start) | collective-permute-done | bytes 84000 | tf_op jit(solution)/shard_map/ppermute | solution.py:440
  17.0 1.0 %collective-permute-start.1 = (bf16[8,5248]{1,0:T(8,128)(2,1)S(1)}, bf16[8,5248]{1,0:T(8,128)(2,1)S(1)}, u32[]{:S(2)}, u32[]{:S(2)}) collective-permute-start(bf16[8,5248]{1,0:T(8,128)(2,1)S(1)} %get-tuple-element.34), channel_id=1, source_target_pairs={{0,4},{1,5},{2,6},{3,7},{4,0},{5,1},{6,2},{7,3},{8,12},{9,13},{10,... | collective-permute-start | bytes 251912 | tf_op jit(solution)/shard_map/ppermute | solution.py:440
  18.0 2.0 %collective-permute-start.2 = (bf16[8,5248]{1,0:T(8,128)(2,1)S(1)}, bf16[8,5248]{1,0:T(8,128)(2,1)S(1)}, u32[]{:S(2)}, u32[]{:S(2)}) collective-permute-start(bf16[8,5248]{1,0:T(8,128)(2,1)S(1)} %get-tuple-element.35), channel_id=1, source_target_pairs={{0,6},{1,7},{2,4},{3,5},{4,2},{5,3},{6,0},{7,1},{8,14},{9,15},{10,... | collective-permute-start | bytes 251912 | tf_op jit(solution)/shard_map/ppermute | solution.py:440
  20.0 0.5 %shard_map.108 = (bf16[8,5248]{1,0:T(8,128)(2,1)S(1)}, bf16[8,5248]{1,0:T(8,128)(2,1)S(1)}, bf16[8,5248]{1,0:T(8,128)(2,1)S(1)}, bf16[8,5248]{1,0:T(8,128)(2,1)S(1)}, bf16[96,32]{1,0:T(8,128)(2,1)S(1)}) custom-call(s32[8,128]{1,0:T(8,128)S(1)} %get-tuple-element.45.table_ref, bf16[32,2048]{1,0:T(8,128)(2,1)S(1)} %collective-permute-done.9.x_ref, ...), custom_call_target="tpu_custom_call" | custom-call | flops 12582912 | bytes 786432 | tf_op jit(solution)/shard_map/pallas_call | solution.py:281
  20.5 1.2 %collective-permute-done.1.refs_2_ = bf16[8,5248]{1,0:T(8,128)(2,1)S(1)} collective-permute-done((bf16[8,5248]{1,0:T(8,128)(2,1)S(1)}, bf16[8,5248]{1,0:T(8,128)(2,1)S(1)}, u32[]{:S(2)}, u32[]{:S(2)}) %collective-permute-start.1) | collective-permute-done | bytes 84000 | tf_op jit(solution)/shard_map/ppermute | solution.py:440
  21.8 1.2 %collective-permute-start.11 = (bf16[8,5248]{1,0:T(8,128)(2,1)S(1)}, bf16[8,5248]{1,0:T(8,128)(2,1)S(1)}, u32[]{:S(2)}, u32[]{:S(2)}) collective-permute-start(bf16[8,5248]{1,0:T(8,128)(2,1)S(1)} %get-tuple-element.48), channel_id=1, source_target_pairs={{0,2},{1,3},{2,0},{3,1},{4,6},{5,7},{6,4},{7,5},{8,10},{9,11},{10,... | collective-permute-start | bytes 251912 | tf_op jit(solution)/shard_map/ppermute | solution.py:440
  23.0 0.4 collective-permute-done.2.refs_3_
  23.4 1.0 %collective-permute-start.12 = (bf16[8,5248]{1,0:T(8,128)(2,1)S(1)}, bf16[8,5248]{1,0:T(8,128)(2,1)S(1)}, u32[]{:S(2)}, u32[]{:S(2)}) collective-permute-start(bf16[8,5248]{1,0:T(8,128)(2,1)S(1)} %get-tuple-element.49), channel_id=1, source_target_pairs={{0,4},{1,5},{2,6},{3,7},{4,0},{5,1},{6,2},{7,3},{8,12},{9,13},{10,... | collective-permute-start | bytes 251912 | tf_op jit(solution)/shard_map/ppermute | solution.py:440
  24.4 2.0 %collective-permute-start.13 = (bf16[8,5248]{1,0:T(8,128)(2,1)S(1)}, bf16[8,5248]{1,0:T(8,128)(2,1)S(1)}, u32[]{:S(2)}, u32[]{:S(2)}) collective-permute-start(bf16[8,5248]{1,0:T(8,128)(2,1)S(1)} %get-tuple-element.50), channel_id=1, source_target_pairs={{0,6},{1,7},{2,4},{3,5},{4,2},{5,3},{6,0},{7,1},{8,14},{9,15},{10,... | collective-permute-start | bytes 251912 | tf_op jit(solution)/shard_map/ppermute | solution.py:440
  26.5 1.4 %shard_map.105.refs_6_ = bf16[1,2048,384]{2,1,0:T(8,128)(2,1)S(1)} custom-call(bf16[1,2048,384]{2,1,0:T(8,128)(2,1)} %refs_0_.3), custom_call_target="tpu_custom_call" | custom-call | bytes 3145728 | tf_op jit(solution)/shard_map/pallas_call | solution.py:306
  27.9 2.2 %shard_map.106 = (bf16[8,5120]{1,0:T(8,128)(2,1)S(1)}, bf16[8,5120]{1,0:T(8,128)(2,1)S(1)}, bf16[8,5120]{1,0:T(8,128)(2,1)S(1)}, bf16[8,5120]{1,0:T(8,128)(2,1)S(1)}, f32[8,128]{1,0:T(8,128)S(1)}) custom-call(bf16[8,5248]{1,0:T(8,128)(2,1)S(1)} %get-tuple-element.32.refs_0_, bf16[8,5248]{1,0:T(8,128)(2,1)S(1)} %collective-permute-done.refs_1_, ...), custom_call_target="tpu_custom_call" | custom-call | flops 754974720 | bytes 10092544 | tf_op jit(solution)/shard_map/pallas_call | solution.py:344
  30.2 2.2 %shard_map.109 = (bf16[8,5120]{1,0:T(8,128)(2,1)S(1)}, bf16[8,5120]{1,0:T(8,128)(2,1)S(1)}, bf16[8,5120]{1,0:T(8,128)(2,1)S(1)}, bf16[8,5120]{1,0:T(8,128)(2,1)S(1)}, f32[8,128]{1,0:T(8,128)S(1)}) custom-call(bf16[8,5248]{1,0:T(8,128)(2,1)S(1)} %get-tuple-element.47.refs_0_, bf16[8,5248]{1,0:T(8,128)(2,1)S(1)} %collective-permute-done.11.refs_1_, ...), custom_call_target="tpu_custom_call" | custom-call | flops 754974720 | bytes 10092544 | tf_op jit(solution)/shard_map/pallas_call | solution.py:344
  32.4 1.2 %collective-permute-start.15 = (bf16[8,5120]{1,0:T(8,128)(2,1)S(1)}, bf16[8,5120]{1,0:T(8,128)(2,1)S(1)}, u32[]{:S(2)}, u32[]{:S(2)}) collective-permute-start(bf16[8,5120]{1,0:T(8,128)(2,1)S(1)} %get-tuple-element.55), channel_id=1, source_target_pairs={{0,2},{1,3},{2,0},{3,1},{4,6},{5,7},{6,4},{7,5},{8,10},{9,11},{10,... | collective-permute-start | bytes 245768 | tf_op jit(solution)/shard_map/ppermute | solution.py:440
  33.6 1.1 %collective-permute-start.16 = (bf16[8,5120]{1,0:T(8,128)(2,1)S(1)}, bf16[8,5120]{1,0:T(8,128)(2,1)S(1)}, u32[]{:S(2)}, u32[]{:S(2)}) collective-permute-start(bf16[8,5120]{1,0:T(8,128)(2,1)S(1)} %get-tuple-element.56), channel_id=1, source_target_pairs={{0,4},{1,5},{2,6},{3,7},{4,0},{5,1},{6,2},{7,3},{8,12},{9,13},{10,... | collective-permute-start | bytes 245768 | tf_op jit(solution)/shard_map/ppermute | solution.py:440
  34.7 1.3 %collective-permute-start.17 = (bf16[8,5120]{1,0:T(8,128)(2,1)S(1)}, bf16[8,5120]{1,0:T(8,128)(2,1)S(1)}, u32[]{:S(2)}, u32[]{:S(2)}) collective-permute-start(bf16[8,5120]{1,0:T(8,128)(2,1)S(1)} %get-tuple-element.57), channel_id=1, source_target_pairs={{0,6},{1,7},{2,4},{3,5},{4,2},{5,3},{6,0},{7,1},{8,14},{9,15},{10,... | collective-permute-start | bytes 245768 | tf_op jit(solution)/shard_map/ppermute | solution.py:440
  36.0 1.0 %collective-permute-done.15.refs_1_ = bf16[8,5120]{1,0:T(8,128)(2,1)S(1)} collective-permute-done((bf16[8,5120]{1,0:T(8,128)(2,1)S(1)}, bf16[8,5120]{1,0:T(8,128)(2,1)S(1)}, u32[]{:S(2)}, u32[]{:S(2)}) %collective-permute-start.15) | collective-permute-done | bytes 81952 | tf_op jit(solution)/shard_map/ppermute | solution.py:440
  36.9 1.1 %collective-permute-done.16.refs_2_ = bf16[8,5120]{1,0:T(8,128)(2,1)S(1)} collective-permute-done((bf16[8,5120]{1,0:T(8,128)(2,1)S(1)}, bf16[8,5120]{1,0:T(8,128)(2,1)S(1)}, u32[]{:S(2)}, u32[]{:S(2)}) %collective-permute-start.16) | collective-permute-done | bytes 81952 | tf_op jit(solution)/shard_map/ppermute | solution.py:440
  38.0 3.4 %collective-permute-done.17.refs_3_ = bf16[8,5120]{1,0:T(8,128)(2,1)S(1)} collective-permute-done((bf16[8,5120]{1,0:T(8,128)(2,1)S(1)}, bf16[8,5120]{1,0:T(8,128)(2,1)S(1)}, u32[]{:S(2)}, u32[]{:S(2)}) %collective-permute-start.17) | collective-permute-done | bytes 81952 | tf_op jit(solution)/shard_map/ppermute | solution.py:440
  41.7 2.5 %collective-permute-start.18 = (bf16[32,2048]{1,0:T(8,128)(2,1)S(1)}, bf16[32,2048]{1,0:T(8,128)(2,1)S(1)}, u32[]{:S(2)}, u32[]{:S(2)}) collective-permute-start(bf16[32,2048]{1,0:T(8,128)(2,1)S(1)} %shard_map.110), channel_id=1, source_target_pairs={{0,8},{1,9},{2,10},{3,11},{4,12},{5,13},{6,14},{7,15},{8,0},{9,1},... | collective-permute-start | bytes 393224 | tf_op jit(solution)/shard_map/ppermute | solution.py:440
  44.1 0.5 %collective-permute-start.6 = (bf16[8,5120]{1,0:T(8,128)(2,1)S(1)}, bf16[8,5120]{1,0:T(8,128)(2,1)S(1)}, u32[]{:S(2)}, u32[]{:S(2)}) collective-permute-start(bf16[8,5120]{1,0:T(8,128)(2,1)S(1)} %get-tuple-element.40), channel_id=1, source_target_pairs={{0,2},{1,3},{2,0},{3,1},{4,6},{5,7},{6,4},{7,5},{8,10},{9,11},{10,... | collective-permute-start | bytes 245768 | tf_op jit(solution)/shard_map/ppermute | solution.py:440
  44.7 1.2 %collective-permute-start.7 = (bf16[8,5120]{1,0:T(8,128)(2,1)S(1)}, bf16[8,5120]{1,0:T(8,128)(2,1)S(1)}, u32[]{:S(2)}, u32[]{:S(2)}) collective-permute-start(bf16[8,5120]{1,0:T(8,128)(2,1)S(1)} %get-tuple-element.41), channel_id=1, source_target_pairs={{0,4},{1,5},{2,6},{3,7},{4,0},{5,1},{6,2},{7,3},{8,12},{9,13},{10,... | collective-permute-start | bytes 245768 | tf_op jit(solution)/shard_map/ppermute | solution.py:440
  45.9 1.7 %collective-permute-start.8 = (bf16[8,5120]{1,0:T(8,128)(2,1)S(1)}, bf16[8,5120]{1,0:T(8,128)(2,1)S(1)}, u32[]{:S(2)}, u32[]{:S(2)}) collective-permute-start(bf16[8,5120]{1,0:T(8,128)(2,1)S(1)} %get-tuple-element.42), channel_id=1, source_target_pairs={{0,6},{1,7},{2,4},{3,5},{4,2},{5,3},{6,0},{7,1},{8,14},{9,15},{10,... | collective-permute-start | bytes 245768 | tf_op jit(solution)/shard_map/ppermute | solution.py:440
  47.6 0.9 %collective-permute-done.6.refs_1_ = bf16[8,5120]{1,0:T(8,128)(2,1)S(1)} collective-permute-done((bf16[8,5120]{1,0:T(8,128)(2,1)S(1)}, bf16[8,5120]{1,0:T(8,128)(2,1)S(1)}, u32[]{:S(2)}, u32[]{:S(2)}) %collective-permute-start.6) | collective-permute-done | bytes 81952 | tf_op jit(solution)/shard_map/ppermute | solution.py:440
  48.6 0.5 %collective-permute-done.7.refs_2_ = bf16[8,5120]{1,0:T(8,128)(2,1)S(1)} collective-permute-done((bf16[8,5120]{1,0:T(8,128)(2,1)S(1)}, bf16[8,5120]{1,0:T(8,128)(2,1)S(1)}, u32[]{:S(2)}, u32[]{:S(2)}) %collective-permute-start.7) | collective-permute-done | bytes 81952 | tf_op jit(solution)/shard_map/ppermute | solution.py:440
  49.1 2.1 %collective-permute-done.8.refs_3_ = bf16[8,5120]{1,0:T(8,128)(2,1)S(1)} collective-permute-done((bf16[8,5120]{1,0:T(8,128)(2,1)S(1)}, bf16[8,5120]{1,0:T(8,128)(2,1)S(1)}, u32[]{:S(2)}, u32[]{:S(2)}) %collective-permute-start.8) | collective-permute-done | bytes 81952 | tf_op jit(solution)/shard_map/ppermute | solution.py:440
  51.5 0.8 %shard_map.111 = (bf16[32,2048]{1,0:T(8,128)(2,1)}, s32[1]{0:T(128)}) custom-call(bf16[32,2048]{1,0:T(8,128)(2,1)S(1)} %get-tuple-element.43.own_ref, f32[32,128]{1,0:T(8,128)S(1)} %get-tuple-element.44.scale_ref, f32[8,128]{1,0:T(8,128)S(1)} %get-tuple-element.52.load_ref, f32[8,128]{1,0:T(8,128)S(1)} %collective-permute-done.14.load_far_ref, ...), custom_call_target="tpu_custom_call" | custom-call | flops 16777472 | bytes 274432 | tf_op jit(solution)/shard_map/pallas_call | solution.py:403
  (16 shorter events, 0.6 us)
Async XLA Ops:
  0.6 23.8 %collective-permute-start.3 = (bf16[1,2048,384]{2,1,0:T(8,128)(2,1)}, bf16[1,2048,384]{2,1,0:T(8,128)(2,1)S(1)}, u32[]{:S(2)}, u32[]{:S(2)}) collective-permute-start(bf16[1,2048,384]{2,1,0:T(8,128)(2,1)} %refs_0_.2), channel_id=1, source_target_pairs={{0,1},{1,0},{2,3},{3,2},{4,5},{5,4},{6,7},{7,6},{8,9},{9,8},{10,11... | collective-permute-start | bytes 4718600 | tf_op jit(solution)/shard_map/ppermute | solution.py:440
  1.2 26.7 %collective-permute-start.4 = (bf16[1,2048,384]{2,1,0:T(8,128)(2,1)}, bf16[1,2048,384]{2,1,0:T(8,128)(2,1)S(1)}, u32[]{:S(2)}, u32[]{:S(2)}) collective-permute-start(bf16[1,2048,384]{2,1,0:T(8,128)(2,1)} %refs_1_.1), channel_id=1, source_target_pairs={{0,1},{1,0},{2,3},{3,2},{4,5},{5,4},{6,7},{7,6},{8,9},{9,8},{10,11... | collective-permute-start | bytes 4718600 | tf_op jit(solution)/shard_map/ppermute | solution.py:440
  1.3 26.6 %collective-permute-start.5 = (bf16[1,2048,384]{2,1,0:T(8,128)(2,1)}, bf16[1,2048,384]{2,1,0:T(8,128)(2,1)S(1)}, u32[]{:S(2)}, u32[]{:S(2)}) collective-permute-start(bf16[1,2048,384]{2,1,0:T(8,128)(2,1)} %refs_0_.3), channel_id=1, source_target_pairs={{0,1},{1,0},{2,3},{3,2},{4,5},{5,4},{6,7},{7,6},{8,9},{9,8},{10,11... | collective-permute-start | bytes 4718600 | tf_op jit(solution)/shard_map/ppermute | solution.py:440
  1.7 16.3 %collective-permute-start.9 = (bf16[32,2048]{1,0:T(8,128)(2,1)}, bf16[32,2048]{1,0:T(8,128)(2,1)S(1)}, u32[]{:S(2)}, u32[]{:S(2)}) collective-permute-start(bf16[32,2048]{1,0:T(8,128)(2,1)} %bitcast.6), channel_id=1, source_target_pairs={{0,8},{1,9},{2,10},{3,11},{4,12},{5,13},{6,14},{7,15},{8,0},{9,1},... | collective-permute-start | bytes 393224 | tf_op jit(solution)/shard_map/ppermute | solution.py:440
  7.4 5.1 %collective-permute-start.10 = (s32[4,16]{1,0:T(4,128)S(1)}, s32[4,16]{1,0:T(4,128)S(1)}, u32[]{:S(2)}, u32[]{:S(2)}) collective-permute-start(s32[4,16]{1,0:T(4,128)S(1)} %get-tuple-element.46), channel_id=1, source_target_pairs={{0,8},{1,9},{2,10},{3,11},{4,12},{5,13},{6,14},{7,15},{8,0},{9,1},... | collective-permute-start | bytes 776 | tf_op jit(solution)/shard_map/ppermute | solution.py:440
  12.5 4.5 %collective-permute-start = (bf16[8,5248]{1,0:T(8,128)(2,1)S(1)}, bf16[8,5248]{1,0:T(8,128)(2,1)S(1)}, u32[]{:S(2)}, u32[]{:S(2)}) collective-permute-start(bf16[8,5248]{1,0:T(8,128)(2,1)S(1)} %get-tuple-element.33), channel_id=1, source_target_pairs={{0,2},{1,3},{2,0},{3,1},{4,6},{5,7},{6,4},{7,5},{8,10},{9,11},{10,... | collective-permute-start | bytes 251912 | tf_op jit(solution)/shard_map/ppermute | solution.py:440
  17.0 4.8 %collective-permute-start.1 = (bf16[8,5248]{1,0:T(8,128)(2,1)S(1)}, bf16[8,5248]{1,0:T(8,128)(2,1)S(1)}, u32[]{:S(2)}, u32[]{:S(2)}) collective-permute-start(bf16[8,5248]{1,0:T(8,128)(2,1)S(1)} %get-tuple-element.34), channel_id=1, source_target_pairs={{0,4},{1,5},{2,6},{3,7},{4,0},{5,1},{6,2},{7,3},{8,12},{9,13},{10,... | collective-permute-start | bytes 251912 | tf_op jit(solution)/shard_map/ppermute | solution.py:440
  18.0 5.4 %collective-permute-start.2 = (bf16[8,5248]{1,0:T(8,128)(2,1)S(1)}, bf16[8,5248]{1,0:T(8,128)(2,1)S(1)}, u32[]{:S(2)}, u32[]{:S(2)}) collective-permute-start(bf16[8,5248]{1,0:T(8,128)(2,1)S(1)} %get-tuple-element.35), channel_id=1, source_target_pairs={{0,6},{1,7},{2,4},{3,5},{4,2},{5,3},{6,0},{7,1},{8,14},{9,15},{10,... | collective-permute-start | bytes 251912 | tf_op jit(solution)/shard_map/ppermute | solution.py:440
  21.8 8.4 %collective-permute-start.11 = (bf16[8,5248]{1,0:T(8,128)(2,1)S(1)}, bf16[8,5248]{1,0:T(8,128)(2,1)S(1)}, u32[]{:S(2)}, u32[]{:S(2)}) collective-permute-start(bf16[8,5248]{1,0:T(8,128)(2,1)S(1)} %get-tuple-element.48), channel_id=1, source_target_pairs={{0,2},{1,3},{2,0},{3,1},{4,6},{5,7},{6,4},{7,5},{8,10},{9,11},{10,... | collective-permute-start | bytes 251912 | tf_op jit(solution)/shard_map/ppermute | solution.py:440
  23.4 6.8 %collective-permute-start.12 = (bf16[8,5248]{1,0:T(8,128)(2,1)S(1)}, bf16[8,5248]{1,0:T(8,128)(2,1)S(1)}, u32[]{:S(2)}, u32[]{:S(2)}) collective-permute-start(bf16[8,5248]{1,0:T(8,128)(2,1)S(1)} %get-tuple-element.49), channel_id=1, source_target_pairs={{0,4},{1,5},{2,6},{3,7},{4,0},{5,1},{6,2},{7,3},{8,12},{9,13},{10,... | collective-permute-start | bytes 251912 | tf_op jit(solution)/shard_map/ppermute | solution.py:440
  24.4 5.7 %collective-permute-start.13 = (bf16[8,5248]{1,0:T(8,128)(2,1)S(1)}, bf16[8,5248]{1,0:T(8,128)(2,1)S(1)}, u32[]{:S(2)}, u32[]{:S(2)}) collective-permute-start(bf16[8,5248]{1,0:T(8,128)(2,1)S(1)} %get-tuple-element.50), channel_id=1, source_target_pairs={{0,6},{1,7},{2,4},{3,5},{4,2},{5,3},{6,0},{7,1},{8,14},{9,15},{10,... | collective-permute-start | bytes 251912 | tf_op jit(solution)/shard_map/ppermute | solution.py:440
  30.2 21.1 %copy-start = (f32[2,16,1]{1,2,0:T(1,128)S(1)}, f32[2,16,1]{1,2,0:T(1,128)}, u32[]{:S(2)}) copy-start(f32[2,16,1]{1,2,0:T(1,128)} %param.10) | copy-start | bytes 388
  32.4 4.5 %collective-permute-start.15 = (bf16[8,5120]{1,0:T(8,128)(2,1)S(1)}, bf16[8,5120]{1,0:T(8,128)(2,1)S(1)}, u32[]{:S(2)}, u32[]{:S(2)}) collective-permute-start(bf16[8,5120]{1,0:T(8,128)(2,1)S(1)} %get-tuple-element.55), channel_id=1, source_target_pairs={{0,2},{1,3},{2,0},{3,1},{4,6},{5,7},{6,4},{7,5},{8,10},{9,11},{10,... | collective-permute-start | bytes 245768 | tf_op jit(solution)/shard_map/ppermute | solution.py:440
  33.6 4.4 %collective-permute-start.16 = (bf16[8,5120]{1,0:T(8,128)(2,1)S(1)}, bf16[8,5120]{1,0:T(8,128)(2,1)S(1)}, u32[]{:S(2)}, u32[]{:S(2)}) collective-permute-start(bf16[8,5120]{1,0:T(8,128)(2,1)S(1)} %get-tuple-element.56), channel_id=1, source_target_pairs={{0,4},{1,5},{2,6},{3,7},{4,0},{5,1},{6,2},{7,3},{8,12},{9,13},{10,... | collective-permute-start | bytes 245768 | tf_op jit(solution)/shard_map/ppermute | solution.py:440
  34.7 6.8 %collective-permute-start.17 = (bf16[8,5120]{1,0:T(8,128)(2,1)S(1)}, bf16[8,5120]{1,0:T(8,128)(2,1)S(1)}, u32[]{:S(2)}, u32[]{:S(2)}) collective-permute-start(bf16[8,5120]{1,0:T(8,128)(2,1)S(1)} %get-tuple-element.57), channel_id=1, source_target_pairs={{0,6},{1,7},{2,4},{3,5},{4,2},{5,3},{6,0},{7,1},{8,14},{9,15},{10,... | collective-permute-start | bytes 245768 | tf_op jit(solution)/shard_map/ppermute | solution.py:440
  41.7 9.8 %collective-permute-start.18 = (bf16[32,2048]{1,0:T(8,128)(2,1)S(1)}, bf16[32,2048]{1,0:T(8,128)(2,1)S(1)}, u32[]{:S(2)}, u32[]{:S(2)}) collective-permute-start(bf16[32,2048]{1,0:T(8,128)(2,1)S(1)} %shard_map.110), channel_id=1, source_target_pairs={{0,8},{1,9},{2,10},{3,11},{4,12},{5,13},{6,14},{7,15},{8,0},{9,1},... | collective-permute-start | bytes 393224 | tf_op jit(solution)/shard_map/ppermute | solution.py:440
  44.1 4.4 %collective-permute-start.6 = (bf16[8,5120]{1,0:T(8,128)(2,1)S(1)}, bf16[8,5120]{1,0:T(8,128)(2,1)S(1)}, u32[]{:S(2)}, u32[]{:S(2)}) collective-permute-start(bf16[8,5120]{1,0:T(8,128)(2,1)S(1)} %get-tuple-element.40), channel_id=1, source_target_pairs={{0,2},{1,3},{2,0},{3,1},{4,6},{5,7},{6,4},{7,5},{8,10},{9,11},{10,... | collective-permute-start | bytes 245768 | tf_op jit(solution)/shard_map/ppermute | solution.py:440
  44.7 4.4 %collective-permute-start.7 = (bf16[8,5120]{1,0:T(8,128)(2,1)S(1)}, bf16[8,5120]{1,0:T(8,128)(2,1)S(1)}, u32[]{:S(2)}, u32[]{:S(2)}) collective-permute-start(bf16[8,5120]{1,0:T(8,128)(2,1)S(1)} %get-tuple-element.41), channel_id=1, source_target_pairs={{0,4},{1,5},{2,6},{3,7},{4,0},{5,1},{6,2},{7,3},{8,12},{9,13},{10,... | collective-permute-start | bytes 245768 | tf_op jit(solution)/shard_map/ppermute | solution.py:440
  45.9 5.3 %collective-permute-start.8 = (bf16[8,5120]{1,0:T(8,128)(2,1)S(1)}, bf16[8,5120]{1,0:T(8,128)(2,1)S(1)}, u32[]{:S(2)}, u32[]{:S(2)}) collective-permute-start(bf16[8,5120]{1,0:T(8,128)(2,1)S(1)} %get-tuple-element.42), channel_id=1, source_target_pairs={{0,6},{1,7},{2,4},{3,5},{4,2},{5,3},{6,0},{7,1},{8,14},{9,15},{10,... | collective-permute-start | bytes 245768 | tf_op jit(solution)/shard_map/ppermute | solution.py:440
  47.6 3.9 %collective-permute-start.14 = (f32[8,128]{1,0:T(8,128)S(1)}, f32[8,128]{1,0:T(8,128)S(1)}, u32[]{:S(2)}, u32[]{:S(2)}) collective-permute-start(f32[8,128]{1,0:T(8,128)S(1)} %get-tuple-element.52.load_ref), channel_id=1, source_target_pairs={{0,1},{1,0},{2,3},{3,2},{4,5},{5,4},{6,7},{7,6},{8,9},{9,8},{10,11... | collective-permute-start | bytes 12296 | tf_op jit(solution)/shard_map/ppermute | solution.py:440

commit v5 on v4

--- a/solution.py
+++ b/solution.py
@@ -13,6 +13,7 @@
 LANES = 128
 SQUARE = 4
 TILE = 8
+PEERS = ((0, 1, 2, 3), (0, 3, 1, 2))
 PANELS = 2
 SMALL = 4 << 20
 LARGE = 20 << 20
@@ -74,6 +75,14 @@
     return whole
 
 
+def peer_of(slot, core):
+    value = jnp.zeros_like(slot)
+    for index in range(1, SQUARE):
+        peer = jnp.where(core == 0, PEERS[0][index], PEERS[1][index])
+        value = jnp.where(slot == index, peer, value)
+    return value
+
+
 def tiling(count):
     full, rest = divmod(count, TILE)
     fold = TILE // rest if rest and TILE % rest == 0 else 1
@@ -131,6 +140,7 @@
     count = batches * tokens
     high = block_rows(batches, cap)
     chip = lax.axis_index("expert") // 2
+    side = lax.axis_index("expert") % 2
 
     def batch_of(index):
         return steps(index, tokens, batches)
@@ -166,6 +176,7 @@
     row = lax.broadcasted_iota(jnp.int32, (SQUARE * high, count), 0)
     peer = steps(row, high, SQUARE)
     left = row - high * peer
+    peer = peer_of(peer, side)
     group = steps(left, cap, batches + 1)
     left = left - cap * group
     lane = batch_of(lax.broadcasted_iota(jnp.int32, (SQUARE * high, count), 1))
@@ -200,6 +211,7 @@
         copy.start()
     zero_ref[...] = jnp.zeros(zero_ref.shape, zero_ref.dtype)
     chip = lax.axis_index("expert") // 2
+    side = lax.axis_index("expert") % 2
     slots = new_ref.shape[0]
     experts = home_ref.shape[0]
     for copy in copies[:4]:
@@ -212,7 +224,7 @@
     for expert in range(experts):
         table = jnp.where((row == 0) & (lane == expert), home_ref[expert], table)
     for at in range(2 * SQUARE):
-        slot = 2 * (chip ^ (at // 2)) + at % 2
+        slot = 2 * (chip ^ peer_of(jnp.int32(at // 2), side)) + at % 2
         mine = new_ref[slot]
         rank = jnp.int32(0)
         for other in range(slots):
@@ -415,7 +427,7 @@
 
 
 def swapped(size, bits):
-    return [(index, index ^ bits) for index in range(size)]
+    return [(index, index ^ bits[index % 2]) for index in range(size)]
 
 
 def dispatched(
@@ -434,18 +446,22 @@
     rows = batches * tokens
     cap = min(CAP * REPL, tokens)
     count = batches * cap
-    distant = 2 * SQUARE
+    distant = (2 * SQUARE, 2 * SQUARE)
+    beside = (1, 1)
 
     def swap(value, bits):
         return lax.ppermute(value, "expert", swapped(size, bits))
 
     def around(blocks):
-        return [blocks[0]] + [swap(blocks[q], 2 * q) for q in range(1, SQUARE)]
+        return [blocks[0]] + [
+            swap(blocks[q], [2 * order[q] for order in PEERS])
+            for q in range(1, SQUARE)
+        ]
 
     x = activations.reshape(rows, width)
     x_far = swap(x, distant)
     panels = (gate_panel, up_panel, down_panel)
-    panels_far = [swap(panel, 1) for panel in panels]
+    panels_far = [swap(panel, beside) for panel in panels]
     *blocks, sel, table, picks, zero, gate_own, up_own = pick_own(
         cap,
         old_home,
@@ -464,7 +480,7 @@
     *results_far, load = run_expert(count, blocks_far, panels, panels_far, load)
     results_far = around(results_far)
     results = around(results)
-    load_far = swap(load, 1)
+    load_far = swap(load, beside)
     whole = jax.ShapeDtypeStruct((rows, width), jnp.bfloat16)
     (far,) = small_call(functools.partial(merge_kernel, count), [whole], sel_far, *results_far)
     back = swap(far, distant)

time: 52.4 us -> 55 us (1.050)
  waiting for transfers between devices: 18.7 us -> 22.2 us
  starting transfers between devices: 23.1 us -> 22.3 us
    ppermute x19, waiting for transfers between devices: 18.7 us -> 22.2 us  [swap(): return lax.ppermute(value, 'expert', swapped(size, bits))]
    ppermute x19, starting transfers between devices: 23.1 us -> 22.3 us  [swap(): return lax.ppermute(value, 'expert', swapped(size, bits))]
where the time goes in v5:
time: 55 us; the launch traced here: 54.9 us
  starting transfers between devices  22.3 us (41%)
  waiting for transfers between devices  22.2 us (40%)
  Pallas kernels  9.64 us (18%)
  between operations  0.75 us (1%)
    ppermute x19, starting transfers between devices, swap(): return lax.ppermute(value, 'expert', swapped(size, bits))  22.3 us
    ppermute x19, waiting for transfers between devices, swap(): return lax.ppermute(value, 'expert', swapped(size, bits))  22.2 us
    pallas_call x2, Pallas kernels, run_expert(): pl.pallas_call(functools.partial(expert_kernel, count), out_shape=[block]...  4.43 us
    pallas_call x1, Pallas kernels, pick_own(): pl.pallas_call(functools.partial(pick_own_kernel, cap), out_shape=shapes,...  2.05 us
    pallas_call x1, Pallas kernels, fetched(): pl.pallas_call(fetch_kernel, out_shape=[jax.ShapeDtypeStruct(value.shape,...  1.42 us
    pallas_call x3, Pallas kernels, small_call(): pl.pallas_call(kernel, out_shape=shapes, in_specs=[pl.BlockSpec(memory_sp...  1.21 us
  transfers between devices with their start and end apart: 19, of which 10 were waited for; matrix products, arithmetic and copies ran while one was open for 0% of the time, Pallas kernels for 12%

profile of v5, /device:TPU:0, one launch (start us, length us, event | category | flops | bytes accessed | tf_op | source)
XLA Modules:
  0.0 54.9 jit_solution(6260606446115861307)
XLA Ops:
  0.6 0.6 %collective-permute-start.3 = (bf16[1,2048,384]{2,1,0:T(8,128)(2,1)}, bf16[1,2048,384]{2,1,0:T(8,128)(2,1)S(1)}, u32[]{:S(2)}, u32[]{:S(2)}) collective-permute-start(bf16[1,2048,384]{2,1,0:T(8,128)(2,1)} %refs_0_.2), channel_id=1, source_target_pairs={{0,1},{1,0},{2,3},{3,2},{4,5},{5,4},{6,7},{7,6},{8,9},{9,8},{10,11... | collective-permute-start | bytes 4718600 | tf_op jit(solution)/shard_map/ppermute | solution.py:453
  1.3 0.4 collective-permute-start.5
  1.7 3.6 %collective-permute-start.9 = (bf16[32,2048]{1,0:T(8,128)(2,1)}, bf16[32,2048]{1,0:T(8,128)(2,1)S(1)}, u32[]{:S(2)}, u32[]{:S(2)}) collective-permute-start(bf16[32,2048]{1,0:T(8,128)(2,1)} %bitcast.6), channel_id=1, source_target_pairs={{0,8},{1,9},{2,10},{3,11},{4,12},{5,13},{6,14},{7,15},{8,0},{9,1},... | collective-permute-start | bytes 393224 | tf_op jit(solution)/shard_map/ppermute | solution.py:453
  5.4 2.1 %shard_map.104 = (bf16[8,5248]{1,0:T(8,128)(2,1)S(1)}, bf16[8,5248]{1,0:T(8,128)(2,1)S(1)}, bf16[8,5248]{1,0:T(8,128)(2,1)S(1)}, bf16[8,5248]{1,0:T(8,128)(2,1)S...) custom-call(s32[8]{0:T(128)} %home_hbm.1, ...), custom_call_target="tpu_custom_call" | custom-call | flops 12582912 | bytes 786432 | tf_op jit(solution)/shard_map/pallas_call | solution.py:273
  7.5 5.0 %collective-permute-done.10.picks_ref = s32[4,16]{1,0:T(4,128)S(1)} collective-permute-done((s32[4,16]{1,0:T(4,128)S(1)}, s32[4,16]{1,0:T(4,128)S(1)}, u32[]{:S(2)}, u32[]{:S(2)}) %collective-permute-start.10) | collective-permute-done | bytes 288 | tf_op jit(solution)/shard_map/ppermute | solution.py:453
  12.5 1.5 %collective-permute-start = (bf16[8,5248]{1,0:T(8,128)(2,1)S(1)}, bf16[8,5248]{1,0:T(8,128)(2,1)S(1)}, u32[]{:S(2)}, u32[]{:S(2)}) collective-permute-start(bf16[8,5248]{1,0:T(8,128)(2,1)S(1)} %get-tuple-element.33), channel_id=1, source_target_pairs={{0,2},{1,7},{2,0},{3,5},{4,6},{5,3},{6,4},{7,1},{8,10},{9,15},{10,... | collective-permute-start | bytes 251912 | tf_op jit(solution)/shard_map/ppermute | solution.py:453
  14.1 3.6 %collective-permute-done.refs_1_ = bf16[8,5248]{1,0:T(8,128)(2,1)S(1)} collective-permute-done((bf16[8,5248]{1,0:T(8,128)(2,1)S(1)}, bf16[8,5248]{1,0:T(8,128)(2,1)S(1)}, u32[]{:S(2)}, u32[]{:S(2)}) %collective-permute-start) | collective-permute-done | bytes 84000 | tf_op jit(solution)/shard_map/ppermute | solution.py:453
  17.7 1.0 %collective-permute-start.1 = (bf16[8,5248]{1,0:T(8,128)(2,1)S(1)}, bf16[8,5248]{1,0:T(8,128)(2,1)S(1)}, u32[]{:S(2)}, u32[]{:S(2)}) collective-permute-start(bf16[8,5248]{1,0:T(8,128)(2,1)S(1)} %get-tuple-element.34), channel_id=1, source_target_pairs={{0,4},{1,3},{2,6},{3,1},{4,0},{5,7},{6,2},{7,5},{8,12},{9,11},{10,... | collective-permute-start | bytes 251912 | tf_op jit(solution)/shard_map/ppermute | solution.py:453
  18.7 1.7 %collective-permute-start.2 = (bf16[8,5248]{1,0:T(8,128)(2,1)S(1)}, bf16[8,5248]{1,0:T(8,128)(2,1)S(1)}, u32[]{:S(2)}, u32[]{:S(2)}) collective-permute-start(bf16[8,5248]{1,0:T(8,128)(2,1)S(1)} %get-tuple-element.35), channel_id=1, source_target_pairs={{0,6},{1,5},{2,4},{3,7},{4,2},{5,1},{6,0},{7,3},{8,14},{9,13},{10,... | collective-permute-start | bytes 251912 | tf_op jit(solution)/shard_map/ppermute | solution.py:453
  20.4 0.5 shard_map.108
  20.9 1.2 %collective-permute-done.1.refs_2_ = bf16[8,5248]{1,0:T(8,128)(2,1)S(1)} collective-permute-done((bf16[8,5248]{1,0:T(8,128)(2,1)S(1)}, bf16[8,5248]{1,0:T(8,128)(2,1)S(1)}, u32[]{:S(2)}, u32[]{:S(2)}) %collective-permute-start.1) | collective-permute-done | bytes 84000 | tf_op jit(solution)/shard_map/ppermute | solution.py:453
  22.1 1.2 %collective-permute-start.11 = (bf16[8,5248]{1,0:T(8,128)(2,1)S(1)}, bf16[8,5248]{1,0:T(8,128)(2,1)S(1)}, u32[]{:S(2)}, u32[]{:S(2)}) collective-permute-start(bf16[8,5248]{1,0:T(8,128)(2,1)S(1)} %get-tuple-element.48), channel_id=1, source_target_pairs={{0,2},{1,7},{2,0},{3,5},{4,6},{5,3},{6,4},{7,1},{8,10},{9,15},{10,... | collective-permute-start | bytes 251912 | tf_op jit(solution)/shard_map/ppermute | solution.py:453
  23.4 1.3 %collective-permute-done.2.refs_3_ = bf16[8,5248]{1,0:T(8,128)(2,1)S(1)} collective-permute-done((bf16[8,5248]{1,0:T(8,128)(2,1)S(1)}, bf16[8,5248]{1,0:T(8,128)(2,1)S(1)}, u32[]{:S(2)}, u32[]{:S(2)}) %collective-permute-start.2) | collective-permute-done | bytes 84000 | tf_op jit(solution)/shard_map/ppermute | solution.py:453
  24.7 1.0 %collective-permute-start.12 = (bf16[8,5248]{1,0:T(8,128)(2,1)S(1)}, bf16[8,5248]{1,0:T(8,128)(2,1)S(1)}, u32[]{:S(2)}, u32[]{:S(2)}) collective-permute-start(bf16[8,5248]{1,0:T(8,128)(2,1)S(1)} %get-tuple-element.49), channel_id=1, source_target_pairs={{0,4},{1,3},{2,6},{3,1},{4,0},{5,7},{6,2},{7,5},{8,12},{9,11},{10,... | collective-permute-start | bytes 251912 | tf_op jit(solution)/shard_map/ppermute | solution.py:453
  25.7 2.3 %collective-permute-start.13 = (bf16[8,5248]{1,0:T(8,128)(2,1)S(1)}, bf16[8,5248]{1,0:T(8,128)(2,1)S(1)}, u32[]{:S(2)}, u32[]{:S(2)}) collective-permute-start(bf16[8,5248]{1,0:T(8,128)(2,1)S(1)} %get-tuple-element.50), channel_id=1, source_target_pairs={{0,6},{1,5},{2,4},{3,7},{4,2},{5,1},{6,0},{7,3},{8,14},{9,13},{10,... | collective-permute-start | bytes 251912 | tf_op jit(solution)/shard_map/ppermute | solution.py:453
  28.0 1.4 %shard_map.105.refs_6_ = bf16[1,2048,384]{2,1,0:T(8,128)(2,1)S(1)} custom-call(bf16[1,2048,384]{2,1,0:T(8,128)(2,1)} %refs_0_.3), custom_call_target="tpu_custom_call" | custom-call | bytes 3145728 | tf_op jit(solution)/shard_map/pallas_call | solution.py:318
  29.4 2.2 %shard_map.106 = (bf16[8,5120]{1,0:T(8,128)(2,1)S(1)}, bf16[8,5120]{1,0:T(8,128)(2,1)S(1)}, bf16[8,5120]{1,0:T(8,128)(2,1)S(1)}, bf16[8,5120]{1,0:T(8,128)(2,1)S(1)}, f32[8,128]{1,0:T(8,128)S(1)}) custom-call(bf16[8,5248]{1,0:T(8,128)(2,1)S(1)} %get-tuple-element.32.refs_0_, bf16[8,5248]{1,0:T(8,128)(2,1)S(1)} %collective-permute-done.refs_1_, ...), custom_call_target="tpu_custom_call" | custom-call | flops 754974720 | bytes 10092544 | tf_op jit(solution)/shard_map/pallas_call | solution.py:356
  31.7 2.2 %shard_map.109 = (bf16[8,5120]{1,0:T(8,128)(2,1)S(1)}, bf16[8,5120]{1,0:T(8,128)(2,1)S(1)}, bf16[8,5120]{1,0:T(8,128)(2,1)S(1)}, bf16[8,5120]{1,0:T(8,128)(2,1)S(1)}, f32[8,128]{1,0:T(8,128)S(1)}) custom-call(bf16[8,5248]{1,0:T(8,128)(2,1)S(1)} %get-tuple-element.47.refs_0_, bf16[8,5248]{1,0:T(8,128)(2,1)S(1)} %collective-permute-done.11.refs_1_, ...), custom_call_target="tpu_custom_call" | custom-call | flops 754974720 | bytes 10092544 | tf_op jit(solution)/shard_map/pallas_call | solution.py:356
  33.9 0.4 collective-permute-start.15
  34.4 1.8 %collective-permute-start.16 = (bf16[8,5120]{1,0:T(8,128)(2,1)S(1)}, bf16[8,5120]{1,0:T(8,128)(2,1)S(1)}, u32[]{:S(2)}, u32[]{:S(2)}) collective-permute-start(bf16[8,5120]{1,0:T(8,128)(2,1)S(1)} %get-tuple-element.56), channel_id=1, source_target_pairs={{0,4},{1,3},{2,6},{3,1},{4,0},{5,7},{6,2},{7,5},{8,12},{9,11},{10,... | collective-permute-start | bytes 245768 | tf_op jit(solution)/shard_map/ppermute | solution.py:453
  36.2 1.3 %collective-permute-start.17 = (bf16[8,5120]{1,0:T(8,128)(2,1)S(1)}, bf16[8,5120]{1,0:T(8,128)(2,1)S(1)}, u32[]{:S(2)}, u32[]{:S(2)}) collective-permute-start(bf16[8,5120]{1,0:T(8,128)(2,1)S(1)} %get-tuple-element.57), channel_id=1, source_target_pairs={{0,6},{1,5},{2,4},{3,7},{4,2},{5,1},{6,0},{7,3},{8,14},{9,13},{10,... | collective-permute-start | bytes 245768 | tf_op jit(solution)/shard_map/ppermute | solution.py:453
  37.5 1.0 %collective-permute-done.15.refs_1_ = bf16[8,5120]{1,0:T(8,128)(2,1)S(1)} collective-permute-done((bf16[8,5120]{1,0:T(8,128)(2,1)S(1)}, bf16[8,5120]{1,0:T(8,128)(2,1)S(1)}, u32[]{:S(2)}, u32[]{:S(2)}) %collective-permute-start.15) | collective-permute-done | bytes 81952 | tf_op jit(solution)/shard_map/ppermute | solution.py:453
  38.4 0.8 %collective-permute-done.16.refs_2_ = bf16[8,5120]{1,0:T(8,128)(2,1)S(1)} collective-permute-done((bf16[8,5120]{1,0:T(8,128)(2,1)S(1)}, bf16[8,5120]{1,0:T(8,128)(2,1)S(1)}, u32[]{:S(2)}, u32[]{:S(2)}) %collective-permute-start.16) | collective-permute-done | bytes 81952 | tf_op jit(solution)/shard_map/ppermute | solution.py:453
  39.2 4.1 %collective-permute-done.17.refs_3_ = bf16[8,5120]{1,0:T(8,128)(2,1)S(1)} collective-permute-done((bf16[8,5120]{1,0:T(8,128)(2,1)S(1)}, bf16[8,5120]{1,0:T(8,128)(2,1)S(1)}, u32[]{:S(2)}, u32[]{:S(2)}) %collective-permute-start.17) | collective-permute-done | bytes 81952 | tf_op jit(solution)/shard_map/ppermute | solution.py:453
  43.5 1.7 %collective-permute-start.18 = (bf16[32,2048]{1,0:T(8,128)(2,1)S(1)}, bf16[32,2048]{1,0:T(8,128)(2,1)S(1)}, u32[]{:S(2)}, u32[]{:S(2)}) collective-permute-start(bf16[32,2048]{1,0:T(8,128)(2,1)S(1)} %shard_map.110), channel_id=1, source_target_pairs={{0,8},{1,9},{2,10},{3,11},{4,12},{5,13},{6,14},{7,15},{8,0},{9,1},... | collective-permute-start | bytes 393224 | tf_op jit(solution)/shard_map/ppermute | solution.py:453
  45.3 0.9 %collective-permute-start.6 = (bf16[8,5120]{1,0:T(8,128)(2,1)S(1)}, bf16[8,5120]{1,0:T(8,128)(2,1)S(1)}, u32[]{:S(2)}, u32[]{:S(2)}) collective-permute-start(bf16[8,5120]{1,0:T(8,128)(2,1)S(1)} %get-tuple-element.40), channel_id=1, source_target_pairs={{0,2},{1,7},{2,0},{3,5},{4,6},{5,3},{6,4},{7,1},{8,10},{9,15},{10,... | collective-permute-start | bytes 245768 | tf_op jit(solution)/shard_map/ppermute | solution.py:453
  46.2 2.3 %collective-permute-start.7 = (bf16[8,5120]{1,0:T(8,128)(2,1)S(1)}, bf16[8,5120]{1,0:T(8,128)(2,1)S(1)}, u32[]{:S(2)}, u32[]{:S(2)}) collective-permute-start(bf16[8,5120]{1,0:T(8,128)(2,1)S(1)} %get-tuple-element.41), channel_id=1, source_target_pairs={{0,4},{1,3},{2,6},{3,1},{4,0},{5,7},{6,2},{7,5},{8,12},{9,11},{10,... | collective-permute-start | bytes 245768 | tf_op jit(solution)/shard_map/ppermute | solution.py:453
  48.7 0.9 %collective-permute-done.6.refs_1_ = bf16[8,5120]{1,0:T(8,128)(2,1)S(1)} collective-permute-done((bf16[8,5120]{1,0:T(8,128)(2,1)S(1)}, bf16[8,5120]{1,0:T(8,128)(2,1)S(1)}, u32[]{:S(2)}, u32[]{:S(2)}) %collective-permute-start.6) | collective-permute-done | bytes 81952 | tf_op jit(solution)/shard_map/ppermute | solution.py:453
  49.7 2.1 %collective-permute-done.7.refs_2_ = bf16[8,5120]{1,0:T(8,128)(2,1)S(1)} collective-permute-done((bf16[8,5120]{1,0:T(8,128)(2,1)S(1)}, bf16[8,5120]{1,0:T(8,128)(2,1)S(1)}, u32[]{:S(2)}, u32[]{:S(2)}) %collective-permute-start.7) | collective-permute-done | bytes 81952 | tf_op jit(solution)/shard_map/ppermute | solution.py:453
  51.8 2.1 %collective-permute-done.8.refs_3_ = bf16[8,5120]{1,0:T(8,128)(2,1)S(1)} collective-permute-done((bf16[8,5120]{1,0:T(8,128)(2,1)S(1)}, bf16[8,5120]{1,0:T(8,128)(2,1)S(1)}, u32[]{:S(2)}, u32[]{:S(2)}) %collective-permute-start.8) | collective-permute-done | bytes 81952 | tf_op jit(solution)/shard_map/ppermute | solution.py:453
  53.9 0.2 shard_map.107
  54.1 0.8 %shard_map.111 = (bf16[32,2048]{1,0:T(8,128)(2,1)}, s32[1]{0:T(128)}) custom-call(bf16[32,2048]{1,0:T(8,128)(2,1)S(1)} %get-tuple-element.43.own_ref, f32[32,128]{1,0:T(8,128)S(1)} %get-tuple-element.44.scale_ref, f32[8,128]{1,0:T(8,128)S(1)} %get-tuple-element.52.load_ref, f32[8,128]{1,0:T(8,128)S(1)} %collective-permute-done.14.load_far_ref, ...), custom_call_target="tpu_custom_call" | custom-call | flops 16777472 | bytes 274432 | tf_op jit(solution)/shard_map/pallas_call | solution.py:415
  (16 shorter events, 0.6 us)
Async XLA Ops:
  0.6 25.0 %collective-permute-start.3 = (bf16[1,2048,384]{2,1,0:T(8,128)(2,1)}, bf16[1,2048,384]{2,1,0:T(8,128)(2,1)S(1)}, u32[]{:S(2)}, u32[]{:S(2)}) collective-permute-start(bf16[1,2048,384]{2,1,0:T(8,128)(2,1)} %refs_0_.2), channel_id=1, source_target_pairs={{0,1},{1,0},{2,3},{3,2},{4,5},{5,4},{6,7},{7,6},{8,9},{9,8},{10,11... | collective-permute-start | bytes 4718600 | tf_op jit(solution)/shard_map/ppermute | solution.py:453
  1.2 28.2 %collective-permute-start.4 = (bf16[1,2048,384]{2,1,0:T(8,128)(2,1)}, bf16[1,2048,384]{2,1,0:T(8,128)(2,1)S(1)}, u32[]{:S(2)}, u32[]{:S(2)}) collective-permute-start(bf16[1,2048,384]{2,1,0:T(8,128)(2,1)} %refs_1_.1), channel_id=1, source_target_pairs={{0,1},{1,0},{2,3},{3,2},{4,5},{5,4},{6,7},{7,6},{8,9},{9,8},{10,11... | collective-permute-start | bytes 4718600 | tf_op jit(solution)/shard_map/ppermute | solution.py:453
  1.3 28.2 %collective-permute-start.5 = (bf16[1,2048,384]{2,1,0:T(8,128)(2,1)}, bf16[1,2048,384]{2,1,0:T(8,128)(2,1)S(1)}, u32[]{:S(2)}, u32[]{:S(2)}) collective-permute-start(bf16[1,2048,384]{2,1,0:T(8,128)(2,1)} %refs_0_.3), channel_id=1, source_target_pairs={{0,1},{1,0},{2,3},{3,2},{4,5},{5,4},{6,7},{7,6},{8,9},{9,8},{10,11... | collective-permute-start | bytes 4718600 | tf_op jit(solution)/shard_map/ppermute | solution.py:453
  1.7 17.0 %collective-permute-start.9 = (bf16[32,2048]{1,0:T(8,128)(2,1)}, bf16[32,2048]{1,0:T(8,128)(2,1)S(1)}, u32[]{:S(2)}, u32[]{:S(2)}) collective-permute-start(bf16[32,2048]{1,0:T(8,128)(2,1)} %bitcast.6), channel_id=1, source_target_pairs={{0,8},{1,9},{2,10},{3,11},{4,12},{5,13},{6,14},{7,15},{8,0},{9,1},... | collective-permute-start | bytes 393224 | tf_op jit(solution)/shard_map/ppermute | solution.py:453
  7.4 5.1 %collective-permute-start.10 = (s32[4,16]{1,0:T(4,128)S(1)}, s32[4,16]{1,0:T(4,128)S(1)}, u32[]{:S(2)}, u32[]{:S(2)}) collective-permute-start(s32[4,16]{1,0:T(4,128)S(1)} %get-tuple-element.46), channel_id=1, source_target_pairs={{0,8},{1,9},{2,10},{3,11},{4,12},{5,13},{6,14},{7,15},{8,0},{9,1},... | collective-permute-start | bytes 776 | tf_op jit(solution)/shard_map/ppermute | solution.py:453
  12.5 5.1 %collective-permute-start = (bf16[8,5248]{1,0:T(8,128)(2,1)S(1)}, bf16[8,5248]{1,0:T(8,128)(2,1)S(1)}, u32[]{:S(2)}, u32[]{:S(2)}) collective-permute-start(bf16[8,5248]{1,0:T(8,128)(2,1)S(1)} %get-tuple-element.33), channel_id=1, source_target_pairs={{0,2},{1,7},{2,0},{3,5},{4,6},{5,3},{6,4},{7,1},{8,10},{9,15},{10,... | collective-permute-start | bytes 251912 | tf_op jit(solution)/shard_map/ppermute | solution.py:453
  17.7 4.5 %collective-permute-start.1 = (bf16[8,5248]{1,0:T(8,128)(2,1)S(1)}, bf16[8,5248]{1,0:T(8,128)(2,1)S(1)}, u32[]{:S(2)}, u32[]{:S(2)}) collective-permute-start(bf16[8,5248]{1,0:T(8,128)(2,1)S(1)} %get-tuple-element.34), channel_id=1, source_target_pairs={{0,4},{1,3},{2,6},{3,1},{4,0},{5,7},{6,2},{7,5},{8,12},{9,11},{10,... | collective-permute-start | bytes 251912 | tf_op jit(solution)/shard_map/ppermute | solution.py:453
  18.7 6.0 %collective-permute-start.2 = (bf16[8,5248]{1,0:T(8,128)(2,1)S(1)}, bf16[8,5248]{1,0:T(8,128)(2,1)S(1)}, u32[]{:S(2)}, u32[]{:S(2)}) collective-permute-start(bf16[8,5248]{1,0:T(8,128)(2,1)S(1)} %get-tuple-element.35), channel_id=1, source_target_pairs={{0,6},{1,5},{2,4},{3,7},{4,2},{5,1},{6,0},{7,3},{8,14},{9,13},{10,... | collective-permute-start | bytes 251912 | tf_op jit(solution)/shard_map/ppermute | solution.py:453
  22.1 9.5 %collective-permute-start.11 = (bf16[8,5248]{1,0:T(8,128)(2,1)S(1)}, bf16[8,5248]{1,0:T(8,128)(2,1)S(1)}, u32[]{:S(2)}, u32[]{:S(2)}) collective-permute-start(bf16[8,5248]{1,0:T(8,128)(2,1)S(1)} %get-tuple-element.48), channel_id=1, source_target_pairs={{0,2},{1,7},{2,0},{3,5},{4,6},{5,3},{6,4},{7,1},{8,10},{9,15},{10,... | collective-permute-start | bytes 251912 | tf_op jit(solution)/shard_map/ppermute | solution.py:453
  24.7 7.0 %collective-permute-start.12 = (bf16[8,5248]{1,0:T(8,128)(2,1)S(1)}, bf16[8,5248]{1,0:T(8,128)(2,1)S(1)}, u32[]{:S(2)}, u32[]{:S(2)}) collective-permute-start(bf16[8,5248]{1,0:T(8,128)(2,1)S(1)} %get-tuple-element.49), channel_id=1, source_target_pairs={{0,4},{1,3},{2,6},{3,1},{4,0},{5,7},{6,2},{7,5},{8,12},{9,11},{10,... | collective-permute-start | bytes 251912 | tf_op jit(solution)/shard_map/ppermute | solution.py:453
  25.7 6.0 %collective-permute-start.13 = (bf16[8,5248]{1,0:T(8,128)(2,1)S(1)}, bf16[8,5248]{1,0:T(8,128)(2,1)S(1)}, u32[]{:S(2)}, u32[]{:S(2)}) collective-permute-start(bf16[8,5248]{1,0:T(8,128)(2,1)S(1)} %get-tuple-element.50), channel_id=1, source_target_pairs={{0,6},{1,5},{2,4},{3,7},{4,2},{5,1},{6,0},{7,3},{8,14},{9,13},{10,... | collective-permute-start | bytes 251912 | tf_op jit(solution)/shard_map/ppermute | solution.py:453
  31.7 22.2 %copy-start = (f32[2,16,1]{1,2,0:T(1,128)S(1)}, f32[2,16,1]{1,2,0:T(1,128)}, u32[]{:S(2)}) copy-start(f32[2,16,1]{1,2,0:T(1,128)} %param.10) | copy-start | bytes 388
  33.9 4.5 %collective-permute-start.15 = (bf16[8,5120]{1,0:T(8,128)(2,1)S(1)}, bf16[8,5120]{1,0:T(8,128)(2,1)S(1)}, u32[]{:S(2)}, u32[]{:S(2)}) collective-permute-start(bf16[8,5120]{1,0:T(8,128)(2,1)S(1)} %get-tuple-element.55), channel_id=1, source_target_pairs={{0,2},{1,7},{2,0},{3,5},{4,6},{5,3},{6,4},{7,1},{8,10},{9,15},{10,... | collective-permute-start | bytes 245768 | tf_op jit(solution)/shard_map/ppermute | solution.py:453
  34.4 4.9 %collective-permute-start.16 = (bf16[8,5120]{1,0:T(8,128)(2,1)S(1)}, bf16[8,5120]{1,0:T(8,128)(2,1)S(1)}, u32[]{:S(2)}, u32[]{:S(2)}) collective-permute-start(bf16[8,5120]{1,0:T(8,128)(2,1)S(1)} %get-tuple-element.56), channel_id=1, source_target_pairs={{0,4},{1,3},{2,6},{3,1},{4,0},{5,7},{6,2},{7,5},{8,12},{9,11},{10,... | collective-permute-start | bytes 245768 | tf_op jit(solution)/shard_map/ppermute | solution.py:453
  36.2 7.1 %collective-permute-start.17 = (bf16[8,5120]{1,0:T(8,128)(2,1)S(1)}, bf16[8,5120]{1,0:T(8,128)(2,1)S(1)}, u32[]{:S(2)}, u32[]{:S(2)}) collective-permute-start(bf16[8,5120]{1,0:T(8,128)(2,1)S(1)} %get-tuple-element.57), channel_id=1, source_target_pairs={{0,6},{1,5},{2,4},{3,7},{4,2},{5,1},{6,0},{7,3},{8,14},{9,13},{10,... | collective-permute-start | bytes 245768 | tf_op jit(solution)/shard_map/ppermute | solution.py:453
  43.5 10.6 %collective-permute-start.18 = (bf16[32,2048]{1,0:T(8,128)(2,1)S(1)}, bf16[32,2048]{1,0:T(8,128)(2,1)S(1)}, u32[]{:S(2)}, u32[]{:S(2)}) collective-permute-start(bf16[32,2048]{1,0:T(8,128)(2,1)S(1)} %shard_map.110), channel_id=1, source_target_pairs={{0,8},{1,9},{2,10},{3,11},{4,12},{5,13},{6,14},{7,15},{8,0},{9,1},... | collective-permute-start | bytes 393224 | tf_op jit(solution)/shard_map/ppermute | solution.py:453
  45.3 4.4 %collective-permute-start.6 = (bf16[8,5120]{1,0:T(8,128)(2,1)S(1)}, bf16[8,5120]{1,0:T(8,128)(2,1)S(1)}, u32[]{:S(2)}, u32[]{:S(2)}) collective-permute-start(bf16[8,5120]{1,0:T(8,128)(2,1)S(1)} %get-tuple-element.40), channel_id=1, source_target_pairs={{0,2},{1,7},{2,0},{3,5},{4,6},{5,3},{6,4},{7,1},{8,10},{9,15},{10,... | collective-permute-start | bytes 245768 | tf_op jit(solution)/shard_map/ppermute | solution.py:453
  46.2 5.6 %collective-permute-start.7 = (bf16[8,5120]{1,0:T(8,128)(2,1)S(1)}, bf16[8,5120]{1,0:T(8,128)(2,1)S(1)}, u32[]{:S(2)}, u32[]{:S(2)}) collective-permute-start(bf16[8,5120]{1,0:T(8,128)(2,1)S(1)} %get-tuple-element.41), channel_id=1, source_target_pairs={{0,4},{1,3},{2,6},{3,1},{4,0},{5,7},{6,2},{7,5},{8,12},{9,11},{10,... | collective-permute-start | bytes 245768 | tf_op jit(solution)/shard_map/ppermute | solution.py:453
  48.5 5.3 %collective-permute-start.8 = (bf16[8,5120]{1,0:T(8,128)(2,1)S(1)}, bf16[8,5120]{1,0:T(8,128)(2,1)S(1)}, u32[]{:S(2)}, u32[]{:S(2)}) collective-permute-start(bf16[8,5120]{1,0:T(8,128)(2,1)S(1)} %get-tuple-element.42), channel_id=1, source_target_pairs={{0,6},{1,5},{2,4},{3,7},{4,2},{5,1},{6,0},{7,3},{8,14},{9,13},{10,... | collective-permute-start | bytes 245768 | tf_op jit(solution)/shard_map/ppermute | solution.py:453
  48.7 5.4 %collective-permute-start.14 = (f32[8,128]{1,0:T(8,128)S(1)}, f32[8,128]{1,0:T(8,128)S(1)}, u32[]{:S(2)}, u32[]{:S(2)}) collective-permute-start(f32[8,128]{1,0:T(8,128)S(1)} %get-tuple-element.52.load_ref), channel_id=1, source_target_pairs={{0,1},{1,0},{2,3},{3,2},{4,5},{5,4},{6,7},{7,6},{8,9},{9,8},{10,11... | collective-permute-start | bytes 12296 | tf_op jit(solution)/shard_map/ppermute | solution.py:453

commit v6 on v5

--- a/solution.py
+++ b/solution.py
@@ -14,7 +14,6 @@
 SQUARE = 4
 TILE = 8
 PEERS = ((0, 1, 2, 3), (0, 3, 1, 2))
-PANELS = 2
 SMALL = 4 << 20
 LARGE = 20 << 20
 VMEM = pltpu.VMEM
@@ -197,12 +196,10 @@
 
 
 def pick_own_kernel(cap, home_hbm, new_hbm, x_hbm, ids_hbm, reps_hbm, *refs):
-    panels_hbm, refs = refs[:PANELS], refs[PANELS:]
     blocks, (sel_ref, table_ref, picks_ref, zero_ref) = refs[:SQUARE], refs[SQUARE : SQUARE + 4]
-    panels, refs = refs[SQUARE + 4 : SQUARE + 4 + PANELS], refs[SQUARE + 4 + PANELS :]
-    home_ref, new_ref, x_ref, ids_ref, reps_ref, sem = refs
-    sources = (home_hbm, new_hbm, ids_hbm, reps_hbm, x_hbm, *panels_hbm)
-    targets = (home_ref, new_ref, ids_ref, reps_ref, x_ref, *panels)
+    home_ref, new_ref, x_ref, ids_ref, reps_ref, sem = refs[SQUARE + 4 :]
+    sources = (home_hbm, new_hbm, ids_hbm, reps_hbm, x_hbm)
+    targets = (home_ref, new_ref, ids_ref, reps_ref, x_ref)
     copies = [
         pltpu.make_async_copy(source, target, sem.at[index])
         for index, (source, target) in enumerate(zip(sources, targets))
@@ -214,7 +211,7 @@
     side = lax.axis_index("expert") % 2
     slots = new_ref.shape[0]
     experts = home_ref.shape[0]
-    for copy in copies[:4]:
+    for copy in copies[:-1]:
         copy.wait()
     picks = jnp.concatenate([ids_ref[...], reps_ref[...]], axis=0)
     picks_ref[...] = picks
@@ -234,12 +231,10 @@
     table_ref[...] = table
 
     def rows():
-        copies[4].wait()
+        copies[-1].wait()
         return x_ref[...]
 
     pick(cap, table, picks, rows, blocks, sel_ref, experts)
-    for copy in copies[5:]:
-        copy.wait()
 
 
 def pick_far_kernel(cap, experts, table_ref, x_ref, picks_ref, *refs):
@@ -261,7 +256,7 @@
     return [block] * SQUARE + [sel], cost
 
 
-def pick_own(cap, home, new, x, ids, reps, panels):
+def pick_own(cap, home, new, x, ids, reps):
     batches, tokens = ids.shape
     shapes, cost = pick_shapes(cap, x, batches)
     shapes += [
@@ -269,11 +264,10 @@
         jax.ShapeDtypeStruct((2 * batches, tokens), jnp.int32),
         jax.ShapeDtypeStruct((8, LANES), jnp.float32),
     ]
-    shapes += [jax.ShapeDtypeStruct(panel.shape, panel.dtype) for panel in panels]
     return pl.pallas_call(
         functools.partial(pick_own_kernel, cap),
         out_shape=shapes,
-        in_specs=[pl.BlockSpec(memory_space=HBM)] * (5 + len(panels)),
+        in_specs=[pl.BlockSpec(memory_space=HBM)] * 5,
         out_specs=[pl.BlockSpec(memory_space=VMEM)] * len(shapes),
         scratch_shapes=[
             SMEM(home.shape, jnp.int32),
@@ -281,11 +275,11 @@
             VMEM(x.shape, x.dtype),
             VMEM(ids.shape, ids.dtype),
             VMEM(reps.shape, reps.dtype),
-            pltpu.SemaphoreType.DMA((5 + len(panels),)),
+            pltpu.SemaphoreType.DMA((5,)),
         ],
         cost_estimate=cost,
-        compiler_params=pltpu.CompilerParams(vmem_limit_bytes=LARGE),
-    )(*(pltpu.with_memory_space_constraint(value, HBM) for value in (home, new, x, ids, reps, *panels)))
+        compiler_params=pltpu.CompilerParams(vmem_limit_bytes=SMALL),
+    )(*(pltpu.with_memory_space_constraint(value, HBM) for value in (home, new, x, ids, reps)))
 
 
 def pick_far(cap, experts, table, x, picks):
@@ -300,37 +294,21 @@
     )(table, x, picks)
 
 
-def fetch_kernel(*refs):
-    count = len(refs) // 2
-    sources, targets, sem = refs[:count], refs[count : 2 * count], refs[2 * count]
-    copies = [
-        pltpu.make_async_copy(source, target, sem.at[index])
-        for index, (source, target) in enumerate(zip(sources, targets))
-    ]
-    for copy in copies:
-        copy.start()
-    for copy in copies:
-        copy.wait()
-
-
-def fetched(values):
-    count = len(values)
-    return pl.pallas_call(
-        fetch_kernel,
-        out_shape=[jax.ShapeDtypeStruct(value.shape, value.dtype) for value in values],
-        in_specs=[pl.BlockSpec(memory_space=HBM)] * count,
-        out_specs=[pl.BlockSpec(memory_space=VMEM)] * count,
-        scratch_shapes=[pltpu.SemaphoreType.DMA((count,))],
-        cost_estimate=pl.CostEstimate(
-            flops=0, bytes_accessed=4 * sum(value.size for value in values), transcendentals=0
-        ),
-        compiler_params=pltpu.CompilerParams(vmem_limit_bytes=LARGE),
-    )(*(pltpu.with_memory_space_constraint(value, HBM) for value in values))
-
-
-def expert_kernel(count, *refs):
+def expert_kernel(count, stream, *refs):
     blocks, panels, prior_ref = refs[:SQUARE], refs[SQUARE : SQUARE + 6], refs[SQUARE + 6]
     outs, load_ref = refs[SQUARE + 7 : 2 * SQUARE + 7], refs[2 * SQUARE + 7]
+    own, copies = list(panels[:3]), {}
+    if stream:
+        *held, sem = refs[2 * SQUARE + 8 :]
+        for index, target in enumerate(held):
+            own[index] = target
+            copies[index] = pltpu.make_async_copy(panels[index], target, sem.at[index])
+            copies[index].start()
+
+    def ready(own_half, place):
+        if own_half and place in copies:
+            copies[place].wait()
+
     x = stacked(count, panels[0].shape[1], blocks)
     high = x.shape[0] // SQUARE
     contract = (((1,), (1,)), ((), ()))
@@ -339,26 +317,37 @@
         load = load + block[:, block.shape[1] - LANES :].astype(jnp.float32)
     load_ref[...] = load
     total = None
-    for gate_ref, up_ref, down_ref in (panels[:3], panels[3:]):
+    for own_half, (gate_ref, up_ref, down_ref) in enumerate((panels[3:], own)):
+        ready(own_half, 0)
         gate = jnp.dot(x, gate_ref[0], preferred_element_type=jnp.float32)
+        ready(own_half, 1)
         up = jnp.dot(x, up_ref[0], preferred_element_type=jnp.float32)
         hidden = (gate / (1.0 + jnp.exp(-gate)) * up).astype(jnp.bfloat16)
+        ready(own_half, 2)
         part = lax.dot_general(hidden, down_ref[0], contract, preferred_element_type=jnp.float32)
         total = part if total is None else total + part
     for q in range(SQUARE):
         packed(count, total[q * high : (q + 1) * high], outs[q])
 
 
-def run_expert(count, blocks, panels, panels_far, prior):
+def run_expert(count, stream, blocks, panels, panels_far, prior):
     width, half = panels[0].shape[1:]
     rows = SQUARE * count
     block = jax.ShapeDtypeStruct((TILE, block_lanes(count, width)), jnp.bfloat16)
+    shapes = [block] * SQUARE + [jax.ShapeDtypeStruct(prior.shape, prior.dtype)]
+    places = [VMEM] * (SQUARE + 7)
+    scratch = []
+    if stream:
+        panels = [pltpu.with_memory_space_constraint(panel, HBM) for panel in panels]
+        shapes += [jax.ShapeDtypeStruct(panel.shape, panel.dtype) for panel in panels]
+        places[SQUARE : SQUARE + 3] = [HBM] * len(panels)
+        scratch.append(pltpu.SemaphoreType.DMA((len(panels),)))
     return pl.pallas_call(
-        functools.partial(expert_kernel, count),
-        out_shape=[block] * SQUARE
-        + [jax.ShapeDtypeStruct(prior.shape, prior.dtype)],
-        in_specs=[pl.BlockSpec(memory_space=VMEM)] * (SQUARE + 7),
-        out_specs=[pl.BlockSpec(memory_space=VMEM)] * (SQUARE + 1),
+        functools.partial(expert_kernel, count, stream),
+        out_shape=shapes,
+        in_specs=[pl.BlockSpec(memory_space=place) for place in places],
+        out_specs=[pl.BlockSpec(memory_space=VMEM)] * len(shapes),
+        scratch_shapes=scratch,
         cost_estimate=pl.CostEstimate(
             flops=2 * rows * width * half * 6,
             bytes_accessed=6 * 2 * width * half + 4 * rows * width,
@@ -462,22 +451,21 @@
     x_far = swap(x, distant)
     panels = (gate_panel, up_panel, down_panel)
     panels_far = [swap(panel, beside) for panel in panels]
-    *blocks, sel, table, picks, zero, gate_own, up_own = pick_own(
+    *blocks, sel, table, picks, zero = pick_own(
         cap,
         old_home,
         new_expert,
         x,
         expert_ids.reshape(batches, tokens),
         replica.reshape(batches, tokens),
-        panels[:PANELS],
     )
     picks_far = swap(picks, distant)
     blocks = around(blocks)
     *blocks_far, sel_far = pick_far(cap, old_home.shape[0], table, x_far, picks_far)
     blocks_far = around(blocks_far)
-    panels = (gate_own, up_own, *fetched(panels[PANELS:]))
-    *results, load = run_expert(count, blocks, panels, panels_far, zero)
-    *results_far, load = run_expert(count, blocks_far, panels, panels_far, load)
+    made = run_expert(count, True, blocks, panels, panels_far, zero)
+    results, load, panels = made[:SQUARE], made[SQUARE], made[SQUARE + 1 :]
+    *results_far, load = run_expert(count, False, blocks_far, panels, panels_far, load)
     results_far = around(results_far)
     results = around(results)
     load_far = swap(load, beside)

time: 55 us -> 54.9 us (level)
  Pallas kernels: 9.64 us -> 8.93 us
    pallas_call x1, Pallas kernels: 2.05 us -> 1.47 us  [pick_own(): pl.pallas_call(functools.partial(pick_own_kernel, cap), out_shape=shapes,...]
    pallas_call x3 -> x2, Pallas kernels: 5.85 us -> 5.71 us  [run_expert(): pl.pallas_call(functools.partial(expert_kernel, count, stream), out_shape...]
  transfers between devices with their start and end apart: 19 -> 19, of which waited for: 10 -> 10; matrix products, arithmetic and copies ran while one was open for 0% -> 0% of each run, Pallas kernels for 12% -> 10%
where the time goes in v6:
time: 54.9 us; the launch traced here: 54.7 us
  waiting for transfers between devices  22.7 us (41%)
  starting transfers between devices  22.4 us (41%)
  Pallas kernels  8.93 us (16%)
  between operations  0.73 us (1%)
    ppermute x19, waiting for transfers between devices, swap(): return lax.ppermute(value, 'expert', swapped(size, bits))  22.7 us
    ppermute x19, starting transfers between devices, swap(): return lax.ppermute(value, 'expert', swapped(size, bits))  22.4 us
    pallas_call x2, Pallas kernels, run_expert(): pl.pallas_call(functools.partial(expert_kernel, count, stream), out_shape...  5.71 us
    pallas_call x1, Pallas kernels, pick_own(): pl.pallas_call(functools.partial(pick_own_kernel, cap), out_shape=shapes,...  1.47 us
    pallas_call x3, Pallas kernels, small_call(): pl.pallas_call(kernel, out_shape=shapes, in_specs=[pl.BlockSpec(memory_sp...  1.21 us
  transfers between devices with their start and end apart: 19, of which 10 were waited for; matrix products, arithmetic and copies ran while one was open for 0% of the time, Pallas kernels for 10%

profile of v6, /device:TPU:0, one launch (start us, length us, event | category | flops | bytes accessed | tf_op | source)
XLA Modules:
  0.0 54.7 jit_solution(2527206727647891569)
XLA Ops:
  0.6 0.6 %collective-permute-start.3 = (bf16[1,2048,384]{2,1,0:T(8,128)(2,1)}, bf16[1,2048,384]{2,1,0:T(8,128)(2,1)S(1)}, u32[]{:S(2)}, u32[]{:S(2)}) collective-permute-start(bf16[1,2048,384]{2,1,0:T(8,128)(2,1)} %refs_4_.1), channel_id=1, source_target_pairs={{0,1},{1,0},{2,3},{3,2},{4,5},{5,4},{6,7},{7,6},{8,9},{9,8},{10,11... | collective-permute-start | bytes 4718600 | tf_op jit(solution)/shard_map/ppermute | solution.py:442
  1.3 0.4 collective-permute-start.5
  1.7 3.7 %collective-permute-start.9 = (bf16[32,2048]{1,0:T(8,128)(2,1)}, bf16[32,2048]{1,0:T(8,128)(2,1)S(1)}, u32[]{:S(2)}, u32[]{:S(2)}) collective-permute-start(bf16[32,2048]{1,0:T(8,128)(2,1)} %bitcast.6), channel_id=1, source_target_pairs={{0,8},{1,9},{2,10},{3,11},{4,12},{5,13},{6,14},{7,15},{8,0},{9,1},... | collective-permute-start | bytes 393224 | tf_op jit(solution)/shard_map/ppermute | solution.py:442
  5.4 1.5 %shard_map.104 = (bf16[8,5248]{1,0:T(8,128)(2,1)S(1)}, bf16[8,5248]{1,0:T(8,128)(2,1)S(1)}, bf16[8,5248]{1,0:T(8,128)(2,1)S(1)}, bf16[8,5248]{1,0:T(8,128)(2,1)S...) custom-call(s32[8]{0:T(128)} %home_hbm.1, s32[16]{0:T(128)} %new_hbm.1, ...), custom_call_target="tpu_custom_call" | custom-call | flops 12582912 | bytes 786432 | tf_op jit(solution)/shard_map/pallas_call | solution.py:267
  6.9 5.6 %collective-permute-done.10.picks_ref = s32[4,16]{1,0:T(4,128)S(1)} collective-permute-done((s32[4,16]{1,0:T(4,128)S(1)}, s32[4,16]{1,0:T(4,128)S(1)}, u32[]{:S(2)}, u32[]{:S(2)}) %collective-permute-start.10) | collective-permute-done | bytes 288 | tf_op jit(solution)/shard_map/ppermute | solution.py:442
  12.5 1.5 %collective-permute-start = (bf16[8,5248]{1,0:T(8,128)(2,1)S(1)}, bf16[8,5248]{1,0:T(8,128)(2,1)S(1)}, u32[]{:S(2)}, u32[]{:S(2)}) collective-permute-start(bf16[8,5248]{1,0:T(8,128)(2,1)S(1)} %get-tuple-element.34), channel_id=1, source_target_pairs={{0,2},{1,7},{2,0},{3,5},{4,6},{5,3},{6,4},{7,1},{8,10},{9,15},{10,... | collective-permute-start | bytes 251912 | tf_op jit(solution)/shard_map/ppermute | solution.py:442
  14.1 3.6 %collective-permute-done.refs_1_ = bf16[8,5248]{1,0:T(8,128)(2,1)S(1)} collective-permute-done((bf16[8,5248]{1,0:T(8,128)(2,1)S(1)}, bf16[8,5248]{1,0:T(8,128)(2,1)S(1)}, u32[]{:S(2)}, u32[]{:S(2)}) %collective-permute-start) | collective-permute-done | bytes 84000 | tf_op jit(solution)/shard_map/ppermute | solution.py:442
  17.7 1.0 %collective-permute-start.1 = (bf16[8,5248]{1,0:T(8,128)(2,1)S(1)}, bf16[8,5248]{1,0:T(8,128)(2,1)S(1)}, u32[]{:S(2)}, u32[]{:S(2)}) collective-permute-start(bf16[8,5248]{1,0:T(8,128)(2,1)S(1)} %get-tuple-element.35), channel_id=1, source_target_pairs={{0,4},{1,3},{2,6},{3,1},{4,0},{5,7},{6,2},{7,5},{8,12},{9,11},{10,... | collective-permute-start | bytes 251912 | tf_op jit(solution)/shard_map/ppermute | solution.py:442
  18.7 1.7 %collective-permute-start.2 = (bf16[8,5248]{1,0:T(8,128)(2,1)S(1)}, bf16[8,5248]{1,0:T(8,128)(2,1)S(1)}, u32[]{:S(2)}, u32[]{:S(2)}) collective-permute-start(bf16[8,5248]{1,0:T(8,128)(2,1)S(1)} %get-tuple-element.36), channel_id=1, source_target_pairs={{0,6},{1,5},{2,4},{3,7},{4,2},{5,1},{6,0},{7,3},{8,14},{9,13},{10,... | collective-permute-start | bytes 251912 | tf_op jit(solution)/shard_map/ppermute | solution.py:442
  20.4 0.5 shard_map.107
  20.9 1.2 %collective-permute-done.1.refs_2_ = bf16[8,5248]{1,0:T(8,128)(2,1)S(1)} collective-permute-done((bf16[8,5248]{1,0:T(8,128)(2,1)S(1)}, bf16[8,5248]{1,0:T(8,128)(2,1)S(1)}, u32[]{:S(2)}, u32[]{:S(2)}) %collective-permute-start.1) | collective-permute-done | bytes 84000 | tf_op jit(solution)/shard_map/ppermute | solution.py:442
  22.1 1.3 %collective-permute-start.11 = (bf16[8,5248]{1,0:T(8,128)(2,1)S(1)}, bf16[8,5248]{1,0:T(8,128)(2,1)S(1)}, u32[]{:S(2)}, u32[]{:S(2)}) collective-permute-start(bf16[8,5248]{1,0:T(8,128)(2,1)S(1)} %get-tuple-element.47), channel_id=1, source_target_pairs={{0,2},{1,7},{2,0},{3,5},{4,6},{5,3},{6,4},{7,1},{8,10},{9,15},{10,... | collective-permute-start | bytes 251912 | tf_op jit(solution)/shard_map/ppermute | solution.py:442
  23.4 1.3 %collective-permute-done.2.refs_3_ = bf16[8,5248]{1,0:T(8,128)(2,1)S(1)} collective-permute-done((bf16[8,5248]{1,0:T(8,128)(2,1)S(1)}, bf16[8,5248]{1,0:T(8,128)(2,1)S(1)}, u32[]{:S(2)}, u32[]{:S(2)}) %collective-permute-start.2) | collective-permute-done | bytes 84000 | tf_op jit(solution)/shard_map/ppermute | solution.py:442
  24.7 1.0 %collective-permute-start.12 = (bf16[8,5248]{1,0:T(8,128)(2,1)S(1)}, bf16[8,5248]{1,0:T(8,128)(2,1)S(1)}, u32[]{:S(2)}, u32[]{:S(2)}) collective-permute-start(bf16[8,5248]{1,0:T(8,128)(2,1)S(1)} %get-tuple-element.48), channel_id=1, source_target_pairs={{0,4},{1,3},{2,6},{3,1},{4,0},{5,7},{6,2},{7,5},{8,12},{9,11},{10,... | collective-permute-start | bytes 251912 | tf_op jit(solution)/shard_map/ppermute | solution.py:442
  25.6 2.3 %collective-permute-start.13 = (bf16[8,5248]{1,0:T(8,128)(2,1)S(1)}, bf16[8,5248]{1,0:T(8,128)(2,1)S(1)}, u32[]{:S(2)}, u32[]{:S(2)}) collective-permute-start(bf16[8,5248]{1,0:T(8,128)(2,1)S(1)} %get-tuple-element.49), channel_id=1, source_target_pairs={{0,6},{1,5},{2,4},{3,7},{4,2},{5,1},{6,0},{7,3},{8,14},{9,13},{10,... | collective-permute-start | bytes 251912 | tf_op jit(solution)/shard_map/ppermute | solution.py:442
  28.0 3.5 %shard_map.105 = (bf16[8,5120]{1,0:T(8,128)(2,1)S(1)}, bf16[8,5120]{1,0:T(8,128)(2,1)S(1)}, bf16[8,5120]{1,0:T(8,128)(2,1)S(1)}, bf16[8,5120]{1,0:T(8,128)(2,1)S...) custom-call(bf16[8,5248]{1,0:T(8,128)(2,1)S(1)} %get-tuple-element.3, ...), custom_call_target="tpu_custom_call" | custom-call | flops 754974720 | bytes 10092544 | tf_op jit(solution)/shard_map/pallas_call | solution.py:345
  31.5 2.2 %shard_map.108 = (bf16[8,5120]{1,0:T(8,128)(2,1)S(1)}, bf16[8,5120]{1,0:T(8,128)(2,1)S(1)}, bf16[8,5120]{1,0:T(8,128)(2,1)S(1)}, bf16[8,5120]{1,0:T(8,128)(2,1)S(1)}, f32[8,128]{1,0:T(8,128)S(1)}) custom-call(bf16[8,5248]{1,0:T(8,128)(2,1)S(1)} %get-tuple-element.46.refs_0_, bf16[8,5248]{1,0:T(8,128)(2,1)S(1)} %collective-permute-done.11.refs_1_, ...), custom_call_target="tpu_custom_call" | custom-call | flops 754974720 | bytes 10092544 | tf_op jit(solution)/shard_map/pallas_call | solution.py:345
  33.7 0.7 %collective-permute-start.15 = (bf16[8,5120]{1,0:T(8,128)(2,1)S(1)}, bf16[8,5120]{1,0:T(8,128)(2,1)S(1)}, u32[]{:S(2)}, u32[]{:S(2)}) collective-permute-start(bf16[8,5120]{1,0:T(8,128)(2,1)S(1)} %get-tuple-element.57), channel_id=1, source_target_pairs={{0,2},{1,7},{2,0},{3,5},{4,6},{5,3},{6,4},{7,1},{8,10},{9,15},{10,... | collective-permute-start | bytes 245768 | tf_op jit(solution)/shard_map/ppermute | solution.py:442
  34.4 1.8 %collective-permute-start.16 = (bf16[8,5120]{1,0:T(8,128)(2,1)S(1)}, bf16[8,5120]{1,0:T(8,128)(2,1)S(1)}, u32[]{:S(2)}, u32[]{:S(2)}) collective-permute-start(bf16[8,5120]{1,0:T(8,128)(2,1)S(1)} %get-tuple-element.58), channel_id=1, source_target_pairs={{0,4},{1,3},{2,6},{3,1},{4,0},{5,7},{6,2},{7,5},{8,12},{9,11},{10,... | collective-permute-start | bytes 245768 | tf_op jit(solution)/shard_map/ppermute | solution.py:442
  36.2 1.1 %collective-permute-start.17 = (bf16[8,5120]{1,0:T(8,128)(2,1)S(1)}, bf16[8,5120]{1,0:T(8,128)(2,1)S(1)}, u32[]{:S(2)}, u32[]{:S(2)}) collective-permute-start(bf16[8,5120]{1,0:T(8,128)(2,1)S(1)} %get-tuple-element.59), channel_id=1, source_target_pairs={{0,6},{1,5},{2,4},{3,7},{4,2},{5,1},{6,0},{7,3},{8,14},{9,13},{10,... | collective-permute-start | bytes 245768 | tf_op jit(solution)/shard_map/ppermute | solution.py:442
  37.3 1.0 %collective-permute-done.15.refs_1_ = bf16[8,5120]{1,0:T(8,128)(2,1)S(1)} collective-permute-done((bf16[8,5120]{1,0:T(8,128)(2,1)S(1)}, bf16[8,5120]{1,0:T(8,128)(2,1)S(1)}, u32[]{:S(2)}, u32[]{:S(2)}) %collective-permute-start.15) | collective-permute-done | bytes 81952 | tf_op jit(solution)/shard_map/ppermute | solution.py:442
  38.2 1.0 %collective-permute-done.16.refs_2_ = bf16[8,5120]{1,0:T(8,128)(2,1)S(1)} collective-permute-done((bf16[8,5120]{1,0:T(8,128)(2,1)S(1)}, bf16[8,5120]{1,0:T(8,128)(2,1)S(1)}, u32[]{:S(2)}, u32[]{:S(2)}) %collective-permute-start.16) | collective-permute-done | bytes 81952 | tf_op jit(solution)/shard_map/ppermute | solution.py:442
  39.3 4.0 %collective-permute-done.17.refs_3_ = bf16[8,5120]{1,0:T(8,128)(2,1)S(1)} collective-permute-done((bf16[8,5120]{1,0:T(8,128)(2,1)S(1)}, bf16[8,5120]{1,0:T(8,128)(2,1)S(1)}, u32[]{:S(2)}, u32[]{:S(2)}) %collective-permute-start.17) | collective-permute-done | bytes 81952 | tf_op jit(solution)/shard_map/ppermute | solution.py:442
  43.5 1.7 %collective-permute-start.18 = (bf16[32,2048]{1,0:T(8,128)(2,1)S(1)}, bf16[32,2048]{1,0:T(8,128)(2,1)S(1)}, u32[]{:S(2)}, u32[]{:S(2)}) collective-permute-start(bf16[32,2048]{1,0:T(8,128)(2,1)S(1)} %shard_map.109), channel_id=1, source_target_pairs={{0,8},{1,9},{2,10},{3,11},{4,12},{5,13},{6,14},{7,15},{8,0},{9,1},... | collective-permute-start | bytes 393224 | tf_op jit(solution)/shard_map/ppermute | solution.py:442
  45.3 0.8 %collective-permute-start.6 = (bf16[8,5120]{1,0:T(8,128)(2,1)S(1)}, bf16[8,5120]{1,0:T(8,128)(2,1)S(1)}, u32[]{:S(2)}, u32[]{:S(2)}) collective-permute-start(bf16[8,5120]{1,0:T(8,128)(2,1)S(1)} %get-tuple-element.39), channel_id=1, source_target_pairs={{0,2},{1,7},{2,0},{3,5},{4,6},{5,3},{6,4},{7,1},{8,10},{9,15},{10,... | collective-permute-start | bytes 245768 | tf_op jit(solution)/shard_map/ppermute | solution.py:442
  46.1 2.3 %collective-permute-start.7 = (bf16[8,5120]{1,0:T(8,128)(2,1)S(1)}, bf16[8,5120]{1,0:T(8,128)(2,1)S(1)}, u32[]{:S(2)}, u32[]{:S(2)}) collective-permute-start(bf16[8,5120]{1,0:T(8,128)(2,1)S(1)} %get-tuple-element.40), channel_id=1, source_target_pairs={{0,4},{1,3},{2,6},{3,1},{4,0},{5,7},{6,2},{7,5},{8,12},{9,11},{10,... | collective-permute-start | bytes 245768 | tf_op jit(solution)/shard_map/ppermute | solution.py:442
  48.4 0.4 collective-permute-start.8
  48.8 0.9 %collective-permute-done.6.refs_1_ = bf16[8,5120]{1,0:T(8,128)(2,1)S(1)} collective-permute-done((bf16[8,5120]{1,0:T(8,128)(2,1)S(1)}, bf16[8,5120]{1,0:T(8,128)(2,1)S(1)}, u32[]{:S(2)}, u32[]{:S(2)}) %collective-permute-start.6) | collective-permute-done | bytes 81952 | tf_op jit(solution)/shard_map/ppermute | solution.py:442
  49.7 1.9 %collective-permute-done.7.refs_2_ = bf16[8,5120]{1,0:T(8,128)(2,1)S(1)} collective-permute-done((bf16[8,5120]{1,0:T(8,128)(2,1)S(1)}, bf16[8,5120]{1,0:T(8,128)(2,1)S(1)}, u32[]{:S(2)}, u32[]{:S(2)}) %collective-permute-start.7) | collective-permute-done | bytes 81952 | tf_op jit(solution)/shard_map/ppermute | solution.py:442
  51.7 2.1 %collective-permute-done.8.refs_3_ = bf16[8,5120]{1,0:T(8,128)(2,1)S(1)} collective-permute-done((bf16[8,5120]{1,0:T(8,128)(2,1)S(1)}, bf16[8,5120]{1,0:T(8,128)(2,1)S(1)}, u32[]{:S(2)}, u32[]{:S(2)}) %collective-permute-start.8) | collective-permute-done | bytes 81952 | tf_op jit(solution)/shard_map/ppermute | solution.py:442
  53.7 0.2 shard_map.106
  54.0 0.8 %shard_map.110 = (bf16[32,2048]{1,0:T(8,128)(2,1)}, s32[1]{0:T(128)}) custom-call(bf16[32,2048]{1,0:T(8,128)(2,1)S(1)} %get-tuple-element.42.own_ref, f32[32,128]{1,0:T(8,128)S(1)} %get-tuple-element.43.scale_ref, f32[8,128]{1,0:T(8,128)S(1)} %get-tuple-element.54.load_ref, f32[8,128]{1,0:T(8,128)S(1)} %collective-permute-done.14.load_far_ref, ...), custom_call_target="tpu_custom_call" | custom-call | flops 16777472 | bytes 274432 | tf_op jit(solution)/shard_map/pallas_call | solution.py:404
  (15 shorter events, 0.4 us)
Async XLA Ops:
  0.6 25.0 %collective-permute-start.3 = (bf16[1,2048,384]{2,1,0:T(8,128)(2,1)}, bf16[1,2048,384]{2,1,0:T(8,128)(2,1)S(1)}, u32[]{:S(2)}, u32[]{:S(2)}) collective-permute-start(bf16[1,2048,384]{2,1,0:T(8,128)(2,1)} %refs_4_.1), channel_id=1, source_target_pairs={{0,1},{1,0},{2,3},{3,2},{4,5},{5,4},{6,7},{7,6},{8,9},{9,8},{10,11... | collective-permute-start | bytes 4718600 | tf_op jit(solution)/shard_map/ppermute | solution.py:442
  1.2 26.8 %collective-permute-start.4 = (bf16[1,2048,384]{2,1,0:T(8,128)(2,1)}, bf16[1,2048,384]{2,1,0:T(8,128)(2,1)S(1)}, u32[]{:S(2)}, u32[]{:S(2)}) collective-permute-start(bf16[1,2048,384]{2,1,0:T(8,128)(2,1)} %refs_5_.1), channel_id=1, source_target_pairs={{0,1},{1,0},{2,3},{3,2},{4,5},{5,4},{6,7},{7,6},{8,9},{9,8},{10,11... | collective-permute-start | bytes 4718600 | tf_op jit(solution)/shard_map/ppermute | solution.py:442
  1.3 26.7 %collective-permute-start.5 = (bf16[1,2048,384]{2,1,0:T(8,128)(2,1)}, bf16[1,2048,384]{2,1,0:T(8,128)(2,1)S(1)}, u32[]{:S(2)}, u32[]{:S(2)}) collective-permute-start(bf16[1,2048,384]{2,1,0:T(8,128)(2,1)} %refs_6_.1), channel_id=1, source_target_pairs={{0,1},{1,0},{2,3},{3,2},{4,5},{5,4},{6,7},{7,6},{8,9},{9,8},{10,11... | collective-permute-start | bytes 4718600 | tf_op jit(solution)/shard_map/ppermute | solution.py:442
  1.7 17.0 %collective-permute-start.9 = (bf16[32,2048]{1,0:T(8,128)(2,1)}, bf16[32,2048]{1,0:T(8,128)(2,1)S(1)}, u32[]{:S(2)}, u32[]{:S(2)}) collective-permute-start(bf16[32,2048]{1,0:T(8,128)(2,1)} %bitcast.6), channel_id=1, source_target_pairs={{0,8},{1,9},{2,10},{3,11},{4,12},{5,13},{6,14},{7,15},{8,0},{9,1},... | collective-permute-start | bytes 393224 | tf_op jit(solution)/shard_map/ppermute | solution.py:442
  6.8 5.7 %collective-permute-start.10 = (s32[4,16]{1,0:T(4,128)S(1)}, s32[4,16]{1,0:T(4,128)S(1)}, u32[]{:S(2)}, u32[]{:S(2)}) collective-permute-start(s32[4,16]{1,0:T(4,128)S(1)} %get-tuple-element.45), channel_id=1, source_target_pairs={{0,8},{1,9},{2,10},{3,11},{4,12},{5,13},{6,14},{7,15},{8,0},{9,1},... | collective-permute-start | bytes 776 | tf_op jit(solution)/shard_map/ppermute | solution.py:442
  12.5 5.1 %collective-permute-start = (bf16[8,5248]{1,0:T(8,128)(2,1)S(1)}, bf16[8,5248]{1,0:T(8,128)(2,1)S(1)}, u32[]{:S(2)}, u32[]{:S(2)}) collective-permute-start(bf16[8,5248]{1,0:T(8,128)(2,1)S(1)} %get-tuple-element.34), channel_id=1, source_target_pairs={{0,2},{1,7},{2,0},{3,5},{4,6},{5,3},{6,4},{7,1},{8,10},{9,15},{10,... | collective-permute-start | bytes 251912 | tf_op jit(solution)/shard_map/ppermute | solution.py:442
  17.7 4.5 %collective-permute-start.1 = (bf16[8,5248]{1,0:T(8,128)(2,1)S(1)}, bf16[8,5248]{1,0:T(8,128)(2,1)S(1)}, u32[]{:S(2)}, u32[]{:S(2)}) collective-permute-start(bf16[8,5248]{1,0:T(8,128)(2,1)S(1)} %get-tuple-element.35), channel_id=1, source_target_pairs={{0,4},{1,3},{2,6},{3,1},{4,0},{5,7},{6,2},{7,5},{8,12},{9,11},{10,... | collective-permute-start | bytes 251912 | tf_op jit(solution)/shard_map/ppermute | solution.py:442
  18.7 6.0 %collective-permute-start.2 = (bf16[8,5248]{1,0:T(8,128)(2,1)S(1)}, bf16[8,5248]{1,0:T(8,128)(2,1)S(1)}, u32[]{:S(2)}, u32[]{:S(2)}) collective-permute-start(bf16[8,5248]{1,0:T(8,128)(2,1)S(1)} %get-tuple-element.36), channel_id=1, source_target_pairs={{0,6},{1,5},{2,4},{3,7},{4,2},{5,1},{6,0},{7,3},{8,14},{9,13},{10,... | collective-permute-start | bytes 251912 | tf_op jit(solution)/shard_map/ppermute | solution.py:442
  22.1 9.3 %collective-permute-start.11 = (bf16[8,5248]{1,0:T(8,128)(2,1)S(1)}, bf16[8,5248]{1,0:T(8,128)(2,1)S(1)}, u32[]{:S(2)}, u32[]{:S(2)}) collective-permute-start(bf16[8,5248]{1,0:T(8,128)(2,1)S(1)} %get-tuple-element.47), channel_id=1, source_target_pairs={{0,2},{1,7},{2,0},{3,5},{4,6},{5,3},{6,4},{7,1},{8,10},{9,15},{10,... | collective-permute-start | bytes 251912 | tf_op jit(solution)/shard_map/ppermute | solution.py:442
  24.7 6.8 %collective-permute-start.12 = (bf16[8,5248]{1,0:T(8,128)(2,1)S(1)}, bf16[8,5248]{1,0:T(8,128)(2,1)S(1)}, u32[]{:S(2)}, u32[]{:S(2)}) collective-permute-start(bf16[8,5248]{1,0:T(8,128)(2,1)S(1)} %get-tuple-element.48), channel_id=1, source_target_pairs={{0,4},{1,3},{2,6},{3,1},{4,0},{5,7},{6,2},{7,5},{8,12},{9,11},{10,... | collective-permute-start | bytes 251912 | tf_op jit(solution)/shard_map/ppermute | solution.py:442
  25.6 5.8 %collective-permute-start.13 = (bf16[8,5248]{1,0:T(8,128)(2,1)S(1)}, bf16[8,5248]{1,0:T(8,128)(2,1)S(1)}, u32[]{:S(2)}, u32[]{:S(2)}) collective-permute-start(bf16[8,5248]{1,0:T(8,128)(2,1)S(1)} %get-tuple-element.49), channel_id=1, source_target_pairs={{0,6},{1,5},{2,4},{3,7},{4,2},{5,1},{6,0},{7,3},{8,14},{9,13},{10,... | collective-permute-start | bytes 251912 | tf_op jit(solution)/shard_map/ppermute | solution.py:442
  31.5 22.2 %copy-start = (f32[2,16,1]{1,2,0:T(1,128)S(1)}, f32[2,16,1]{1,2,0:T(1,128)}, u32[]{:S(2)}) copy-start(f32[2,16,1]{1,2,0:T(1,128)} %param.10) | copy-start | bytes 388
  33.7 4.5 %collective-permute-start.15 = (bf16[8,5120]{1,0:T(8,128)(2,1)S(1)}, bf16[8,5120]{1,0:T(8,128)(2,1)S(1)}, u32[]{:S(2)}, u32[]{:S(2)}) collective-permute-start(bf16[8,5120]{1,0:T(8,128)(2,1)S(1)} %get-tuple-element.57), channel_id=1, source_target_pairs={{0,2},{1,7},{2,0},{3,5},{4,6},{5,3},{6,4},{7,1},{8,10},{9,15},{10,... | collective-permute-start | bytes 245768 | tf_op jit(solution)/shard_map/ppermute | solution.py:442
  34.4 4.9 %collective-permute-start.16 = (bf16[8,5120]{1,0:T(8,128)(2,1)S(1)}, bf16[8,5120]{1,0:T(8,128)(2,1)S(1)}, u32[]{:S(2)}, u32[]{:S(2)}) collective-permute-start(bf16[8,5120]{1,0:T(8,128)(2,1)S(1)} %get-tuple-element.58), channel_id=1, source_target_pairs={{0,4},{1,3},{2,6},{3,1},{4,0},{5,7},{6,2},{7,5},{8,12},{9,11},{10,... | collective-permute-start | bytes 245768 | tf_op jit(solution)/shard_map/ppermute | solution.py:442
  36.2 7.1 %collective-permute-start.17 = (bf16[8,5120]{1,0:T(8,128)(2,1)S(1)}, bf16[8,5120]{1,0:T(8,128)(2,1)S(1)}, u32[]{:S(2)}, u32[]{:S(2)}) collective-permute-start(bf16[8,5120]{1,0:T(8,128)(2,1)S(1)} %get-tuple-element.59), channel_id=1, source_target_pairs={{0,6},{1,5},{2,4},{3,7},{4,2},{5,1},{6,0},{7,3},{8,14},{9,13},{10,... | collective-permute-start | bytes 245768 | tf_op jit(solution)/shard_map/ppermute | solution.py:442
  43.5 10.4 %collective-permute-start.18 = (bf16[32,2048]{1,0:T(8,128)(2,1)S(1)}, bf16[32,2048]{1,0:T(8,128)(2,1)S(1)}, u32[]{:S(2)}, u32[]{:S(2)}) collective-permute-start(bf16[32,2048]{1,0:T(8,128)(2,1)S(1)} %shard_map.109), channel_id=1, source_target_pairs={{0,8},{1,9},{2,10},{3,11},{4,12},{5,13},{6,14},{7,15},{8,0},{9,1},... | collective-permute-start | bytes 393224 | tf_op jit(solution)/shard_map/ppermute | solution.py:442
  45.3 4.4 %collective-permute-start.6 = (bf16[8,5120]{1,0:T(8,128)(2,1)S(1)}, bf16[8,5120]{1,0:T(8,128)(2,1)S(1)}, u32[]{:S(2)}, u32[]{:S(2)}) collective-permute-start(bf16[8,5120]{1,0:T(8,128)(2,1)S(1)} %get-tuple-element.39), channel_id=1, source_target_pairs={{0,2},{1,7},{2,0},{3,5},{4,6},{5,3},{6,4},{7,1},{8,10},{9,15},{10,... | collective-permute-start | bytes 245768 | tf_op jit(solution)/shard_map/ppermute | solution.py:442
  46.1 5.6 %collective-permute-start.7 = (bf16[8,5120]{1,0:T(8,128)(2,1)S(1)}, bf16[8,5120]{1,0:T(8,128)(2,1)S(1)}, u32[]{:S(2)}, u32[]{:S(2)}) collective-permute-start(bf16[8,5120]{1,0:T(8,128)(2,1)S(1)} %get-tuple-element.40), channel_id=1, source_target_pairs={{0,4},{1,3},{2,6},{3,1},{4,0},{5,7},{6,2},{7,5},{8,12},{9,11},{10,... | collective-permute-start | bytes 245768 | tf_op jit(solution)/shard_map/ppermute | solution.py:442
  48.4 5.3 %collective-permute-start.8 = (bf16[8,5120]{1,0:T(8,128)(2,1)S(1)}, bf16[8,5120]{1,0:T(8,128)(2,1)S(1)}, u32[]{:S(2)}, u32[]{:S(2)}) collective-permute-start(bf16[8,5120]{1,0:T(8,128)(2,1)S(1)} %get-tuple-element.41), channel_id=1, source_target_pairs={{0,6},{1,5},{2,4},{3,7},{4,2},{5,1},{6,0},{7,3},{8,14},{9,13},{10,... | collective-permute-start | bytes 245768 | tf_op jit(solution)/shard_map/ppermute | solution.py:442
  48.8 5.2 %collective-permute-start.14 = (f32[8,128]{1,0:T(8,128)S(1)}, f32[8,128]{1,0:T(8,128)S(1)}, u32[]{:S(2)}, u32[]{:S(2)}) collective-permute-start(f32[8,128]{1,0:T(8,128)S(1)} %get-tuple-element.54.load_ref), channel_id=1, source_target_pairs={{0,1},{1,0},{2,3},{3,2},{4,5},{5,4},{6,7},{7,6},{8,9},{9,8},{10,11... | collective-permute-start | bytes 12296 | tf_op jit(solution)/shard_map/ppermute | solution.py:442

commit v7 on v6

--- a/solution.py
+++ b/solution.py
@@ -220,14 +220,16 @@
     table = jnp.zeros(table_ref.shape, jnp.int32)
     for expert in range(experts):
         table = jnp.where((row == 0) & (lane == expert), home_ref[expert], table)
-    for at in range(2 * SQUARE):
-        slot = 2 * (chip ^ peer_of(jnp.int32(at // 2), side)) + at % 2
-        mine = new_ref[slot]
-        rank = jnp.int32(0)
-        for other in range(slots):
-            rank = rank + ((new_ref[other] == mine) & (slot > other)).astype(jnp.int32)
-        table = jnp.where((row == 1) & (lane == at), mine, table)
-        table = jnp.where((row == 2) & (lane == at), rank, table)
+    pair = peer_of(steps(lane, 2, SQUARE), side)
+    slot = 2 * (chip ^ pair) + lane % 2
+    mine = jnp.zeros(table_ref.shape, jnp.int32)
+    for other in range(slots):
+        mine = jnp.where(slot == other, new_ref[other], mine)
+    rank = jnp.zeros(table_ref.shape, jnp.int32)
+    for other in range(slots):
+        rank = rank + ((new_ref[other] == mine) & (slot > other)).astype(jnp.int32)
+    table = jnp.where((row == 1) & (lane < 2 * SQUARE), mine, table)
+    table = jnp.where((row == 2) & (lane < 2 * SQUARE), rank, table)
     table_ref[...] = table
 
     def rows():

time: 54.9 us -> 54.9 us (level)
  no operation moved by 1% of the time
where the time goes in v7:
time: 54.9 us; the launch traced here: 54.7 us
  waiting for transfers between devices  22.9 us (42%)
  starting transfers between devices  22.4 us (41%)
  Pallas kernels  8.74 us (16%)
  between operations  0.73 us (1%)
    ppermute x19, waiting for transfers between devices, swap(): return lax.ppermute(value, 'expert', swapped(size, bits))  22.9 us
    ppermute x19, starting transfers between devices, swap(): return lax.ppermute(value, 'expert', swapped(size, bits))  22.4 us
    pallas_call x2, Pallas kernels, run_expert(): pl.pallas_call(functools.partial(expert_kernel, count, stream), out_shape...  5.71 us
    pallas_call x1, Pallas kernels, pick_own(): pl.pallas_call(functools.partial(pick_own_kernel, cap), out_shape=shapes,...  1.29 us
    pallas_call x3, Pallas kernels, small_call(): pl.pallas_call(kernel, out_shape=shapes, in_specs=[pl.BlockSpec(memory_sp...  1.21 us
  transfers between devices with their start and end apart: 19, of which 10 were waited for; matrix products, arithmetic and copies ran while one was open for 0% of the time, Pallas kernels for 10%

profile of v7, /device:TPU:0, one launch (start us, length us, event | category | flops | bytes accessed | tf_op | source)
XLA Modules:
  0.0 54.7 jit_solution(1731065460028815802)
XLA Ops:
  0.6 0.6 %collective-permute-start.3 = (bf16[1,2048,384]{2,1,0:T(8,128)(2,1)}, bf16[1,2048,384]{2,1,0:T(8,128)(2,1)S(1)}, u32[]{:S(2)}, u32[]{:S(2)}) collective-permute-start(bf16[1,2048,384]{2,1,0:T(8,128)(2,1)} %refs_4_.1), channel_id=1, source_target_pairs={{0,1},{1,0},{2,3},{3,2},{4,5},{5,4},{6,7},{7,6},{8,9},{9,8},{10,11... | collective-permute-start | bytes 4718600 | tf_op jit(solution)/shard_map/ppermute | solution.py:444
  1.3 0.4 collective-permute-start.5
  1.7 3.7 %collective-permute-start.9 = (bf16[32,2048]{1,0:T(8,128)(2,1)}, bf16[32,2048]{1,0:T(8,128)(2,1)S(1)}, u32[]{:S(2)}, u32[]{:S(2)}) collective-permute-start(bf16[32,2048]{1,0:T(8,128)(2,1)} %bitcast.6), channel_id=1, source_target_pairs={{0,8},{1,9},{2,10},{3,11},{4,12},{5,13},{6,14},{7,15},{8,0},{9,1},... | collective-permute-start | bytes 393224 | tf_op jit(solution)/shard_map/ppermute | solution.py:444
  5.4 1.3 %shard_map.104 = (bf16[8,5248]{1,0:T(8,128)(2,1)S(1)}, bf16[8,5248]{1,0:T(8,128)(2,1)S(1)}, bf16[8,5248]{1,0:T(8,128)(2,1)S(1)}, bf16[8,5248]{1,0:T(8,128)(2,1)S...) custom-call(s32[8]{0:T(128)} %home_hbm.1, s32[16]{0:T(128)} %new_hbm.1, ...), custom_call_target="tpu_custom_call" | custom-call | flops 12582912 | bytes 786432 | tf_op jit(solution)/shard_map/pallas_call | solution.py:269
  6.7 5.8 %collective-permute-done.10.picks_ref = s32[4,16]{1,0:T(4,128)S(1)} collective-permute-done((s32[4,16]{1,0:T(4,128)S(1)}, s32[4,16]{1,0:T(4,128)S(1)}, u32[]{:S(2)}, u32[]{:S(2)}) %collective-permute-start.10) | collective-permute-done | bytes 288 | tf_op jit(solution)/shard_map/ppermute | solution.py:444
  12.5 1.5 %collective-permute-start = (bf16[8,5248]{1,0:T(8,128)(2,1)S(1)}, bf16[8,5248]{1,0:T(8,128)(2,1)S(1)}, u32[]{:S(2)}, u32[]{:S(2)}) collective-permute-start(bf16[8,5248]{1,0:T(8,128)(2,1)S(1)} %get-tuple-element.34), channel_id=1, source_target_pairs={{0,2},{1,7},{2,0},{3,5},{4,6},{5,3},{6,4},{7,1},{8,10},{9,15},{10,... | collective-permute-start | bytes 251912 | tf_op jit(solution)/shard_map/ppermute | solution.py:444
  14.1 3.6 %collective-permute-done.refs_1_ = bf16[8,5248]{1,0:T(8,128)(2,1)S(1)} collective-permute-done((bf16[8,5248]{1,0:T(8,128)(2,1)S(1)}, bf16[8,5248]{1,0:T(8,128)(2,1)S(1)}, u32[]{:S(2)}, u32[]{:S(2)}) %collective-permute-start) | collective-permute-done | bytes 84000 | tf_op jit(solution)/shard_map/ppermute | solution.py:444
  17.7 1.0 %collective-permute-start.1 = (bf16[8,5248]{1,0:T(8,128)(2,1)S(1)}, bf16[8,5248]{1,0:T(8,128)(2,1)S(1)}, u32[]{:S(2)}, u32[]{:S(2)}) collective-permute-start(bf16[8,5248]{1,0:T(8,128)(2,1)S(1)} %get-tuple-element.35), channel_id=1, source_target_pairs={{0,4},{1,3},{2,6},{3,1},{4,0},{5,7},{6,2},{7,5},{8,12},{9,11},{10,... | collective-permute-start | bytes 251912 | tf_op jit(solution)/shard_map/ppermute | solution.py:444
  18.7 1.7 %collective-permute-start.2 = (bf16[8,5248]{1,0:T(8,128)(2,1)S(1)}, bf16[8,5248]{1,0:T(8,128)(2,1)S(1)}, u32[]{:S(2)}, u32[]{:S(2)}) collective-permute-start(bf16[8,5248]{1,0:T(8,128)(2,1)S(1)} %get-tuple-element.36), channel_id=1, source_target_pairs={{0,6},{1,5},{2,4},{3,7},{4,2},{5,1},{6,0},{7,3},{8,14},{9,13},{10,... | collective-permute-start | bytes 251912 | tf_op jit(solution)/shard_map/ppermute | solution.py:444
  20.4 0.5 shard_map.107
  20.9 1.2 %collective-permute-done.1.refs_2_ = bf16[8,5248]{1,0:T(8,128)(2,1)S(1)} collective-permute-done((bf16[8,5248]{1,0:T(8,128)(2,1)S(1)}, bf16[8,5248]{1,0:T(8,128)(2,1)S(1)}, u32[]{:S(2)}, u32[]{:S(2)}) %collective-permute-start.1) | collective-permute-done | bytes 84000 | tf_op jit(solution)/shard_map/ppermute | solution.py:444
  22.1 1.3 %collective-permute-start.11 = (bf16[8,5248]{1,0:T(8,128)(2,1)S(1)}, bf16[8,5248]{1,0:T(8,128)(2,1)S(1)}, u32[]{:S(2)}, u32[]{:S(2)}) collective-permute-start(bf16[8,5248]{1,0:T(8,128)(2,1)S(1)} %get-tuple-element.47), channel_id=1, source_target_pairs={{0,2},{1,7},{2,0},{3,5},{4,6},{5,3},{6,4},{7,1},{8,10},{9,15},{10,... | collective-permute-start | bytes 251912 | tf_op jit(solution)/shard_map/ppermute | solution.py:444
  23.4 1.3 %collective-permute-done.2.refs_3_ = bf16[8,5248]{1,0:T(8,128)(2,1)S(1)} collective-permute-done((bf16[8,5248]{1,0:T(8,128)(2,1)S(1)}, bf16[8,5248]{1,0:T(8,128)(2,1)S(1)}, u32[]{:S(2)}, u32[]{:S(2)}) %collective-permute-start.2) | collective-permute-done | bytes 84000 | tf_op jit(solution)/shard_map/ppermute | solution.py:444
  24.7 1.0 %collective-permute-start.12 = (bf16[8,5248]{1,0:T(8,128)(2,1)S(1)}, bf16[8,5248]{1,0:T(8,128)(2,1)S(1)}, u32[]{:S(2)}, u32[]{:S(2)}) collective-permute-start(bf16[8,5248]{1,0:T(8,128)(2,1)S(1)} %get-tuple-element.48), channel_id=1, source_target_pairs={{0,4},{1,3},{2,6},{3,1},{4,0},{5,7},{6,2},{7,5},{8,12},{9,11},{10,... | collective-permute-start | bytes 251912 | tf_op jit(solution)/shard_map/ppermute | solution.py:444
  25.7 2.3 %collective-permute-start.13 = (bf16[8,5248]{1,0:T(8,128)(2,1)S(1)}, bf16[8,5248]{1,0:T(8,128)(2,1)S(1)}, u32[]{:S(2)}, u32[]{:S(2)}) collective-permute-start(bf16[8,5248]{1,0:T(8,128)(2,1)S(1)} %get-tuple-element.49), channel_id=1, source_target_pairs={{0,6},{1,5},{2,4},{3,7},{4,2},{5,1},{6,0},{7,3},{8,14},{9,13},{10,... | collective-permute-start | bytes 251912 | tf_op jit(solution)/shard_map/ppermute | solution.py:444
  28.0 3.5 %shard_map.105 = (bf16[8,5120]{1,0:T(8,128)(2,1)S(1)}, bf16[8,5120]{1,0:T(8,128)(2,1)S(1)}, bf16[8,5120]{1,0:T(8,128)(2,1)S(1)}, bf16[8,5120]{1,0:T(8,128)(2,1)S...) custom-call(bf16[8,5248]{1,0:T(8,128)(2,1)S(1)} %get-tuple-element.3, ...), custom_call_target="tpu_custom_call" | custom-call | flops 754974720 | bytes 10092544 | tf_op jit(solution)/shard_map/pallas_call | solution.py:347
  31.5 2.2 %shard_map.108 = (bf16[8,5120]{1,0:T(8,128)(2,1)S(1)}, bf16[8,5120]{1,0:T(8,128)(2,1)S(1)}, bf16[8,5120]{1,0:T(8,128)(2,1)S(1)}, bf16[8,5120]{1,0:T(8,128)(2,1)S(1)}, f32[8,128]{1,0:T(8,128)S(1)}) custom-call(bf16[8,5248]{1,0:T(8,128)(2,1)S(1)} %get-tuple-element.46.refs_0_, bf16[8,5248]{1,0:T(8,128)(2,1)S(1)} %collective-permute-done.11.refs_1_, ...), custom_call_target="tpu_custom_call" | custom-call | flops 754974720 | bytes 10092544 | tf_op jit(solution)/shard_map/pallas_call | solution.py:347
  33.7 0.7 %collective-permute-start.15 = (bf16[8,5120]{1,0:T(8,128)(2,1)S(1)}, bf16[8,5120]{1,0:T(8,128)(2,1)S(1)}, u32[]{:S(2)}, u32[]{:S(2)}) collective-permute-start(bf16[8,5120]{1,0:T(8,128)(2,1)S(1)} %get-tuple-element.57), channel_id=1, source_target_pairs={{0,2},{1,7},{2,0},{3,5},{4,6},{5,3},{6,4},{7,1},{8,10},{9,15},{10,... | collective-permute-start | bytes 245768 | tf_op jit(solution)/shard_map/ppermute | solution.py:444
  34.4 1.8 %collective-permute-start.16 = (bf16[8,5120]{1,0:T(8,128)(2,1)S(1)}, bf16[8,5120]{1,0:T(8,128)(2,1)S(1)}, u32[]{:S(2)}, u32[]{:S(2)}) collective-permute-start(bf16[8,5120]{1,0:T(8,128)(2,1)S(1)} %get-tuple-element.58), channel_id=1, source_target_pairs={{0,4},{1,3},{2,6},{3,1},{4,0},{5,7},{6,2},{7,5},{8,12},{9,11},{10,... | collective-permute-start | bytes 245768 | tf_op jit(solution)/shard_map/ppermute | solution.py:444
  36.2 1.1 %collective-permute-start.17 = (bf16[8,5120]{1,0:T(8,128)(2,1)S(1)}, bf16[8,5120]{1,0:T(8,128)(2,1)S(1)}, u32[]{:S(2)}, u32[]{:S(2)}) collective-permute-start(bf16[8,5120]{1,0:T(8,128)(2,1)S(1)} %get-tuple-element.59), channel_id=1, source_target_pairs={{0,6},{1,5},{2,4},{3,7},{4,2},{5,1},{6,0},{7,3},{8,14},{9,13},{10,... | collective-permute-start | bytes 245768 | tf_op jit(solution)/shard_map/ppermute | solution.py:444
  37.3 1.0 %collective-permute-done.15.refs_1_ = bf16[8,5120]{1,0:T(8,128)(2,1)S(1)} collective-permute-done((bf16[8,5120]{1,0:T(8,128)(2,1)S(1)}, bf16[8,5120]{1,0:T(8,128)(2,1)S(1)}, u32[]{:S(2)}, u32[]{:S(2)}) %collective-permute-start.15) | collective-permute-done | bytes 81952 | tf_op jit(solution)/shard_map/ppermute | solution.py:444
  38.2 1.0 %collective-permute-done.16.refs_2_ = bf16[8,5120]{1,0:T(8,128)(2,1)S(1)} collective-permute-done((bf16[8,5120]{1,0:T(8,128)(2,1)S(1)}, bf16[8,5120]{1,0:T(8,128)(2,1)S(1)}, u32[]{:S(2)}, u32[]{:S(2)}) %collective-permute-start.16) | collective-permute-done | bytes 81952 | tf_op jit(solution)/shard_map/ppermute | solution.py:444
  39.3 4.0 %collective-permute-done.17.refs_3_ = bf16[8,5120]{1,0:T(8,128)(2,1)S(1)} collective-permute-done((bf16[8,5120]{1,0:T(8,128)(2,1)S(1)}, bf16[8,5120]{1,0:T(8,128)(2,1)S(1)}, u32[]{:S(2)}, u32[]{:S(2)}) %collective-permute-start.17) | collective-permute-done | bytes 81952 | tf_op jit(solution)/shard_map/ppermute | solution.py:444
  43.5 1.7 %collective-permute-start.18 = (bf16[32,2048]{1,0:T(8,128)(2,1)S(1)}, bf16[32,2048]{1,0:T(8,128)(2,1)S(1)}, u32[]{:S(2)}, u32[]{:S(2)}) collective-permute-start(bf16[32,2048]{1,0:T(8,128)(2,1)S(1)} %shard_map.109), channel_id=1, source_target_pairs={{0,8},{1,9},{2,10},{3,11},{4,12},{5,13},{6,14},{7,15},{8,0},{9,1},... | collective-permute-start | bytes 393224 | tf_op jit(solution)/shard_map/ppermute | solution.py:444
  45.3 0.8 %collective-permute-start.6 = (bf16[8,5120]{1,0:T(8,128)(2,1)S(1)}, bf16[8,5120]{1,0:T(8,128)(2,1)S(1)}, u32[]{:S(2)}, u32[]{:S(2)}) collective-permute-start(bf16[8,5120]{1,0:T(8,128)(2,1)S(1)} %get-tuple-element.39), channel_id=1, source_target_pairs={{0,2},{1,7},{2,0},{3,5},{4,6},{5,3},{6,4},{7,1},{8,10},{9,15},{10,... | collective-permute-start | bytes 245768 | tf_op jit(solution)/shard_map/ppermute | solution.py:444
  46.1 2.3 %collective-permute-start.7 = (bf16[8,5120]{1,0:T(8,128)(2,1)S(1)}, bf16[8,5120]{1,0:T(8,128)(2,1)S(1)}, u32[]{:S(2)}, u32[]{:S(2)}) collective-permute-start(bf16[8,5120]{1,0:T(8,128)(2,1)S(1)} %get-tuple-element.40), channel_id=1, source_target_pairs={{0,4},{1,3},{2,6},{3,1},{4,0},{5,7},{6,2},{7,5},{8,12},{9,11},{10,... | collective-permute-start | bytes 245768 | tf_op jit(solution)/shard_map/ppermute | solution.py:444
  48.4 0.4 collective-permute-start.8
  48.8 0.9 %collective-permute-done.6.refs_1_ = bf16[8,5120]{1,0:T(8,128)(2,1)S(1)} collective-permute-done((bf16[8,5120]{1,0:T(8,128)(2,1)S(1)}, bf16[8,5120]{1,0:T(8,128)(2,1)S(1)}, u32[]{:S(2)}, u32[]{:S(2)}) %collective-permute-start.6) | collective-permute-done | bytes 81952 | tf_op jit(solution)/shard_map/ppermute | solution.py:444
  49.7 1.9 %collective-permute-done.7.refs_2_ = bf16[8,5120]{1,0:T(8,128)(2,1)S(1)} collective-permute-done((bf16[8,5120]{1,0:T(8,128)(2,1)S(1)}, bf16[8,5120]{1,0:T(8,128)(2,1)S(1)}, u32[]{:S(2)}, u32[]{:S(2)}) %collective-permute-start.7) | collective-permute-done | bytes 81952 | tf_op jit(solution)/shard_map/ppermute | solution.py:444
  51.7 2.1 %collective-permute-done.8.refs_3_ = bf16[8,5120]{1,0:T(8,128)(2,1)S(1)} collective-permute-done((bf16[8,5120]{1,0:T(8,128)(2,1)S(1)}, bf16[8,5120]{1,0:T(8,128)(2,1)S(1)}, u32[]{:S(2)}, u32[]{:S(2)}) %collective-permute-start.8) | collective-permute-done | bytes 81952 | tf_op jit(solution)/shard_map/ppermute | solution.py:444
  53.7 0.2 shard_map.106
  54.0 0.8 %shard_map.110 = (bf16[32,2048]{1,0:T(8,128)(2,1)}, s32[1]{0:T(128)}) custom-call(bf16[32,2048]{1,0:T(8,128)(2,1)S(1)} %get-tuple-element.42.own_ref, f32[32,128]{1,0:T(8,128)S(1)} %get-tuple-element.43.scale_ref, f32[8,128]{1,0:T(8,128)S(1)} %get-tuple-element.54.load_ref, f32[8,128]{1,0:T(8,128)S(1)} %collective-permute-done.14.load_far_ref, ...), custom_call_target="tpu_custom_call" | custom-call | flops 16777472 | bytes 274432 | tf_op jit(solution)/shard_map/pallas_call | solution.py:406
  (15 shorter events, 0.4 us)
Async XLA Ops:
  0.6 25.0 %collective-permute-start.3 = (bf16[1,2048,384]{2,1,0:T(8,128)(2,1)}, bf16[1,2048,384]{2,1,0:T(8,128)(2,1)S(1)}, u32[]{:S(2)}, u32[]{:S(2)}) collective-permute-start(bf16[1,2048,384]{2,1,0:T(8,128)(2,1)} %refs_4_.1), channel_id=1, source_target_pairs={{0,1},{1,0},{2,3},{3,2},{4,5},{5,4},{6,7},{7,6},{8,9},{9,8},{10,11... | collective-permute-start | bytes 4718600 | tf_op jit(solution)/shard_map/ppermute | solution.py:444
  1.2 26.8 %collective-permute-start.4 = (bf16[1,2048,384]{2,1,0:T(8,128)(2,1)}, bf16[1,2048,384]{2,1,0:T(8,128)(2,1)S(1)}, u32[]{:S(2)}, u32[]{:S(2)}) collective-permute-start(bf16[1,2048,384]{2,1,0:T(8,128)(2,1)} %refs_5_.1), channel_id=1, source_target_pairs={{0,1},{1,0},{2,3},{3,2},{4,5},{5,4},{6,7},{7,6},{8,9},{9,8},{10,11... | collective-permute-start | bytes 4718600 | tf_op jit(solution)/shard_map/ppermute | solution.py:444
  1.3 26.7 %collective-permute-start.5 = (bf16[1,2048,384]{2,1,0:T(8,128)(2,1)}, bf16[1,2048,384]{2,1,0:T(8,128)(2,1)S(1)}, u32[]{:S(2)}, u32[]{:S(2)}) collective-permute-start(bf16[1,2048,384]{2,1,0:T(8,128)(2,1)} %refs_6_.1), channel_id=1, source_target_pairs={{0,1},{1,0},{2,3},{3,2},{4,5},{5,4},{6,7},{7,6},{8,9},{9,8},{10,11... | collective-permute-start | bytes 4718600 | tf_op jit(solution)/shard_map/ppermute | solution.py:444
  1.7 17.0 %collective-permute-start.9 = (bf16[32,2048]{1,0:T(8,128)(2,1)}, bf16[32,2048]{1,0:T(8,128)(2,1)S(1)}, u32[]{:S(2)}, u32[]{:S(2)}) collective-permute-start(bf16[32,2048]{1,0:T(8,128)(2,1)} %bitcast.6), channel_id=1, source_target_pairs={{0,8},{1,9},{2,10},{3,11},{4,12},{5,13},{6,14},{7,15},{8,0},{9,1},... | collective-permute-start | bytes 393224 | tf_op jit(solution)/shard_map/ppermute | solution.py:444
  6.7 5.9 %collective-permute-start.10 = (s32[4,16]{1,0:T(4,128)S(1)}, s32[4,16]{1,0:T(4,128)S(1)}, u32[]{:S(2)}, u32[]{:S(2)}) collective-permute-start(s32[4,16]{1,0:T(4,128)S(1)} %get-tuple-element.45), channel_id=1, source_target_pairs={{0,8},{1,9},{2,10},{3,11},{4,12},{5,13},{6,14},{7,15},{8,0},{9,1},... | collective-permute-start | bytes 776 | tf_op jit(solution)/shard_map/ppermute | solution.py:444
  12.5 5.1 %collective-permute-start = (bf16[8,5248]{1,0:T(8,128)(2,1)S(1)}, bf16[8,5248]{1,0:T(8,128)(2,1)S(1)}, u32[]{:S(2)}, u32[]{:S(2)}) collective-permute-start(bf16[8,5248]{1,0:T(8,128)(2,1)S(1)} %get-tuple-element.34), channel_id=1, source_target_pairs={{0,2},{1,7},{2,0},{3,5},{4,6},{5,3},{6,4},{7,1},{8,10},{9,15},{10,... | collective-permute-start | bytes 251912 | tf_op jit(solution)/shard_map/ppermute | solution.py:444
  17.7 4.5 %collective-permute-start.1 = (bf16[8,5248]{1,0:T(8,128)(2,1)S(1)}, bf16[8,5248]{1,0:T(8,128)(2,1)S(1)}, u32[]{:S(2)}, u32[]{:S(2)}) collective-permute-start(bf16[8,5248]{1,0:T(8,128)(2,1)S(1)} %get-tuple-element.35), channel_id=1, source_target_pairs={{0,4},{1,3},{2,6},{3,1},{4,0},{5,7},{6,2},{7,5},{8,12},{9,11},{10,... | collective-permute-start | bytes 251912 | tf_op jit(solution)/shard_map/ppermute | solution.py:444
  18.7 6.0 %collective-permute-start.2 = (bf16[8,5248]{1,0:T(8,128)(2,1)S(1)}, bf16[8,5248]{1,0:T(8,128)(2,1)S(1)}, u32[]{:S(2)}, u32[]{:S(2)}) collective-permute-start(bf16[8,5248]{1,0:T(8,128)(2,1)S(1)} %get-tuple-element.36), channel_id=1, source_target_pairs={{0,6},{1,5},{2,4},{3,7},{4,2},{5,1},{6,0},{7,3},{8,14},{9,13},{10,... | collective-permute-start | bytes 251912 | tf_op jit(solution)/shard_map/ppermute | solution.py:444
  22.1 9.3 %collective-permute-start.11 = (bf16[8,5248]{1,0:T(8,128)(2,1)S(1)}, bf16[8,5248]{1,0:T(8,128)(2,1)S(1)}, u32[]{:S(2)}, u32[]{:S(2)}) collective-permute-start(bf16[8,5248]{1,0:T(8,128)(2,1)S(1)} %get-tuple-element.47), channel_id=1, source_target_pairs={{0,2},{1,7},{2,0},{3,5},{4,6},{5,3},{6,4},{7,1},{8,10},{9,15},{10,... | collective-permute-start | bytes 251912 | tf_op jit(solution)/shard_map/ppermute | solution.py:444
  24.7 6.8 %collective-permute-start.12 = (bf16[8,5248]{1,0:T(8,128)(2,1)S(1)}, bf16[8,5248]{1,0:T(8,128)(2,1)S(1)}, u32[]{:S(2)}, u32[]{:S(2)}) collective-permute-start(bf16[8,5248]{1,0:T(8,128)(2,1)S(1)} %get-tuple-element.48), channel_id=1, source_target_pairs={{0,4},{1,3},{2,6},{3,1},{4,0},{5,7},{6,2},{7,5},{8,12},{9,11},{10,... | collective-permute-start | bytes 251912 | tf_op jit(solution)/shard_map/ppermute | solution.py:444
  25.7 5.8 %collective-permute-start.13 = (bf16[8,5248]{1,0:T(8,128)(2,1)S(1)}, bf16[8,5248]{1,0:T(8,128)(2,1)S(1)}, u32[]{:S(2)}, u32[]{:S(2)}) collective-permute-start(bf16[8,5248]{1,0:T(8,128)(2,1)S(1)} %get-tuple-element.49), channel_id=1, source_target_pairs={{0,6},{1,5},{2,4},{3,7},{4,2},{5,1},{6,0},{7,3},{8,14},{9,13},{10,... | collective-permute-start | bytes 251912 | tf_op jit(solution)/shard_map/ppermute | solution.py:444
  31.5 22.2 %copy-start = (f32[2,16,1]{1,2,0:T(1,128)S(1)}, f32[2,16,1]{1,2,0:T(1,128)}, u32[]{:S(2)}) copy-start(f32[2,16,1]{1,2,0:T(1,128)} %param.10) | copy-start | bytes 388
  33.7 4.5 %collective-permute-start.15 = (bf16[8,5120]{1,0:T(8,128)(2,1)S(1)}, bf16[8,5120]{1,0:T(8,128)(2,1)S(1)}, u32[]{:S(2)}, u32[]{:S(2)}) collective-permute-start(bf16[8,5120]{1,0:T(8,128)(2,1)S(1)} %get-tuple-element.57), channel_id=1, source_target_pairs={{0,2},{1,7},{2,0},{3,5},{4,6},{5,3},{6,4},{7,1},{8,10},{9,15},{10,... | collective-permute-start | bytes 245768 | tf_op jit(solution)/shard_map/ppermute | solution.py:444
  34.4 4.9 %collective-permute-start.16 = (bf16[8,5120]{1,0:T(8,128)(2,1)S(1)}, bf16[8,5120]{1,0:T(8,128)(2,1)S(1)}, u32[]{:S(2)}, u32[]{:S(2)}) collective-permute-start(bf16[8,5120]{1,0:T(8,128)(2,1)S(1)} %get-tuple-element.58), channel_id=1, source_target_pairs={{0,4},{1,3},{2,6},{3,1},{4,0},{5,7},{6,2},{7,5},{8,12},{9,11},{10,... | collective-permute-start | bytes 245768 | tf_op jit(solution)/shard_map/ppermute | solution.py:444
  36.2 7.1 %collective-permute-start.17 = (bf16[8,5120]{1,0:T(8,128)(2,1)S(1)}, bf16[8,5120]{1,0:T(8,128)(2,1)S(1)}, u32[]{:S(2)}, u32[]{:S(2)}) collective-permute-start(bf16[8,5120]{1,0:T(8,128)(2,1)S(1)} %get-tuple-element.59), channel_id=1, source_target_pairs={{0,6},{1,5},{2,4},{3,7},{4,2},{5,1},{6,0},{7,3},{8,14},{9,13},{10,... | collective-permute-start | bytes 245768 | tf_op jit(solution)/shard_map/ppermute | solution.py:444
  43.5 10.4 %collective-permute-start.18 = (bf16[32,2048]{1,0:T(8,128)(2,1)S(1)}, bf16[32,2048]{1,0:T(8,128)(2,1)S(1)}, u32[]{:S(2)}, u32[]{:S(2)}) collective-permute-start(bf16[32,2048]{1,0:T(8,128)(2,1)S(1)} %shard_map.109), channel_id=1, source_target_pairs={{0,8},{1,9},{2,10},{3,11},{4,12},{5,13},{6,14},{7,15},{8,0},{9,1},... | collective-permute-start | bytes 393224 | tf_op jit(solution)/shard_map/ppermute | solution.py:444
  45.3 4.4 %collective-permute-start.6 = (bf16[8,5120]{1,0:T(8,128)(2,1)S(1)}, bf16[8,5120]{1,0:T(8,128)(2,1)S(1)}, u32[]{:S(2)}, u32[]{:S(2)}) collective-permute-start(bf16[8,5120]{1,0:T(8,128)(2,1)S(1)} %get-tuple-element.39), channel_id=1, source_target_pairs={{0,2},{1,7},{2,0},{3,5},{4,6},{5,3},{6,4},{7,1},{8,10},{9,15},{10,... | collective-permute-start | bytes 245768 | tf_op jit(solution)/shard_map/ppermute | solution.py:444
  46.1 5.6 %collective-permute-start.7 = (bf16[8,5120]{1,0:T(8,128)(2,1)S(1)}, bf16[8,5120]{1,0:T(8,128)(2,1)S(1)}, u32[]{:S(2)}, u32[]{:S(2)}) collective-permute-start(bf16[8,5120]{1,0:T(8,128)(2,1)S(1)} %get-tuple-element.40), channel_id=1, source_target_pairs={{0,4},{1,3},{2,6},{3,1},{4,0},{5,7},{6,2},{7,5},{8,12},{9,11},{10,... | collective-permute-start | bytes 245768 | tf_op jit(solution)/shard_map/ppermute | solution.py:444
  48.4 5.3 %collective-permute-start.8 = (bf16[8,5120]{1,0:T(8,128)(2,1)S(1)}, bf16[8,5120]{1,0:T(8,128)(2,1)S(1)}, u32[]{:S(2)}, u32[]{:S(2)}) collective-permute-start(bf16[8,5120]{1,0:T(8,128)(2,1)S(1)} %get-tuple-element.41), channel_id=1, source_target_pairs={{0,6},{1,5},{2,4},{3,7},{4,2},{5,1},{6,0},{7,3},{8,14},{9,13},{10,... | collective-permute-start | bytes 245768 | tf_op jit(solution)/shard_map/ppermute | solution.py:444
  48.8 5.2 %collective-permute-start.14 = (f32[8,128]{1,0:T(8,128)S(1)}, f32[8,128]{1,0:T(8,128)S(1)}, u32[]{:S(2)}, u32[]{:S(2)}) collective-permute-start(f32[8,128]{1,0:T(8,128)S(1)} %get-tuple-element.54.load_ref), channel_id=1, source_target_pairs={{0,1},{1,0},{2,3},{3,2},{4,5},{5,4},{6,7},{7,6},{8,9},{9,8},{10,11... | collective-permute-start | bytes 12296 | tf_op jit(solution)/shard_map/ppermute | solution.py:444
